TPU v7x, 128 devices: a whole 4x4x4 slice. The times are simulated.
128 devices in a mesh: gx: 8 (over z, core), gy: 16 (over x, y).
Axes of the slice: x: 4, y: 4, z: 4, core: 2. Of those that a mesh axis runs over, the one named last changes fastest.
Arguments:
- control: float32 [4, 64, 128, 4096], P(None, None, 'gx', 'gy'), may hold values from -6 to 6
- background: float32 [4, 64, 128, 4096], P(None, None, 'gx', 'gy'), may hold values from -6 to 6
- vert_factor: float32 [4, 64, 64], replicated, may hold values from -0.75 to 0.75
- length_rates: float32 [2, 4, 64], replicated, may hold values from 0.5 to 40
- flash_weights: float32 [4, 64], replicated, may hold values from -3 to 3
- level_weights: float32 [64], replicated, may hold values from -0.75 to 0.75
- obs_owner: int32 [65536, 1], P(('gx', 'gy')), may hold values from 0 to 127; in each aligned block of 512 rows (0 to 511, 512 to 1023, ...) at most 8 rows name the same one
- obs_cell: int32 [65536], P(('gx', 'gy')), may hold values from 0 to 4095
- obs_count: int32 [128], P(('gx', 'gy')), may hold values from 256 to 512, as said below
- flash_obs: float32 [65536], P(('gx', 'gy')), may hold values from 0.1 to 3
- obs_error: float32 [65536], P(('gx', 'gy')), may hold values from 0.3 to 1
Outputs:
- grad: float32 [4, 64, 128, 4096], P(None, None, 'gx', 'gy')
- departure: float32 [65536], P(('gx', 'gy'))
Inputs may be any that keep to these rules, and one draw needn't show every extreme that they name: `obs_owner`: among one device's 512 slots no owner is named more than 8 times, a bound that some block reaches. Only the first obs_count slots of a device are live; some device has all 512 live.
All inputs are finite; a program needn't handle non-finite values.
Results may differ from a plain program's by a relative error of at most 0.0003.
Values sent between devices are 32-bit elements; how exact they have to be, the bound alone decides.
No kernel may reach another device: no remote copies, remote signals or barrier semaphores. Data moves between devices by JAX's collectives and lax.ppermute only.
A program may use at most 128 MiB of HBM per device.

v0:
```python
import functools

import jax
import jax.numpy as jnp
from jax import lax
from jax.experimental import pallas as pl
from jax.experimental.pallas import tpu as pltpu
from jax.sharding import PartitionSpec as P

highest = lax.Precision.HIGHEST
f32 = jnp.float32
bf16 = jnp.bfloat16

CH, LEVELS, XB, YB = 256, 64, 16, 256
OBS, PEERS, CAP = 512, 128, 8
N_X, N_Y = 8, 16
BLOCK = 32
REQ = 32
VMEM_LIMIT = 60 * 1024 * 1024


def iota(shape, dim):
    return lax.broadcasted_iota(jnp.int32, shape, dim)


def split(value):
    high = value.astype(bf16)
    return high, (value - high.astype(f32)).astype(bf16)


def split3(value):
    high = value.astype(bf16)
    rest = value - high.astype(f32)
    middle = rest.astype(bf16)
    return high, middle, (rest - middle.astype(f32)).astype(bf16)


def mm(a, b):
    return jnp.dot(a, b, preferred_element_type=f32)


def mm_nt(a, b):
    return lax.dot_general(a, b, (((1,), (1,)), ((), ())), preferred_element_type=f32)


def column(row):
    halves = [jnp.broadcast_to(row[:, i : i + 128], (128, 128)).T for i in range(0, CH, 128)]
    return jnp.concatenate(halves, axis=0)


def wide(col):
    return jnp.concatenate([col, col], axis=1)


def upper():
    return jnp.where(iota((YB, YB), 0) <= iota((YB, YB), 1), 1.0, 0.0).astype(bf16)


def lower():
    return jnp.where(iota((YB, YB), 0) >= iota((YB, YB), 1), 1.0, 0.0).astype(bf16)


def softplus(x):
    return jnp.maximum(x, 0.0) + jnp.log1p(jnp.exp(-jnp.abs(x)))


def sigmoid(x):
    return 1.0 / (1.0 + jnp.exp(-x))


def take_plane(halves, x, rows, *lead):
    at = lead + (pl.ds(x, rows, stride=XB), slice(None))
    return jnp.concatenate([half[at] for half in halves], axis=1)


def params(**more):
    return pltpu.CompilerParams(vmem_limit_bytes=VMEM_LIMIT, **more)


def edges_kernel(count, control_a, control_b, rates, owner, cell, flash, sigma, sx, msg, rank_out, colx, coly):
    b = pl.program_id(0)

    @pl.when(b == 0)
    def _():
        colx[...] = column(rates[0:1, :] * (1.0 / 128.0))
        coly[...] = column(rates[1:2, :] * (1.0 / 4096.0))
        live = iota((PEERS, OBS), 1) < count[0]
        chosen = (owner[...] == iota((PEERS, OBS), 0)) & live
        earlier = jnp.where(iota((OBS, OBS), 0) < iota((OBS, OBS), 1), 1.0, 0.0).astype(bf16)
        rank = mm(jnp.where(chosen, 1.0, 0.0).astype(bf16), earlier)
        rank = jnp.where(chosen, rank, -1.0)
        rank_out[...] = rank
        rows = iota((8, OBS), 0)
        values = jnp.where(
            rows == 0,
            cell[...].astype(f32) + 1.0,
            jnp.where(rows == 1, flash[...], jnp.where(rows == 2, sigma[...], 0.0)),
        )
        values = jnp.concatenate([values, jnp.zeros((120, OBS), f32)], axis=0)
        pieces = [
            jnp.concatenate([values[:, i : i + 128].T for i in range(0, OBS, 128)], axis=0)
        ]
        pieces = split3(pieces[0])
        total = jnp.zeros((PEERS, 128), f32)
        for r in range(CAP):
            taken = jnp.where(rank == float(r), 1.0, 0.0).astype(bf16)
            found = (mm(taken, pieces[0]) + mm(taken, pieces[1])) + mm(taken, pieces[2])
            total = total + pltpu.roll(found, REQ + 3 * r, 1)
        msg[...] = total

    rows = pl.ds(pl.multiple_of(b * BLOCK, BLOCK), BLOCK)
    cx = wide(colx[rows, :])
    lanes = iota((BLOCK, YB), 1).astype(f32)
    grow_y = jnp.exp(wide(coly[rows, :]) * lanes)
    running = jnp.zeros((BLOCK, YB), f32)
    place = iota((BLOCK, 128), 1) - 16 * (b // 4)
    sums = jnp.zeros((BLOCK, 128), f32)
    for x in range(XB):
        plane = take_plane((control_a, control_b), x, BLOCK)
        running = running + plane * (grow_y * jnp.exp(cx * float(x)))
        sums = jnp.where(place == x, jnp.sum(running, axis=1, keepdims=True), sums)
    sx[...] = running
    back = pl.ds(pl.multiple_of((b % 4) * BLOCK, BLOCK), BLOCK)
    msg[back, :] = msg[back, :] + sums


def edges(count, control, rates, owner, cell, flash, sigma):
    whole = lambda shape: pl.BlockSpec(shape, lambda b: (0, 0))
    return pl.pallas_call(
        edges_kernel,
        grid=(CH // BLOCK,),
        in_specs=[
            pl.BlockSpec(memory_space=pltpu.SMEM),
            pl.BlockSpec((BLOCK * XB, 128), lambda b: (b, 0)),
            pl.BlockSpec((BLOCK * XB, 128), lambda b: (b, 1)),
            whole((2, CH)),
            whole((1, OBS)),
            whole((1, OBS)),
            whole((1, OBS)),
            whole((1, OBS)),
        ],
        out_specs=[
            pl.BlockSpec((BLOCK, YB), lambda b: (b, 0)),
            whole((PEERS, 128)),
            whole((PEERS, OBS)),
        ],
        out_shape=[
            jax.ShapeDtypeStruct((CH, YB), f32),
            jax.ShapeDtypeStruct((PEERS, 128), f32),
            jax.ShapeDtypeStruct((PEERS, OBS), f32),
        ],
        scratch_shapes=[pltpu.VMEM((CH, 128), f32), pltpu.VMEM((CH, 128), f32)],
        compiler_params=params(),
        name="edges",
    )(count, control, control, rates, owner, cell, flash, sigma)


def local_kernel(control_a, control_b, rates, background_a, background_b, weights, matrix, matrix_t, cc, share, mh, ml, th, tl, colx, coly):
    b = pl.program_id(0)

    @pl.when(b == 0)
    def _():
        colx[...] = column(rates[0:1, :] * (1.0 / 128.0))
        coly[...] = column(rates[1:2, :] * (1.0 / 4096.0))

    rows = pl.ds(pl.multiple_of(b * BLOCK, BLOCK), BLOCK)
    cx = wide(colx[rows, :])
    lanes = iota((BLOCK, YB), 1).astype(f32)
    grow_y = jnp.exp(wide(coly[rows, :]) * lanes)
    running = jnp.zeros((BLOCK, YB), f32)
    sums = upper()
    highs, lows = [], []
    for x in range(XB):
        plane = take_plane((control_a, control_b), x, BLOCK)
        running = running + plane * (grow_y * jnp.exp(cx * float(x)))
        high, low = split(running)
        highs.append(high)
        lows.append(low)
    summed = mm(jnp.concatenate(highs, axis=0), sums) + mm(jnp.concatenate(lows, axis=0), sums)
    cc[...] = summed.reshape(XB, BLOCK, YB)
    for x in range(XB):
        part = jnp.zeros((8, YB), f32)
        for v in range(4):
            part = part + take_plane((background_a, background_b), x, 8, v) * weights[:, v : v + 1]
        share[x] = part
    for i in range(2):
        x = (2 * b + i).astype(f32)
        scaled = matrix[...] * jnp.exp(rates[0:1, :] * (x * (-1.0 / 128.0)))
        mh[i], ml[i] = split(scaled)
        scaled_t = matrix_t[...] * jnp.exp(colx[:, :64] * -x)
        th[i], tl[i] = split(scaled_t)


def local(control, rates, background, weights, matrix, matrix_t):
    whole = lambda shape: pl.BlockSpec(shape, lambda b: (0, 0))
    return pl.pallas_call(
        local_kernel,
        grid=(CH // BLOCK,),
        in_specs=[
            pl.BlockSpec((BLOCK * XB, 128), lambda b: (b, 0)),
            pl.BlockSpec((BLOCK * XB, 128), lambda b: (b, 1)),
            whole((2, CH)),
            pl.BlockSpec((4, 128, 128), lambda b: (0, b, 0)),
            pl.BlockSpec((4, 128, 128), lambda b: (0, b, 1)),
            pl.BlockSpec((8, 4), lambda b: (b, 0)),
            whole((LEVELS, CH)),
            whole((CH, LEVELS)),
        ],
        out_specs=[
            pl.BlockSpec((XB, BLOCK, YB), lambda b: (0, b, 0)),
            pl.BlockSpec((XB, 8, YB), lambda b: (0, b, 0)),
            pl.BlockSpec((2, LEVELS, CH), lambda b: (b, 0, 0)),
            pl.BlockSpec((2, LEVELS, CH), lambda b: (b, 0, 0)),
            pl.BlockSpec((2, CH, LEVELS), lambda b: (b, 0, 0)),
            pl.BlockSpec((2, CH, LEVELS), lambda b: (b, 0, 0)),
        ],
        out_shape=[
            jax.ShapeDtypeStruct((XB, CH, YB), f32),
            jax.ShapeDtypeStruct((XB, LEVELS, YB), f32),
            jax.ShapeDtypeStruct((XB, LEVELS, CH), bf16),
            jax.ShapeDtypeStruct((XB, LEVELS, CH), bf16),
            jax.ShapeDtypeStruct((XB, CH, LEVELS), bf16),
            jax.ShapeDtypeStruct((XB, CH, LEVELS), bf16),
        ],
        scratch_shapes=[pltpu.VMEM((CH, 128), f32), pltpu.VMEM((CH, 128), f32)],
        compiler_params=params(),
        cost_estimate=pl.CostEstimate(flops=2 * 2 * 4096 * 256 * 256, bytes_accessed=15 << 20, transcendentals=1 << 20),
        name="local",
    )(control, control, rates, background, background, weights, matrix, matrix_t)


def carry_kernel(reverse, place, sums, rates, out):
    me = place[2]
    d, e = iota((PEERS, PEERS), 0), iota((PEERS, PEERS), 1)
    far_x = (d // N_Y) - (e // N_Y)
    far_y = (d % N_Y) - (e % N_Y)
    if reverse:
        far_x, far_y = -far_x, -far_y
    fx, fy = far_x.astype(f32), far_y.astype(f32)
    lanes = iota((PEERS, 128), 1)
    left, right = [], []
    for c in range(2):
        mine = iota((2, CH), 1) == me + 128 * c
        rate = jnp.sum(jnp.where(mine, rates[...], 0.0), axis=1, keepdims=True)
        down_x = rate[0:1, :] * (XB / 128.0)
        down_y = rate[1:2, :] * (YB / 4096.0)
        along = jnp.exp(-jnp.maximum(fy, 0.0) * down_y)
        left.append(jnp.where((far_x == 0) & (far_y > 0), along, 0.0))
        across = along * jnp.exp(-jnp.maximum(fx, 0.0) * down_x)
        left.append(jnp.where((far_x > 0) & (far_y > 0), across, 0.0))
        own = (lanes >= 16 * c) & (lanes < 16 * c + 16)
        right.append(jnp.where(own, sums[...], 0.0))
        last = 16 * c if reverse else 16 * c + 15
        total = jnp.sum(jnp.where(lanes == last, sums[...], 0.0), axis=1, keepdims=True)
        right.append(jnp.where(own, total, 0.0))
    out[...] = jnp.dot(
        jnp.concatenate(left, axis=1),
        jnp.concatenate(right, axis=0),
        precision=highest,
        preferred_element_type=f32,
    )


def carry(place, sums, rates, reverse):
    return pl.pallas_call(
        functools.partial(carry_kernel, reverse),
        in_specs=[
            pl.BlockSpec(memory_space=pltpu.SMEM),
            pl.BlockSpec(memory_space=pltpu.VMEM),
            pl.BlockSpec(memory_space=pltpu.VMEM),
        ],
        out_specs=pl.BlockSpec(memory_space=pltpu.VMEM),
        out_shape=jax.ShapeDtypeStruct((PEERS, 128), f32),
        compiler_params=params(),
        name="carry_back" if reverse else "carry",
    )(place, sums, rates)


def entering_rows(place, gathered, colx, reverse):
    mine = place[0]
    total = None
    for g in range(N_X):
        far = (g - mine) if reverse else (mine - g)
        decay = jnp.exp(colx * (-float(XB) * jnp.maximum(far, 0).astype(f32)))
        decay = jnp.where(far > 0, decay, 0.0)
        term = wide(decay) * gathered[g]
        total = term if total is None else total + term
    return total


def observe_kernel(
    place, cc, share, mh, ml, th, tl, gathered, cols, asked, rates, level_weights,
    running_out, sx, msg, lh, ll, forced,
):
    colx = column(rates[0:1, :] * (1.0 / 128.0))
    coly = column(rates[1:2, :] * (1.0 / 4096.0))
    decay_y = jnp.exp(-wide(coly) * iota((CH, YB), 1).astype(f32))
    entering = entering_rows(place, gathered, colx, False)
    high, low = split(entering)
    sums = upper()
    entering = mm(high, sums) + mm(low, sums)

    for x in range(XB):
        col = jnp.concatenate([cols[:, x : x + 1], cols[:, 16 + x : 17 + x]], axis=0)
        smooth = decay_y * ((cc[x] + entering) + col)
        high, low = split(smooth)
        level = (mm(mh[x], high) + (mm(ml[x], high) + mm(mh[x], low))) + share[x]
        lh[x * LEVELS : (x + 1) * LEVELS, :], ll[x * LEVELS : (x + 1) * LEVELS, :] = split(level)

    requests = asked[...].T
    weights = level_weights[...]
    departures = []
    for r in range(0, CAP, 2):
        row = lambda i: jnp.concatenate(
            [requests[REQ + 3 * r + i : REQ + 3 * r + i + 1, :], requests[REQ + 3 * r + 3 + i : REQ + 3 * r + 4 + i, :]], axis=1
        )
        where = row(0).astype(jnp.int32) - 1
        valid = where >= 0
        at_x, at_y = where // YB, where % YB
        at_x = jnp.where(valid, at_x, -1)
        chosen = jnp.where(iota((YB, 256), 0) == at_y, 1.0, 0.0).astype(bf16)
        picked = mm(lh[...], chosen) + mm(ll[...], chosen)
        levels = jnp.zeros((LEVELS, 256), f32)
        for x in range(XB):
            levels = jnp.where(at_x == x, picked[x * LEVELS : (x + 1) * LEVELS, :], levels)
        total = jnp.sum(weights * softplus(levels), axis=0, keepdims=True)
        miss = jnp.where(valid, softplus(total) - row(1), 0.0)
        error = jnp.where(valid, row(2), 1.0)
        scale = miss / (error * error) * sigmoid(total)
        adjoint = scale * (weights * sigmoid(levels))
        high, low = adjoint.astype(bf16).astype(f32), None
        low = adjoint - high
        spread_high = jnp.concatenate([jnp.where(at_x == x, high, 0.0).astype(bf16) for x in range(XB)], axis=0)
        spread_low = jnp.concatenate([jnp.where(at_x == x, low, 0.0).astype(bf16) for x in range(XB)], axis=0)
        part = mm_nt(spread_high, chosen) + mm_nt(spread_low, chosen)
        if r == 0:
            forced[...] = part
        else:
            forced[...] = forced[...] + part
        departures += [miss[:, :128], miss[:, 128:]]

    running = jnp.zeros((CH, YB), f32)
    lanes = iota((PEERS, 128), 1)
    message = pltpu.roll(
        jnp.concatenate(departures + [jnp.zeros((120, 128), f32)], axis=0).T, REQ, 1
    )
    for x in range(XB - 1, -1, -1):
        high, low = split(forced[x * LEVELS : (x + 1) * LEVELS, :])
        back = mm(th[x], high) + (mm(tl[x], high) + mm(th[x], low))
        running = running + back * decay_y
        running_out[x] = running
        total = jnp.sum(running, axis=1, keepdims=True)
        message = jnp.where(lanes == x, total[:128], message)
        message = jnp.where(lanes == 16 + x, total[128:], message)
    sx[...] = running
    msg[...] = message


def observations(place, cc, share, mh, ml, th, tl, gathered, cols, asked, rates, level_weights):
    vmem = pl.BlockSpec(memory_space=pltpu.VMEM)
    return pl.pallas_call(
        observe_kernel,
        in_specs=[pl.BlockSpec(memory_space=pltpu.SMEM)] + [vmem] * 11,
        out_specs=[vmem] * 3,
        out_shape=[
            jax.ShapeDtypeStruct((XB, CH, YB), f32),
            jax.ShapeDtypeStruct((CH, YB), f32),
            jax.ShapeDtypeStruct((PEERS, 128), f32),
        ],
        scratch_shapes=[
            pltpu.VMEM((XB * LEVELS, YB), bf16),
            pltpu.VMEM((XB * LEVELS, YB), bf16),
            pltpu.VMEM((XB * LEVELS, YB), f32),
        ],
        compiler_params=params(),
        name="observations",
    )(place, cc, share, mh, ml, th, tl, gathered, cols, asked, rates, level_weights)


def local_back_kernel(control_a, control_b, running, rates, out, colx, coly):
    b = pl.program_id(0)
    columns_once(rates, colx, coly)
    rows = pl.ds(pl.multiple_of(b * BLOCK, BLOCK), BLOCK)
    high, low = split(running[...].reshape(XB * BLOCK, YB))
    sums = lower()
    summed = mm(high, sums) + mm(low, sums)
    cx = wide(colx[rows, :])
    grow_y = jnp.exp(wide(coly[rows, :]) * iota((BLOCK, YB), 1).astype(f32))
    for x in range(XB):
        scale = grow_y * jnp.exp(cx * float(x))
        plane = take_plane((control_a, control_b), x, BLOCK)
        out[x] = plane + scale * summed[x * BLOCK : (x + 1) * BLOCK, :]


def columns_once(rates, colx, coly):
    @pl.when(pl.program_id(0) == 0)
    def _():
        colx[...] = column(rates[0:1, :] * (1.0 / 128.0))
        coly[...] = column(rates[1:2, :] * (1.0 / 4096.0))


def final_kernel(place, partial, gathered, cols, rates, out, colx, coly, whole_a, whole_b, sems):
    b = pl.program_id(0)
    columns_once(rates, colx, coly)
    rows = pl.ds(pl.multiple_of(b * BLOCK, BLOCK), BLOCK)
    cx = wide(colx[rows, :])
    grow_y = jnp.exp(wide(coly[rows, :]) * iota((BLOCK, YB), 1).astype(f32))
    entering = entering_rows(place, gathered, colx[rows, :], True)
    high, low = split(entering)
    sums = lower()
    entering = mm(high, sums) + mm(low, sums)
    back = pl.ds(pl.multiple_of((b % 4) * BLOCK, BLOCK), BLOCK)
    mine = jnp.where(b < 4, cols[back, :], pltpu.roll(cols[back, :], 112, 1))
    for x in range(XB):
        scale = grow_y * jnp.exp(cx * float(x))
        plane = partial[x] + scale * (entering + mine[:, x : x + 1])
        at = pl.ds(b * (BLOCK * XB) + x, BLOCK, stride=XB)
        whole_a[at, :] = plane[:, :128]
        whole_b[at, :] = plane[:, 128:]

    def copies(step):
        at = pl.ds(pl.multiple_of(step * (BLOCK * XB), BLOCK * XB), BLOCK * XB)
        return (
            pltpu.make_async_copy(whole_a.at[at, :], out.at[at, pl.ds(0, 128)], sems.at[step, 0]),
            pltpu.make_async_copy(whole_b.at[at, :], out.at[at, pl.ds(128, 128)], sems.at[step, 1]),
        )

    for copy in copies(b):
        copy.start()

    @pl.when(b == CH // BLOCK - 1)
    def _():
        for step in range(CH // BLOCK):
            for copy in copies(step):
                copy.wait()


def local_back(control, running, rates):
    return pl.pallas_call(
        local_back_kernel,
        grid=(CH // BLOCK,),
        in_specs=[
            pl.BlockSpec((BLOCK * XB, 128), lambda b: (b, 0)),
            pl.BlockSpec((BLOCK * XB, 128), lambda b: (b, 1)),
            pl.BlockSpec((XB, BLOCK, YB), lambda b: (0, b, 0)),
            pl.BlockSpec((2, CH), lambda b: (0, 0)),
        ],
        out_specs=pl.BlockSpec((XB, BLOCK, YB), lambda b: (0, b, 0)),
        out_shape=jax.ShapeDtypeStruct((XB, CH, YB), f32),
        scratch_shapes=[pltpu.VMEM((CH, 128), f32), pltpu.VMEM((CH, 128), f32)],
        compiler_params=params(),
        cost_estimate=pl.CostEstimate(flops=2 * 2 * 4096 * 256 * 256, bytes_accessed=12 << 20, transcendentals=1 << 20),
        name="local_back",
    )(control, control, running, rates)


def final(place, partial, gathered, cols, rates):
    return pl.pallas_call(
        final_kernel,
        grid=(CH // BLOCK,),
        in_specs=[
            pl.BlockSpec(memory_space=pltpu.SMEM),
            pl.BlockSpec((XB, BLOCK, YB), lambda b: (0, b, 0)),
            pl.BlockSpec((N_X, BLOCK, YB), lambda b: (0, b, 0)),
            pl.BlockSpec((PEERS, 128), lambda b: (0, 0)),
            pl.BlockSpec((2, CH), lambda b: (0, 0)),
        ],
        out_specs=pl.BlockSpec(memory_space=pl.ANY),
        out_shape=jax.ShapeDtypeStruct((CH * XB, YB), f32),
        scratch_shapes=[
            pltpu.VMEM((CH, 128), f32),
            pltpu.VMEM((CH, 128), f32),
            pltpu.VMEM((CH * XB, 128), f32),
            pltpu.VMEM((CH * XB, 128), f32),
            pltpu.SemaphoreType.DMA((CH // BLOCK, 2)),
        ],
        compiler_params=params(),
        name="final",
    )(place, partial, gathered, cols, rates)


def departures_kernel(rank, returned, out):
    total = jnp.zeros((1, OBS), f32)
    for r in range(CAP):
        value = returned[:, REQ + r : REQ + r + 1]
        total = total + jnp.sum(jnp.where(rank[...] == float(r), value, 0.0), axis=0, keepdims=True)
    out[...] = total


def departures(rank, returned):
    vmem = pl.BlockSpec(memory_space=pltpu.VMEM)
    return pl.pallas_call(
        departures_kernel,
        in_specs=[vmem] * 2,
        out_specs=vmem,
        out_shape=jax.ShapeDtypeStruct((1, OBS), f32),
        compiler_params=params(),
        cost_estimate=pl.CostEstimate(flops=1 << 20, bytes_accessed=1 << 19, transcendentals=0),
        name="departures",
    )(rank, returned)


def everywhere(rows):
    shaped = rows.reshape(PEERS, 1, 128)
    return lax.all_to_all(shaped, ("gx", "gy"), split_axis=0, concat_axis=0, tiled=True).reshape(PEERS, 128)


def body(
    control,
    background,
    vert_factor,
    length_rates,
    flash_weights,
    level_weights,
    obs_owner,
    obs_cell,
    obs_count,
    flash_obs,
    obs_error,
):
    shape = control.shape
    gx, gy = lax.axis_index("gx"), lax.axis_index("gy")
    place = jnp.stack([gx, gy, gx * N_Y + gy]).astype(jnp.int32)
    flat = control.reshape(CH * XB, YB)
    rates = length_rates.reshape(2, CH)
    sx, msg, rank = edges(
        obs_count, flat, rates, obs_owner.reshape(1, OBS), obs_cell.reshape(1, OBS),
        flash_obs.reshape(1, OBS), obs_error.reshape(1, OBS),
    )
    asked = everywhere(msg)
    gathered = lax.all_gather(sx, "gx")

    step_x, step_y = length_rates[0] / (XB * N_X), length_rates[1] / (YB * N_Y)
    gain = jnp.sqrt(-jnp.expm1(-2.0 * step_x)) * jnp.sqrt(-jnp.expm1(-2.0 * step_y))
    mixed = flash_weights[:, :, None] * vert_factor * gain[:, None, :]
    matrix = mixed.transpose(1, 0, 2).reshape(LEVELS, CH)
    matrix_t = mixed.transpose(0, 2, 1).reshape(CH, LEVELS)
    cc, share, mh, ml, th, tl = local(
        flat, rates, background.reshape(4, LEVELS * XB, YB), flash_weights.T, matrix, matrix_t
    )
    cols = everywhere(carry(place, asked, rates, False))
    running, sx_back, msg_back = observations(
        place, cc, share, mh, ml, th, tl, gathered, cols, asked, rates, level_weights.reshape(LEVELS, 1)
    )
    returned = everywhere(msg_back)
    gathered_back = lax.all_gather(sx_back, "gx")
    partial = local_back(flat, running, rates)
    cols_back = everywhere(carry(place, returned, rates, True))
    departure = departures(rank, returned)
    grad = final(place, partial, gathered_back, cols_back, rates)
    return (grad.reshape(shape), departure.reshape(OBS))


def solution(mesh):
    placed = (
        P(None, None, "gx", "gy"),
        P(None, None, "gx", "gy"),
        P(),
        P(),
        P(),
        P(),
        P(("gx", "gy"), None),
        P(("gx", "gy")),
        P(("gx", "gy")),
        P(("gx", "gy")),
        P(("gx", "gy")),
    )
    return jax.shard_map(
        body,
        mesh=mesh,
        in_specs=placed,
        out_specs=(P(None, None, "gx", "gy"), P(("gx", "gy"))),
        check_vma=False,
    )
```

profile of v0, /device:TPU:1, one launch (start us, length us, event | category | flops | bytes accessed | tf_op | source)
XLA Modules:
  0.0 122.2 jit_solution(14308096302703316376)
XLA Ops:
  7.9 1.3 %reshape.93.rates = f32[2,256]{1,0:T(2,128)} reshape(f32[2,4,64]{2,1,0:T(4,128)} %param.14) | data formatting | bytes 4096 | tf_op jit(solution)/shard_map/reshape | solution.py:525
  9.2 7.8 %edges.1 = (f32[256,256]{1,0:T(8,128)}, f32[128,128]{1,0:T(8,128)}, f32[128,512]{1,0:T(8,128)}) custom-call(s32[1]{0:T(128)S(6)} %copy.25.count, f32[4096,256]{1,0:T(8,128)} %bitcast.38, f32[4096,256]{1,0:T(8,128)} %bitcast.39, f32[2,256]{1,0:T(2,128)} %reshape.93.rates, s32[1,512]{1,0:T(1,128)} %bitcast.62, s32[1,512]{1,0:T(1,128)} %bitcast.63, ...), custom_call_target="tpu_custom_call" | custom-call | tf_op jit(solution)/shard_map/edges/pallas_call | solution.py:129
  17.1 11.5 %all-to-all-start = ((f32[128,1,128]{2,1,0:T(1,128)}), f32[128,1,128]{2,1,0:T(1,128)S(1)}, u32[]{:S(2)}, u32[]{:S(2)}) async-start(f32[128,1,128]{2,1,0:T(1,128)} %bitcast.59), calls=%async_computation | async-start | bytes 131072 | tf_op jit(solution)/shard_map/all_to_all | solution.py:505
  28.6 0.7 copy.22.level_weights
  29.3 0.7 copy.17
  30.1 0.1 fusion
  30.2 0.7 copy.19
  30.9 0.1 copy.18
  31.0 0.8 reshape.95.matrix
  31.8 0.6 pad_add_fusion.place
  32.3 5.8 %all-to-all-done = f32[128,1,128]{2,1,0:T(1,128)S(1)} async-done(((f32[128,1,128]{2,1,0:T(1,128)}), f32[128,1,128]{2,1,0:T(1,128)S(1)}, u32[]{:S(2)}, u32[]{:S(2)}) %all-to-all-start) | async-done | bytes 65568 | tf_op jit(solution)/shard_map/all_to_all | solution.py:505
  38.1 0.6 copy-done
  38.7 1.9 %carry.1 = f32[128,128]{1,0:T(8,128)} custom-call(s32[3]{0:T(128)} %pad_add_fusion.place, f32[128,128]{1,0:T(8,128)} %bitcast.49, f32[2,256]{1,0:T(2,128)} %reshape.93.rates), custom_call_target="tpu_custom_call" | custom-call | tf_op jit(solution)/shard_map/carry/pallas_call | solution.py:265
  40.7 4.5 %all-to-all-start.1 = ((f32[128,1,128]{2,1,0:T(1,128)}), f32[128,1,128]{2,1,0:T(1,128)S(1)}, u32[]{:S(2)}, u32[]{:S(2)}) async-start(f32[128,1,128]{2,1,0:T(1,128)} %bitcast.56), calls=%async_computation.1 | async-start | bytes 131072 | tf_op jit(solution)/shard_map/all_to_all | solution.py:505
  45.2 10.5 %local.1 = (f32[16,256,256]{2,1,0:T(8,128)}, f32[16,64,256]{2,1,0:T(8,128)}, bf16[16,64,256]{2,1,0:T(8,128)(2,1)}, bf16[16,64,256]{2,1,0:T(8,128)(2,1)}, bf16[16...) custom-call(f32[4096,256]{1,0:T(8,128)} %bitcast.40, f32[4096,256]{1,0:T(8,128)} %bitcast.41, ...), custom_call_target="tpu_custom_call" | custom-call | flops 1073741824 | bytes 15728640 | tf_op jit(solution)/shard_map/local/pallas_call | solution.py:196
  55.7 0.6 copy-done.1
  56.3 13.2 %observations.1 = (f32[16,256,256]{2,1,0:T(8,128)}, f32[256,256]{1,0:T(8,128)}, f32[128,128]{1,0:T(8,128)}) custom-call(s32[3]{0:T(128)} %pad_add_fusion.place, f32[16,256,256]{2,1,0:T(8,128)} %get-tuple-element.14.cc, f32[16,64,256]{2,1,0:T(8,128)} %get-tuple-element.15.share, bf16[16,64,256]{2,1,0:T(8,128)(2,1)} %get-tuple-element.16.mh, ...), custom_call_target="tpu_custom_call" | custom-call | tf_op jit(solution)/shard_map/observations/pallas_call | solution.py:361
  69.6 19.7 %all_to_all.20 = f32[128,1,128]{2,1,0:T(1,128)} all-to-all(f32[128,1,128]{2,1,0:T(1,128)} %bitcast.60), channel_id=1, replica_groups=mesh['gx'=8,'gy'=16] {'gx','gy'}, dimensions={0} | all-to-all | bytes 131072 | tf_op jit(solution)/shard_map/all_to_all | solution.py:505
  89.3 1.9 %carry_back.1 = f32[128,128]{1,0:T(8,128)} custom-call(s32[3]{0:T(128)} %pad_add_fusion.place, f32[128,128]{1,0:T(8,128)} %bitcast.51, f32[2,256]{1,0:T(2,128)} %reshape.93.rates), custom_call_target="tpu_custom_call" | custom-call | tf_op jit(solution)/shard_map/carry_back/pallas_call | solution.py:265
  91.2 4.5 %all-to-all-start.3 = ((f32[128,1,128]{2,1,0:T(1,128)}), f32[128,1,128]{2,1,0:T(1,128)S(1)}, u32[]{:S(2)}, u32[]{:S(2)}) async-start(f32[128,1,128]{2,1,0:T(1,128)} %bitcast.57), calls=%async_computation.3 | async-start | bytes 131072 | tf_op jit(solution)/shard_map/all_to_all | solution.py:505
  95.7 9.0 %local_back.1.partial = f32[16,256,256]{2,1,0:T(8,128)} custom-call(f32[4096,256]{1,0:T(8,128)} %bitcast.42, f32[4096,256]{1,0:T(8,128)} %bitcast.43, f32[16,256,256]{2,1,0:T(8,128)} %get-tuple-element.22.running, f32[2,256]{1,0:T(2,128)} %reshape.93.rates), custom_call_target="tpu_custom_call" | custom-call | flops 1073741824 | bytes 12582912 | tf_op jit(solution)/shard_map/local_back/pallas_call | solution.py:439
  104.7 1.8 %departures.1 = f32[1,512]{1,0:T(1,128)} custom-call(f32[128,512]{1,0:T(8,128)} %get-tuple-element.25.rank, f32[128,128]{1,0:T(8,128)} %bitcast.52), custom_call_target="tpu_custom_call" | custom-call | flops 1048576 | bytes 524288 | tf_op jit(solution)/shard_map/departures/pallas_call | solution.py:492
  106.5 0.6 copy-done.2
  107.1 8.2 %final.1 = f32[4096,256]{1,0:T(8,128)} custom-call(s32[3]{0:T(128)} %pad_add_fusion.place, f32[16,256,256]{2,1,0:T(8,128)} %local_back.1.partial, f32[8,256,256]{2,1,0:T(8,128)} %bitcast.48, f32[128,128]{1,0:T(8,128)} %bitcast.55, f32[2,256]{1,0:T(2,128)} %reshape.93.rates), custom_call_target="tpu_custom_call" | custom-call | tf_op jit(solution)/shard_map/final/pallas_call | solution.py:458
  (20 shorter events, 0.2 us)
Async XLA Ops:
  7.2 48.6 %all-gather.5.cloned.1.call-start = ((), (), s32[]{:S(2)}) async-start(), calls=%async_computation.4 | async-start | bytes 2359296 | tf_op jit(solution)/shard_map/all_gather | solution.py:531
  9.2 19.4 %copy-start.6 = (f32[64]{0:T(128)S(1)}, f32[64]{0:T(128)}, u32[]{:S(2)}) copy-start(f32[64]{0:T(128)} %param.16) | copy-start | bytes 772
  9.2 20.1 %copy-start.5 = (f32[4,64]{1,0:T(4,128)S(1)}, f32[4,64]{1,0:T(4,128)}, u32[]{:S(2)}) copy-start(f32[4,64]{1,0:T(4,128)} %param.15) | copy-start | bytes 3076
  9.2 20.8 %copy-start.4 = (f32[2,4,64]{2,1,0:T(4,128)S(1)}, f32[2,4,64]{2,1,0:T(4,128)}, u32[]{:S(2)}) copy-start(f32[2,4,64]{2,1,0:T(4,128)} %param.14) | copy-start | bytes 6148
  9.2 20.8 %copy-start.3 = (f32[4,64,64]{2,1,0:T(8,128)S(1)}, f32[4,64,64]{2,1,0:T(8,128)}, u32[]{:S(2)}) copy-start(f32[4,64,64]{2,1,0:T(8,128)} %param.13) | copy-start | bytes 196612
  17.1 21.0 %all-to-all-start = ((f32[128,1,128]{2,1,0:T(1,128)}), f32[128,1,128]{2,1,0:T(1,128)S(1)}, u32[]{:S(2)}, u32[]{:S(2)}) async-start(f32[128,1,128]{2,1,0:T(1,128)} %bitcast.59), calls=%async_computation | async-start | bytes 131072 | tf_op jit(solution)/shard_map/all_to_all | solution.py:505
  38.1 0.6 copy-start
  40.7 15.0 %all-to-all-start.1 = ((f32[128,1,128]{2,1,0:T(1,128)}), f32[128,1,128]{2,1,0:T(1,128)S(1)}, u32[]{:S(2)}, u32[]{:S(2)}) async-start(f32[128,1,128]{2,1,0:T(1,128)} %bitcast.56), calls=%async_computation.1 | async-start | bytes 131072 | tf_op jit(solution)/shard_map/all_to_all | solution.py:505
  45.1 61.4 %all-gather.7.cloned.1.call-start = ((), (), s32[]{:S(2)}) async-start(), calls=%async_computation.5 | async-start | bytes 2359296 | tf_op jit(solution)/shard_map/all_gather | solution.py:546
  55.7 0.6 copy-start.1
  91.2 15.3 %all-to-all-start.3 = ((f32[128,1,128]{2,1,0:T(1,128)}), f32[128,1,128]{2,1,0:T(1,128)S(1)}, u32[]{:S(2)}, u32[]{:S(2)}) async-start(f32[128,1,128]{2,1,0:T(1,128)} %bitcast.57), calls=%async_computation.3 | async-start | bytes 131072 | tf_op jit(solution)/shard_map/all_to_all | solution.py:505
  106.5 0.6 copy-start.2
Sparse Core Ops, SparseCore 0:
  17.2 29.4 all-gather.4
  69.7 27.6 all-gather.6
where the time goes:
time: 123 us; the launch traced here: 122 us
  Pallas kernels  54.5 us (44%)
  starting transfers between devices  20.6 us (17%)
  blocking collectives  19.7 us (16%)
  between operations  14.8 us (12%)
  local copies, waits for them, and re-layouts  6.19 us (5%)
  waiting for transfers between devices  5.83 us (5%)
    all_to_all x3, starting transfers between devices, everywhere(): lax.all_to_all(shaped, ('gx', 'gy'), split_axis=0, concat_axis=0, tiled=T...  20.5 us
    all_to_all x1, blocking collectives, everywhere(): lax.all_to_all(shaped, ('gx', 'gy'), split_axis=0, concat_axis=0, tiled=T...  19.7 us
    pallas_call x1, Pallas kernels, observations(): pl.pallas_call(observe_kernel, in_specs=[pl.BlockSpec(memory_space=pltpu....  13.2 us
    pallas_call x1, Pallas kernels, local(): pl.pallas_call(local_kernel, grid=(CH // BLOCK,), in_specs=[pl.BlockSpec(...  10.5 us
    pallas_call x1, Pallas kernels, local_back(): pl.pallas_call(local_back_kernel, grid=(CH // BLOCK,), in_specs=[pl.Block...  8.97 us
    pallas_call x1, Pallas kernels, final(): pl.pallas_call(final_kernel, grid=(CH // BLOCK,), in_specs=[pl.BlockSpec(...  8.22 us
    pallas_call x1, Pallas kernels, edges(): pl.pallas_call(edges_kernel, grid=(CH // BLOCK,), in_specs=[pl.BlockSpec(...  7.85 us
    all_to_all x3, waiting for transfers between devices, everywhere(): lax.all_to_all(shaped, ('gx', 'gy'), split_axis=0, concat_axis=0, tiled=T...  5.77 us
  transfers between devices with their start and end apart: 5, of which 1 were waited for; matrix products, arithmetic and copies ran while one was open for 3% of the time, Pallas kernels for 21%

commit v1 on v0

v1 whole, which is shorter than its diff:
```python
import functools

import jax
import jax.numpy as jnp
from jax import lax
from jax.experimental import pallas as pl
from jax.experimental.pallas import tpu as pltpu
from jax.sharding import PartitionSpec as P

highest = lax.Precision.HIGHEST
f32 = jnp.float32
bf16 = jnp.bfloat16

CH, LEVELS, XB, YB = 256, 64, 16, 256
OBS, PEERS, CAP = 512, 128, 8
N_X, N_Y = 8, 16
BLOCK = 32
REQ = 32
ROWS = 5
MIB = 1024 * 1024


def iota(shape, dim):
    return lax.broadcasted_iota(jnp.int32, shape, dim)


def split(value):
    high = value.astype(bf16)
    return high, (value - high.astype(f32)).astype(bf16)


def split3(value):
    high = value.astype(bf16)
    rest = value - high.astype(f32)
    middle = rest.astype(bf16)
    return high, middle, (rest - middle.astype(f32)).astype(bf16)


def mm(a, b):
    return jnp.dot(a, b, preferred_element_type=f32)


def mm_nt(a, b):
    return lax.dot_general(a, b, (((1,), (1,)), ((), ())), preferred_element_type=f32)


def wide(col):
    return jnp.concatenate([col, col], axis=1)


def upper():
    return jnp.where(iota((YB, YB), 0) <= iota((YB, YB), 1), 1.0, 0.0).astype(bf16)


def lower():
    return jnp.where(iota((YB, YB), 0) >= iota((YB, YB), 1), 1.0, 0.0).astype(bf16)


def softplus(x):
    return jnp.maximum(x, 0.0) + jnp.log1p(jnp.exp(-jnp.abs(x)))


def sigmoid(x):
    return 1.0 / (1.0 + jnp.exp(-x))


def take_plane(halves, x, rows, *lead):
    at = lead + (pl.ds(x, rows, stride=XB), slice(None))
    return jnp.concatenate([half[at] for half in halves], axis=1)


def params(mib, **more):
    return pltpu.CompilerParams(vmem_limit_bytes=mib * MIB, **more)


def whole(shape):
    return pl.BlockSpec(shape, lambda b: (0,) * len(shape))


VMEM = pl.BlockSpec(memory_space=pltpu.VMEM)
SMEM = pl.BlockSpec(memory_space=pltpu.SMEM)
ANY = pl.BlockSpec(memory_space=pl.ANY)
CONTROL = [
    pl.BlockSpec((BLOCK * XB, 128), lambda b: (b, 0)),
    pl.BlockSpec((BLOCK * XB, 128), lambda b: (b, 1)),
]
PLANES = pl.BlockSpec((XB, BLOCK, YB), lambda b: (0, b, 0))
STEPS = pl.BlockSpec((BLOCK, 128), lambda b: (b, 0))


def grow(step_y, rows, sign=1.0):
    return jnp.exp(wide(step_y) * (iota((rows, YB), 1).astype(f32) * sign))


def edges_kernel(control_a, control_b, rates, msg, colx, coly, line, tail):
    b = pl.program_id(0)

    @pl.when(b == 0)
    def _():
        for i, (out, count) in enumerate(((colx, 128.0), (coly, 4096.0))):
            for v in range(4):
                line[0:1, 0:LEVELS] = rates[i, v : v + 1, :]
                turned = jnp.broadcast_to(line[0:1, :], (128, 128)).T
                out[v * LEVELS : (v + 1) * LEVELS, :] = turned[0:LEVELS, :] * (1.0 / count)
        tail[...] = jnp.zeros((PEERS, 128), f32)

    rows = pl.ds(pl.multiple_of(b * BLOCK, BLOCK), BLOCK)
    factor = wide(jnp.exp(colx[rows, :]))
    scale = grow(coly[rows, :], BLOCK)
    running = jnp.zeros((BLOCK, YB), f32)
    place = iota((BLOCK, 128), 1) - 16 * (b // 4)
    sums = jnp.zeros((BLOCK, 128), f32)
    for x in range(XB):
        running = running + take_plane((control_a, control_b), x, BLOCK) * scale
        scale = scale * factor
        sums = jnp.where(place == x, jnp.sum(running, axis=1, keepdims=True), sums)
    start = (b % 4) * (BLOCK * ROWS) + 2 * (b // 4)
    msg[pl.ds(start, BLOCK, stride=ROWS), :] = running[:, :128]
    msg[pl.ds(start + 1, BLOCK, stride=ROWS), :] = running[:, 128:]
    back = pl.ds(pl.multiple_of((b % 4) * BLOCK, BLOCK), BLOCK)
    tail[back, :] = tail[back, :] + sums

    @pl.when(b == CH // BLOCK - 1)
    def _():
        msg[pl.ds(4, PEERS, stride=ROWS), :] = tail[...]


def edges(control, length_rates):
    return pl.pallas_call(
        edges_kernel,
        grid=(CH // BLOCK,),
        in_specs=CONTROL + [whole((2, 4, LEVELS))],
        out_specs=[whole((PEERS * ROWS, 128)), whole((CH, 128)), whole((CH, 128))],
        out_shape=[
            jax.ShapeDtypeStruct((PEERS * ROWS, 128), f32),
            jax.ShapeDtypeStruct((CH, 128), f32),
            jax.ShapeDtypeStruct((CH, 128), f32),
        ],
        scratch_shapes=[pltpu.VMEM((8, 128), f32), pltpu.VMEM((PEERS, 128), f32)],
        compiler_params=params(57),
        name="edges",
    )(control, control, length_rates)


def prepare_kernel(place, count, rates, owner, cell, flash, sigma, requests, rank_out, ahead, behind, down):
    live = iota((PEERS, OBS), 1) < count[0]
    chosen = (owner[...] == iota((PEERS, OBS), 0)) & live
    earlier = jnp.where(iota((OBS, OBS), 0) < iota((OBS, OBS), 1), 1.0, 0.0).astype(bf16)
    rank = mm(jnp.where(chosen, 1.0, 0.0).astype(bf16), earlier)
    rank = jnp.where(chosen, rank, -1.0)
    rank_out[...] = rank
    rows = iota((8, OBS), 0)
    values = jnp.where(
        rows == 0,
        cell[...].astype(f32) + 1.0,
        jnp.where(rows == 1, flash[...], jnp.where(rows == 2, sigma[...], 0.0)),
    )
    values = jnp.concatenate([values, jnp.zeros((120, OBS), f32)], axis=0)
    pieces = split3(jnp.concatenate([values[:, i : i + 128].T for i in range(0, OBS, 128)], axis=0))
    total = jnp.zeros((PEERS, 128), f32)
    for r in range(CAP):
        taken = jnp.where(rank == float(r), 1.0, 0.0).astype(bf16)
        found = (mm(taken, pieces[0]) + mm(taken, pieces[1])) + mm(taken, pieces[2])
        total = total + pltpu.roll(found, REQ + 3 * r, 1)
    requests[...] = total

    me = place[2]
    d, e = iota((PEERS, PEERS), 0), iota((PEERS, PEERS), 1)
    far_x = (d // N_Y) - (e // N_Y)
    far_y = (d % N_Y) - (e % N_Y)
    for c in range(2):
        mine = iota((2, CH), 1) == me + 128 * c
        rate = jnp.sum(jnp.where(mine, rates[...], 0.0), axis=1, keepdims=True)
        down_x = rate[0:1, :] * (XB / 128.0)
        down_y = rate[1:2, :] * (YB / 4096.0)
        down[c : c + 1, :] = jnp.broadcast_to(jnp.exp(-down_x), (1, 128))
        along = jnp.exp(-jnp.abs(far_y).astype(f32) * down_y)
        across = along * jnp.exp(-jnp.abs(far_x).astype(f32) * down_x)
        for out, sign in ((ahead, 1), (behind, -1)):
            past_x, past_y = far_x * sign > 0, far_y * sign > 0
            out[:, 256 * c : 256 * c + 128] = jnp.where((far_x == 0) & past_y, along, 0.0)
            out[:, 256 * c + 128 : 256 * c + 256] = jnp.where(past_x & past_y, across, 0.0)
    down[2:8, :] = jnp.zeros((6, 128), f32)


def prepare(place, count, rates, owner, cell, flash, sigma):
    return pl.pallas_call(
        prepare_kernel,
        in_specs=[SMEM, SMEM] + [VMEM] * 5,
        out_specs=[VMEM] * 5,
        out_shape=[
            jax.ShapeDtypeStruct((PEERS, 128), f32),
            jax.ShapeDtypeStruct((PEERS, OBS), f32),
            jax.ShapeDtypeStruct((PEERS, 4 * 128), f32),
            jax.ShapeDtypeStruct((PEERS, 4 * 128), f32),
            jax.ShapeDtypeStruct((8, 128), f32),
        ],
        compiler_params=params(16),
        cost_estimate=pl.CostEstimate(flops=1 << 30, bytes_accessed=1 << 20, transcendentals=1 << 16),
        name="prepare",
    )(place, count, rates, owner, cell, flash, sigma)


def local_kernel(
    control_a, control_b, colx, coly, rates, background_a, background_b, weights, matrix, matrix_t, steps,
    cc, share, mh, ml, th, tl,
):
    b = pl.program_id(0)
    factor = wide(jnp.exp(colx[...]))
    scale = grow(coly[...], BLOCK)
    running = jnp.zeros((BLOCK, YB), f32)
    sums = upper()
    highs, lows = [], []
    for x in range(XB):
        running = running + take_plane((control_a, control_b), x, BLOCK) * scale
        scale = scale * factor
        high, low = split(running)
        highs.append(high)
        lows.append(low)
    summed = mm(jnp.concatenate(highs, axis=0), sums) + mm(jnp.concatenate(lows, axis=0), sums)
    cc[...] = summed.reshape(XB, BLOCK, YB)
    for x in range(XB):
        part = jnp.zeros((8, YB), f32)
        for v in range(4):
            part = part + take_plane((background_a, background_b), x, 8, v) * weights[:, v : v + 1]
        share[x] = part
    for i in range(2):
        x = (2 * b + i).astype(f32)
        mh[i], ml[i] = split(matrix[...] * jnp.exp(rates[0:1, :] * (x * (-1.0 / 128.0))))
        th[i], tl[i] = split(matrix_t[...] * jnp.exp(steps[:, :LEVELS] * -x))


def local(control, colx, coly, rates, background, weights, matrix, matrix_t):
    return pl.pallas_call(
        local_kernel,
        grid=(CH // BLOCK,),
        in_specs=CONTROL
        + [
            STEPS,
            STEPS,
            whole((2, CH)),
            pl.BlockSpec((4, 128, 128), lambda b: (0, b, 0)),
            pl.BlockSpec((4, 128, 128), lambda b: (0, b, 1)),
            pl.BlockSpec((8, 4), lambda b: (b, 0)),
            whole((LEVELS, CH)),
            whole((CH, LEVELS)),
            whole((CH, 128)),
        ],
        out_specs=[
            PLANES,
            pl.BlockSpec((XB, 8, YB), lambda b: (0, b, 0)),
            pl.BlockSpec((2, LEVELS, CH), lambda b: (b, 0, 0)),
            pl.BlockSpec((2, LEVELS, CH), lambda b: (b, 0, 0)),
            pl.BlockSpec((2, CH, LEVELS), lambda b: (b, 0, 0)),
            pl.BlockSpec((2, CH, LEVELS), lambda b: (b, 0, 0)),
        ],
        out_shape=[
            jax.ShapeDtypeStruct((XB, CH, YB), f32),
            jax.ShapeDtypeStruct((XB, LEVELS, YB), f32),
            jax.ShapeDtypeStruct((XB, LEVELS, CH), bf16),
            jax.ShapeDtypeStruct((XB, LEVELS, CH), bf16),
            jax.ShapeDtypeStruct((XB, CH, LEVELS), bf16),
            jax.ShapeDtypeStruct((XB, CH, LEVELS), bf16),
        ],
        compiler_params=params(57),
        cost_estimate=pl.CostEstimate(flops=2 * 2 * 4096 * 256 * 256, bytes_accessed=15 << 20, transcendentals=1 << 20),
        name="local",
    )(control, control, colx, coly, rates, background, background, weights, matrix, matrix_t, colx)


def carry_kernel(reverse, sums, weights, down, requests, out):
    order = list(range(N_X))
    if reverse:
        order = order[::-1]
    for row in range(4):
        decay = down[row // 2 : row // 2 + 1, :]
        total = jnp.zeros((N_Y, 128), f32)
        for g in order:
            at = pl.ds(g * N_Y * ROWS + row, N_Y, stride=ROWS)
            out[at, :] = total
            total = decay * (total + sums[at, :])
    tail = sums[pl.ds(4, PEERS, stride=ROWS), :]
    lanes = iota((PEERS, 128), 1)
    right = []
    for c in range(2):
        own = (lanes >= 16 * c) & (lanes < 16 * c + 16)
        right.append(jnp.where(own, tail, 0.0))
        last = 16 * c if reverse else 16 * c + 15
        total = jnp.sum(jnp.where(lanes == last, tail, 0.0), axis=1, keepdims=True)
        right.append(jnp.where(own, total, 0.0))
    entering = jnp.dot(
        weights[...], jnp.concatenate(right, axis=0), precision=highest, preferred_element_type=f32
    )
    if requests is not None:
        entering = entering + requests[...]
    out[pl.ds(4, PEERS, stride=ROWS), :] = entering


def carry(sums, weights, down, requests=None):
    shape = jax.ShapeDtypeStruct((PEERS * ROWS, 128), f32)
    if requests is None:
        kernel = lambda *refs: carry_kernel(True, *refs[:3], None, refs[3])
        return pl.pallas_call(
            kernel, in_specs=[VMEM] * 3, out_specs=VMEM, out_shape=shape,
            compiler_params=params(8), name="carry_back",
        )(sums, weights, down)
    return pl.pallas_call(
        functools.partial(carry_kernel, False), in_specs=[VMEM] * 4, out_specs=VMEM, out_shape=shape,
        compiler_params=params(8), name="carry",
    )(sums, weights, down, requests)


def observe_kernel(
    cc_hbm, share_hbm, mh_hbm, ml_hbm, th, tl, entered, coly, level_weights,
    running_hbm, msg, lh, ll, forced, cc, share, mh, ml, running_out, sems, out_sems,
):
    def arrivals(x):
        return [
            pltpu.make_async_copy(source.at[x], target.at[x], sems.at[x, i])
            for i, (source, target) in enumerate(
                ((cc_hbm, cc), (share_hbm, share), (mh_hbm, mh), (ml_hbm, ml))
            )
        ]

    for x in range(XB):
        for copy in arrivals(x):
            copy.start()

    decay_y = grow(coly[...], CH, -1.0)
    entering = jnp.concatenate(
        [
            jnp.concatenate(
                [entered[pl.ds(2 * c + h, PEERS, stride=ROWS), :] for h in range(2)], axis=1
            )
            for c in range(2)
        ],
        axis=0,
    )
    tail = entered[pl.ds(4, PEERS, stride=ROWS), :]
    high, low = split(entering)
    sums = upper()
    entering = mm(high, sums) + mm(low, sums)

    for x in range(XB):
        for copy in arrivals(x):
            copy.wait()
        col = jnp.concatenate([tail[:, x : x + 1], tail[:, 16 + x : 17 + x]], axis=0)
        smooth = decay_y * ((cc[x] + entering) + col)
        high, low = split(smooth)
        level = (mm(mh[x], high) + (mm(ml[x], high) + mm(mh[x], low))) + share[x]
        at = slice(x * LEVELS, (x + 1) * LEVELS)
        lh[at, :], ll[at, :] = split(level)

    requests = tail.T
    weights = level_weights[...]
    departures = []
    for r in range(0, CAP, 2):
        first, second = REQ + 3 * r, REQ + 3 * r + 3
        row = lambda i: jnp.concatenate(
            [requests[first + i : first + i + 1, :], requests[second + i : second + i + 1, :]], axis=1
        )
        where = row(0).astype(jnp.int32) - 1
        valid = where >= 0
        at_x, at_y = where // YB, where % YB
        at_x = jnp.where(valid, at_x, -1)
        chosen = jnp.where(iota((YB, 256), 0) == at_y, 1.0, 0.0).astype(bf16)
        picked = mm(lh[...], chosen) + mm(ll[...], chosen)
        levels = jnp.zeros((LEVELS, 256), f32)
        for x in range(XB):
            levels = jnp.where(at_x == x, picked[x * LEVELS : (x + 1) * LEVELS, :], levels)
        total = jnp.sum(weights * softplus(levels), axis=0, keepdims=True)
        miss = jnp.where(valid, softplus(total) - row(1), 0.0)
        error = jnp.where(valid, row(2), 1.0)
        scale = miss / (error * error) * sigmoid(total)
        adjoint = scale * (weights * sigmoid(levels))
        high = adjoint.astype(bf16).astype(f32)
        low = adjoint - high
        spread_high = jnp.concatenate([jnp.where(at_x == x, high, 0.0).astype(bf16) for x in range(XB)], axis=0)
        spread_low = jnp.concatenate([jnp.where(at_x == x, low, 0.0).astype(bf16) for x in range(XB)], axis=0)
        part = mm_nt(spread_high, chosen) + mm_nt(spread_low, chosen)
        if r == 0:
            forced[...] = part
        else:
            forced[...] = forced[...] + part
        departures += [miss[:, :128], miss[:, 128:]]

    def leaving(x):
        return pltpu.make_async_copy(running_out.at[x], running_hbm.at[x], out_sems.at[x])

    running = jnp.zeros((CH, YB), f32)
    lanes = iota((PEERS, 128), 1)
    message = pltpu.roll(
        jnp.concatenate(departures + [jnp.zeros((120, 128), f32)], axis=0).T, REQ, 1
    )
    for x in range(XB - 1, -1, -1):
        high, low = split(forced[x * LEVELS : (x + 1) * LEVELS, :])
        back = mm(th[x], high) + (mm(tl[x], high) + mm(th[x], low))
        running = running + back * decay_y
        running_out[x] = running
        leaving(x).start()
        total = jnp.sum(running, axis=1, keepdims=True)
        message = jnp.where(lanes == x, total[:128], message)
        message = jnp.where(lanes == 16 + x, total[128:], message)
    for c in range(2):
        for h in range(2):
            msg[pl.ds(2 * c + h, PEERS, stride=ROWS), :] = running[128 * c : 128 * c + 128, 128 * h : 128 * h + 128]
    msg[pl.ds(4, PEERS, stride=ROWS), :] = message
    for x in range(XB):
        leaving(x).wait()


def observations(cc, share, mh, ml, th, tl, entered, coly, level_weights):
    return pl.pallas_call(
        observe_kernel,
        in_specs=[ANY] * 4 + [VMEM] * 5,
        out_specs=[ANY, VMEM],
        out_shape=[
            jax.ShapeDtypeStruct((XB, CH, YB), f32),
            jax.ShapeDtypeStruct((PEERS * ROWS, 128), f32),
        ],
        scratch_shapes=[
            pltpu.VMEM((XB * LEVELS, YB), bf16),
            pltpu.VMEM((XB * LEVELS, YB), bf16),
            pltpu.VMEM((XB * LEVELS, YB), f32),
            pltpu.VMEM((XB, CH, YB), f32),
            pltpu.VMEM((XB, LEVELS, YB), f32),
            pltpu.VMEM((XB, LEVELS, CH), bf16),
            pltpu.VMEM((XB, LEVELS, CH), bf16),
            pltpu.VMEM((XB, CH, YB), f32),
            pltpu.SemaphoreType.DMA((XB, 4)),
            pltpu.SemaphoreType.DMA((XB,)),
        ],
        compiler_params=params(57),
        name="observations",
    )(cc, share, mh, ml, th, tl, entered, coly, level_weights)


def local_back_kernel(control_a, control_b, running, colx, coly, out):
    high, low = split(running[...].reshape(XB * BLOCK, YB))
    sums = lower()
    summed = mm(high, sums) + mm(low, sums)
    factor = wide(jnp.exp(colx[...]))
    scale = grow(coly[...], BLOCK)
    for x in range(XB):
        plane = take_plane((control_a, control_b), x, BLOCK)
        out[x] = plane + scale * summed[x * BLOCK : (x + 1) * BLOCK, :]
        scale = scale * factor


def local_back(control, running, colx, coly):
    return pl.pallas_call(
        local_back_kernel,
        grid=(CH // BLOCK,),
        in_specs=CONTROL + [PLANES, STEPS, STEPS],
        out_specs=PLANES,
        out_shape=jax.ShapeDtypeStruct((XB, CH, YB), f32),
        compiler_params=params(57),
        cost_estimate=pl.CostEstimate(flops=2 * 2 * 4096 * 256 * 256, bytes_accessed=12 << 20, transcendentals=1 << 20),
        name="local_back",
    )(control, control, running, colx, coly)


def final_kernel(partial, entered, colx, coly, out, whole_a, whole_b, sems):
    b = pl.program_id(0)
    start = (b % 4) * (BLOCK * ROWS)
    entering = jnp.concatenate(
        [entered[pl.ds(start + 2 * (b // 4) + h, BLOCK, stride=ROWS), :] for h in range(2)], axis=1
    )
    high, low = split(entering)
    sums = lower()
    entering = mm(high, sums) + mm(low, sums)
    tail = entered[pl.ds(start + 4, BLOCK, stride=ROWS), :]
    mine = jnp.where(b < 4, tail, pltpu.roll(tail, 112, 1))
    factor = wide(jnp.exp(colx[...]))
    scale = grow(coly[...], BLOCK)
    for x in range(XB):
        plane = partial[x] + scale * (entering + mine[:, x : x + 1])
        scale = scale * factor
        at = pl.ds(b * (BLOCK * XB) + x, BLOCK, stride=XB)
        whole_a[at, :] = plane[:, :128]
        whole_b[at, :] = plane[:, 128:]

    def copies(step):
        at = pl.ds(pl.multiple_of(step * (BLOCK * XB), BLOCK * XB), BLOCK * XB)
        return (
            pltpu.make_async_copy(whole_a.at[at, :], out.at[at, pl.ds(0, 128)], sems.at[step, 0]),
            pltpu.make_async_copy(whole_b.at[at, :], out.at[at, pl.ds(128, 128)], sems.at[step, 1]),
        )

    for copy in copies(b):
        copy.start()

    @pl.when(b == CH // BLOCK - 1)
    def _():
        for step in range(CH // BLOCK):
            for copy in copies(step):
                copy.wait()


def final(partial, entered, colx, coly):
    return pl.pallas_call(
        final_kernel,
        grid=(CH // BLOCK,),
        in_specs=[PLANES, whole((PEERS * ROWS, 128)), STEPS, STEPS],
        out_specs=ANY,
        out_shape=jax.ShapeDtypeStruct((CH * XB, YB), f32),
        scratch_shapes=[
            pltpu.VMEM((CH * XB, 128), f32),
            pltpu.VMEM((CH * XB, 128), f32),
            pltpu.SemaphoreType.DMA((CH // BLOCK, 2)),
        ],
        compiler_params=params(57),
        name="final",
    )(partial, entered, colx, coly)


def departures_kernel(rank, returned, out):
    total = jnp.zeros((1, OBS), f32)
    values = returned[pl.ds(4, PEERS, stride=ROWS), :]
    for r in range(CAP):
        value = values[:, REQ + r : REQ + r + 1]
        total = total + jnp.sum(jnp.where(rank[...] == float(r), value, 0.0), axis=0, keepdims=True)
    out[...] = total


def departures(rank, returned):
    return pl.pallas_call(
        departures_kernel,
        in_specs=[VMEM] * 2,
        out_specs=VMEM,
        out_shape=jax.ShapeDtypeStruct((1, OBS), f32),
        compiler_params=params(8),
        cost_estimate=pl.CostEstimate(flops=1 << 20, bytes_accessed=1 << 19, transcendentals=0),
        name="departures",
    )(rank, returned)


def everywhere(rows):
    shaped = rows.reshape(PEERS * ROWS, 1, 128)
    moved = lax.all_to_all(shaped, ("gx", "gy"), split_axis=0, concat_axis=0, tiled=True)
    return moved.reshape(PEERS * ROWS, 128)


def body(
    control,
    background,
    vert_factor,
    length_rates,
    flash_weights,
    level_weights,
    obs_owner,
    obs_cell,
    obs_count,
    flash_obs,
    obs_error,
):
    shape = control.shape
    flat = control.reshape(CH * XB, YB)
    msg, colx, coly = edges(flat, length_rates)
    asked = everywhere(msg)

    gx, gy = lax.axis_index("gx"), lax.axis_index("gy")
    place = jnp.stack([gx, gy, gx * N_Y + gy]).astype(jnp.int32)
    rates = length_rates.reshape(2, CH)
    requests, rank, ahead, behind, down = prepare(
        place, obs_count, rates, obs_owner.reshape(1, OBS), obs_cell.reshape(1, OBS),
        flash_obs.reshape(1, OBS), obs_error.reshape(1, OBS),
    )
    step_x, step_y = length_rates[0] / (XB * N_X), length_rates[1] / (YB * N_Y)
    gain = jnp.sqrt(-jnp.expm1(-2.0 * step_x)) * jnp.sqrt(-jnp.expm1(-2.0 * step_y))
    mixed = flash_weights[:, :, None] * vert_factor * gain[:, None, :]
    matrix = mixed.transpose(1, 0, 2).reshape(LEVELS, CH)
    matrix_t = mixed.transpose(0, 2, 1).reshape(CH, LEVELS)
    cc, share, mh, ml, th, tl = local(
        flat, colx, coly, rates, background.reshape(4, LEVELS * XB, YB), flash_weights.T, matrix, matrix_t
    )
    entered = everywhere(carry(asked, ahead, down, requests))
    running, msg_back = observations(
        cc, share, mh, ml, th, tl, entered, coly, level_weights.reshape(LEVELS, 1)
    )
    returned = everywhere(msg_back)
    partial = local_back(flat, running, colx, coly)
    entered_back = everywhere(carry(returned, behind, down))
    departure = departures(rank, returned)
    grad = final(partial, entered_back, colx, coly)
    return (grad.reshape(shape), departure.reshape(OBS))


def solution(mesh):
    placed = (
        P(None, None, "gx", "gy"),
        P(None, None, "gx", "gy"),
        P(),
        P(),
        P(),
        P(),
        P(("gx", "gy"), None),
        P(("gx", "gy")),
        P(("gx", "gy")),
        P(("gx", "gy")),
        P(("gx", "gy")),
    )
    return jax.shard_map(
        body,
        mesh=mesh,
        in_specs=placed,
        out_specs=(P(None, None, "gx", "gy"), P(("gx", "gy"))),
        check_vma=False,
    )
```

time: 123 us -> 113 us (0.919)
  between operations: 14.8 us -> 1.62 us
  waiting for transfers between devices: 5.83 us -> 9.19 us
  local copies, waits for them, and re-layouts: 6.19 us -> 4.58 us
  blocking collectives: 19.7 us -> 21.2 us
    all_to_all x3, waiting for transfers between devices: 5.77 us -> 9.19 us  [everywhere(): lax.all_to_all(shaped, ('gx', 'gy'), split_axis=0, concat_axis=0, tiled=T...]
    all_to_all x1, blocking collectives: 19.7 us -> 21.2 us  [everywhere(): lax.all_to_all(shaped, ('gx', 'gy'), split_axis=0, concat_axis=0, tiled=T...]
    reshape x1, local copies, waits for them, and re-layouts: 1.34 us -> 0.08 us  [body(): rates = length_rates.reshape(2, CH)]
    unnamed x15 -> x23, local copies, waits for them, and re-layouts: 2.55 us -> 2.2 us
    pallas_call x8 -> x9, Pallas kernels: 54.5 us -> 54.2 us  [the longest x1 15.3 us: observations(): pl.pallas_call(observe_kernel, in_specs=[ANY] * 4 + [VMEM] * 5, out_specs...]
  transfers between devices with their start and end apart: 5 -> 3, of which waited for: 1 -> 2; matrix products, arithmetic and copies ran while one was open for 3% -> 3% of each run, Pallas kernels for 21% -> 20%
where the time goes in v1:
time: 113 us; the launch traced here: 112 us
  Pallas kernels  54.2 us (48%)
  blocking collectives  21.2 us (19%)
  starting transfers between devices  20.9 us (18%)
  waiting for transfers between devices  9.19 us (8%)
  local copies, waits for them, and re-layouts  4.58 us (4%)
  between operations  1.62 us (1%)
    all_to_all x1, blocking collectives, everywhere(): lax.all_to_all(shaped, ('gx', 'gy'), split_axis=0, concat_axis=0, tiled=T...  21.2 us
    all_to_all x3, starting transfers between devices, everywhere(): lax.all_to_all(shaped, ('gx', 'gy'), split_axis=0, concat_axis=0, tiled=T...  20.9 us
    pallas_call x1, Pallas kernels, observations(): pl.pallas_call(observe_kernel, in_specs=[ANY] * 4 + [VMEM] * 5, out_specs...  15.3 us
    pallas_call x1, Pallas kernels, local(): pl.pallas_call(local_kernel, grid=(CH // BLOCK,), in_specs=CONTROL + [STE...  10.8 us
    all_to_all x3, waiting for transfers between devices, everywhere(): lax.all_to_all(shaped, ('gx', 'gy'), split_axis=0, concat_axis=0, tiled=T...  9.19 us
    pallas_call x1, Pallas kernels, local_back(): pl.pallas_call(local_back_kernel, grid=(CH // BLOCK,), in_specs=CONTROL +...  8.6 us
    pallas_call x1, Pallas kernels, final(): pl.pallas_call(final_kernel, grid=(CH // BLOCK,), in_specs=[PLANES, whole...  7.77 us
    pallas_call x1, Pallas kernels, edges(): pl.pallas_call(edges_kernel, grid=(CH // BLOCK,), in_specs=CONTROL + [who...  6.56 us
  transfers between devices with their start and end apart: 3, of which 2 were waited for; matrix products, arithmetic and copies ran while one was open for 3% of the time, Pallas kernels for 20%

profile of v1, /device:TPU:1, one launch (start us, length us, event | category | flops | bytes accessed | tf_op | source)
XLA Modules:
  0.0 111.9 jit_solution(5583985970299104776)
XLA Ops:
  0.7 6.6 %edges.1 = (f32[640,128]{1,0:T(8,128)}, f32[256,128]{1,0:T(8,128)}, f32[256,128]{1,0:T(8,128)}) custom-call(f32[4096,256]{1,0:T(8,128)} %bitcast.43, f32[4096,256]{1,0:T(8,128)} %bitcast.44, f32[2,4,64]{2,1,0:T(4,128)} %rates.1), custom_call_target="tpu_custom_call" | custom-call | tf_op jit(solution)/shard_map/edges/pallas_call | solution.py:129
  7.3 11.5 %all-to-all-start = ((f32[640,1,128]{2,1,0:T(1,128)}), f32[640,1,128]{2,1,0:T(1,128)S(1)}, u32[]{:S(2)}, u32[]{:S(2)}) async-start(f32[640,1,128]{2,1,0:T(1,128)} %bitcast.55), calls=%async_computation | async-start | bytes 655360 | tf_op jit(solution)/shard_map/all_to_all | solution.py:540
  18.8 0.1 reshape.93.rates
  19.5 0.7 copy.22.level_weights
  20.2 0.7 copy.17
  21.0 1.9 %prepare.1 = (f32[128,128]{1,0:T(8,128)S(1)}, f32[128,512]{1,0:T(8,128)S(1)}, f32[128,512]{1,0:T(8,128)S(1)}, f32[128,512]{1,0:T(8,128)S(1)}, f32[8,128]{1,0:T(8,128)S(1)}) custom-call(s32[3]{0:T(128)S(1)} %pad_add_fusion.place, s32[1]{0:T(128)S(6)} %copy.25.count, f32[2,256]{1,0:T(2,128)S(1)} %reshape.93.rates, s32[1,512]{1,0:T(1,128)S(1)} %bitcast.39, ...), custom_call_target="tpu_custom_call" | custom-call | flops 1073741824 | bytes 1048576 | tf_op jit(solution)/shard_map/prepare/pallas_call | solution.py:187
  22.9 7.2 %all-to-all-done = f32[640,1,128]{2,1,0:T(1,128)S(1)} async-done(((f32[640,1,128]{2,1,0:T(1,128)}), f32[640,1,128]{2,1,0:T(1,128)S(1)}, u32[]{:S(2)}, u32[]{:S(2)}) %all-to-all-start) | async-done | bytes 327712 | tf_op jit(solution)/shard_map/all_to_all | solution.py:540
  30.1 1.2 %carry.1 = f32[640,128]{1,0:T(8,128)} custom-call(f32[640,128]{1,0:T(8,128)S(1)} %bitcast.38, f32[128,512]{1,0:T(8,128)S(1)} %get-tuple-element.27.weights, f32[8,128]{1,0:T(8,128)S(1)} %get-tuple-element.28.down.refs_2_, f32[128,128]{1,0:T(8,128)S(1)} %get-tuple-element.29.requests), custom_call_target="tpu_custom_call" | custom-call | tf_op jit(solution)/shard_map/carry/pallas_call | solution.py:307
  31.3 4.7 %all-to-all-start.1 = ((f32[640,1,128]{2,1,0:T(1,128)}), f32[640,1,128]{2,1,0:T(1,128)S(1)}, u32[]{:S(2)}, u32[]{:S(2)}) async-start(f32[640,1,128]{2,1,0:T(1,128)} %bitcast.18), calls=%async_computation.1 | async-start | bytes 655360 | tf_op jit(solution)/shard_map/all_to_all | solution.py:540
  36.0 0.1 fusion
  36.1 0.8 copy.19
  36.9 0.1 copy.18
  37.0 0.8 reshape.95.matrix
  37.7 10.8 %local.1 = (f32[16,256,256]{2,1,0:T(8,128)}, f32[16,64,256]{2,1,0:T(8,128)}, bf16[16,64,256]{2,1,0:T(8,128)(2,1)}, bf16[16,64,256]{2,1,0:T(8,128)(2,1)}, bf16[16...) custom-call(f32[4096,256]{1,0:T(8,128)} %bitcast.45, f32[4096,256]{1,0:T(8,128)} %bitcast.46, ...), custom_call_target="tpu_custom_call" | custom-call | flops 1073741824 | bytes 15728640 | tf_op jit(solution)/shard_map/local/pallas_call | solution.py:234
  48.6 0.7 copy-done.5
  49.3 15.3 %observations.1 = (f32[16,256,256]{2,1,0:T(8,128)}, f32[640,128]{1,0:T(8,128)}) custom-call(f32[16,256,256]{2,1,0:T(8,128)} %get-tuple-element.20.cc_hbm, f32[16,64,256]{2,1,0:T(8,128)} %get-tuple-element.21.share_hbm, bf16[16,64,256]{2,1,0:T(8,128)(2,1)} %get-tuple-element.22.mh_hbm, bf16[16,64,256]{2,1,0:T(8,128)(2,1)} %get-tuple-element.23.ml_hbm, ...), custom_call_target="tpu_custom_call" | custom-call | tf_op jit(solution)/shard_map/observations/pallas_call | solution.py:413
  64.6 21.2 %all_to_all.20 = f32[640,1,128]{2,1,0:T(1,128)S(1)} all-to-all(f32[640,1,128]{2,1,0:T(1,128)} %bitcast.56), channel_id=1, replica_groups=mesh['gx'=8,'gy'=16] {'gx','gy'}, dimensions={0} | all-to-all | bytes 655360 | tf_op jit(solution)/shard_map/all_to_all | solution.py:540
  85.9 1.2 %carry_back.1 = f32[640,128]{1,0:T(8,128)} custom-call(f32[640,128]{1,0:T(8,128)S(1)} %bitcast.36, f32[128,512]{1,0:T(8,128)S(1)} %get-tuple-element.32.refs_1_, f32[8,128]{1,0:T(8,128)S(1)} %get-tuple-element.28.down.refs_2_), custom_call_target="tpu_custom_call" | custom-call | tf_op jit(solution)/shard_map/carry_back/pallas_call | solution.py:303
  87.1 4.7 %all-to-all-start.3 = ((f32[640,1,128]{2,1,0:T(1,128)}), f32[640,1,128]{2,1,0:T(1,128)S(1)}, u32[]{:S(2)}, u32[]{:S(2)}) async-start(f32[640,1,128]{2,1,0:T(1,128)} %bitcast.25), calls=%async_computation.3 | async-start | bytes 655360 | tf_op jit(solution)/shard_map/all_to_all | solution.py:540
  91.8 8.6 %local_back.1.partial = f32[16,256,256]{2,1,0:T(8,128)} custom-call(f32[4096,256]{1,0:T(8,128)} %bitcast.47, f32[4096,256]{1,0:T(8,128)} %bitcast.48, f32[16,256,256]{2,1,0:T(8,128)} %get-tuple-element.30.running, f32[256,128]{1,0:T(8,128)} %get-tuple-element.18.colx.steps, f32[256,128]{1,0:T(8,128)} %get-tuple-element.19.coly), custom_call_target="tpu_custom_call" | custom-call | flops 1073741824 | bytes 12582912 | tf_op jit(solution)/shard_map/local_back/pallas_call | solution.py:451
  100.4 0.9 departures.1
  101.2 2.0 %all-to-all-done.3 = f32[640,1,128]{2,1,0:T(1,128)S(1)} async-done(((f32[640,1,128]{2,1,0:T(1,128)}), f32[640,1,128]{2,1,0:T(1,128)S(1)}, u32[]{:S(2)}, u32[]{:S(2)}) %all-to-all-start.3) | async-done | bytes 327712 | tf_op jit(solution)/shard_map/all_to_all | solution.py:540
  103.3 0.7 copy-done.6
  104.0 7.8 %final.1 = f32[4096,256]{1,0:T(8,128)} custom-call(f32[16,256,256]{2,1,0:T(8,128)} %local_back.1.partial, f32[640,128]{1,0:T(8,128)} %bitcast.53, f32[256,128]{1,0:T(8,128)} %get-tuple-element.18.colx.steps, f32[256,128]{1,0:T(8,128)} %get-tuple-element.19.coly), custom_call_target="tpu_custom_call" | custom-call | tf_op jit(solution)/shard_map/final/pallas_call | solution.py:501
  (23 shorter events, 0.1 us)
Async XLA Ops:
  0.6 18.1 %copy-start.8 = (f32[2,4,64]{2,1,0:T(4,128)S(1)}, f32[2,4,64]{2,1,0:T(4,128)}, u32[]{:S(2)}) copy-start(f32[2,4,64]{2,1,0:T(4,128)} %rates.1) | copy-start | bytes 6148
  0.6 18.9 %copy-start.10 = (f32[64]{0:T(128)S(1)}, f32[64]{0:T(128)}, u32[]{:S(2)}) copy-start(f32[64]{0:T(128)} %param.16) | copy-start | bytes 772
  0.7 19.6 %copy-start.9 = (f32[4,64]{1,0:T(4,128)S(1)}, f32[4,64]{1,0:T(4,128)}, u32[]{:S(2)}) copy-start(f32[4,64]{1,0:T(4,128)} %param.15) | copy-start | bytes 3076
  0.7 20.3 %copy-start.1 = (s32[512,1]{0,1:T(1,128)S(1)}, s32[512,1]{0,1:T(1,128)}, u32[]{:S(2)}) copy-start(s32[512,1]{0,1:T(1,128)} %param.17) | copy-start | bytes 6148
  0.7 20.3 %copy-start.2 = (s32[512]{0:T(512)S(1)}, s32[512]{0:T(512)}, u32[]{:S(2)}) copy-start(s32[512]{0:T(512)} %param.18) | copy-start | bytes 6148
  0.7 20.3 %copy-start.3 = (f32[512]{0:T(512)S(1)}, f32[512]{0:T(512)}, u32[]{:S(2)}) copy-start(f32[512]{0:T(512)} %param.20) | copy-start | bytes 6148
  0.7 20.3 %copy-start.4 = (f32[512]{0:T(512)S(1)}, f32[512]{0:T(512)}, u32[]{:S(2)}) copy-start(f32[512]{0:T(512)} %param.21) | copy-start | bytes 6148
  7.3 28.8 %copy-start.7 = (f32[4,64,64]{2,1,0:T(8,128)S(1)}, f32[4,64,64]{2,1,0:T(8,128)}, u32[]{:S(2)}) copy-start(f32[4,64,64]{2,1,0:T(8,128)} %param.13) | copy-start | bytes 196612
  7.3 22.9 %all-to-all-start = ((f32[640,1,128]{2,1,0:T(1,128)}), f32[640,1,128]{2,1,0:T(1,128)S(1)}, u32[]{:S(2)}, u32[]{:S(2)}) async-start(f32[640,1,128]{2,1,0:T(1,128)} %bitcast.55), calls=%async_computation | async-start | bytes 655360 | tf_op jit(solution)/shard_map/all_to_all | solution.py:540
  18.9 18.9 %copy-start = (f32[2,256]{1,0:T(2,128)}, f32[2,256]{1,0:T(2,128)S(1)}, u32[]{:S(2)}) copy-start(f32[2,256]{1,0:T(2,128)S(1)} %reshape.93.rates) | copy-start | bytes 6148
  31.3 17.2 %all-to-all-start.1 = ((f32[640,1,128]{2,1,0:T(1,128)}), f32[640,1,128]{2,1,0:T(1,128)S(1)}, u32[]{:S(2)}, u32[]{:S(2)}) async-start(f32[640,1,128]{2,1,0:T(1,128)} %bitcast.18), calls=%async_computation.1 | async-start | bytes 655360 | tf_op jit(solution)/shard_map/all_to_all | solution.py:540
  48.6 0.7 copy-start.5
  87.1 16.2 %all-to-all-start.3 = ((f32[640,1,128]{2,1,0:T(1,128)}), f32[640,1,128]{2,1,0:T(1,128)S(1)}, u32[]{:S(2)}, u32[]{:S(2)}) async-start(f32[640,1,128]{2,1,0:T(1,128)} %bitcast.25), calls=%async_computation.3 | async-start | bytes 655360 | tf_op jit(solution)/shard_map/all_to_all | solution.py:540
  103.3 0.7 copy-start.6

commit v2 on v1

--- a/solution.py
+++ b/solution.py
@@ -201,11 +201,7 @@
     )(place, count, rates, owner, cell, flash, sigma)
 
 
-def local_kernel(
-    control_a, control_b, colx, coly, rates, background_a, background_b, weights, matrix, matrix_t, steps,
-    cc, share, mh, ml, th, tl,
-):
-    b = pl.program_id(0)
+def local_kernel(control_a, control_b, colx, coly, cc):
     factor = wide(jnp.exp(colx[...]))
     scale = grow(coly[...], BLOCK)
     running = jnp.zeros((BLOCK, YB), f32)
@@ -219,53 +215,84 @@
         lows.append(low)
     summed = mm(jnp.concatenate(highs, axis=0), sums) + mm(jnp.concatenate(lows, axis=0), sums)
     cc[...] = summed.reshape(XB, BLOCK, YB)
+
+
+def local(control, colx, coly):
+    return pl.pallas_call(
+        local_kernel,
+        grid=(CH // BLOCK,),
+        in_specs=CONTROL + [STEPS, STEPS],
+        out_specs=PLANES,
+        out_shape=jax.ShapeDtypeStruct((XB, CH, YB), f32),
+        compiler_params=params(57),
+        cost_estimate=pl.CostEstimate(flops=2 * 2 * 4096 * 256 * 256, bytes_accessed=8 << 20, transcendentals=1 << 16),
+        name="local",
+    )(control, control, colx, coly)
+
+
+def share_kernel(background_a, background_b, weights, share):
     for x in range(XB):
         part = jnp.zeros((8, YB), f32)
         for v in range(4):
             part = part + take_plane((background_a, background_b), x, 8, v) * weights[:, v : v + 1]
         share[x] = part
-    for i in range(2):
-        x = (2 * b + i).astype(f32)
-        mh[i], ml[i] = split(matrix[...] * jnp.exp(rates[0:1, :] * (x * (-1.0 / 128.0))))
-        th[i], tl[i] = split(matrix_t[...] * jnp.exp(steps[:, :LEVELS] * -x))
-
-
-def local(control, colx, coly, rates, background, weights, matrix, matrix_t):
-    return pl.pallas_call(
-        local_kernel,
-        grid=(CH // BLOCK,),
-        in_specs=CONTROL
-        + [
-            STEPS,
-            STEPS,
-            whole((2, CH)),
+
+
+def background_share(background, weights):
+    return pl.pallas_call(
+        share_kernel,
+        grid=(8,),
+        in_specs=[
             pl.BlockSpec((4, 128, 128), lambda b: (0, b, 0)),
             pl.BlockSpec((4, 128, 128), lambda b: (0, b, 1)),
             pl.BlockSpec((8, 4), lambda b: (b, 0)),
-            whole((LEVELS, CH)),
-            whole((CH, LEVELS)),
-            whole((CH, 128)),
         ],
-        out_specs=[
-            PLANES,
-            pl.BlockSpec((XB, 8, YB), lambda b: (0, b, 0)),
-            pl.BlockSpec((2, LEVELS, CH), lambda b: (b, 0, 0)),
-            pl.BlockSpec((2, LEVELS, CH), lambda b: (b, 0, 0)),
-            pl.BlockSpec((2, CH, LEVELS), lambda b: (b, 0, 0)),
-            pl.BlockSpec((2, CH, LEVELS), lambda b: (b, 0, 0)),
+        out_specs=pl.BlockSpec((XB, 8, YB), lambda b: (0, b, 0)),
+        out_shape=jax.ShapeDtypeStruct((XB, LEVELS, YB), f32),
+        compiler_params=params(57),
+        cost_estimate=pl.CostEstimate(flops=1 << 21, bytes_accessed=5 << 20, transcendentals=0),
+        name="share",
+    )(background, background, weights)
+
+
+def levels_kernel(cc, share, coly, rates, matrix, level, scaled, turned_high, turned_low, decay):
+    b = pl.program_id(0)
+
+    @pl.when(b == 0)
+    def _():
+        decay[...] = grow(coly[...], CH, -1.0)
+
+    for i in range(2):
+        x = (2 * b + i).astype(f32)
+        at = slice(i * LEVELS, (i + 1) * LEVELS)
+        part = matrix[...] * jnp.exp(rates[0:1, :] * (x * (-1.0 / 128.0)))
+        scaled[at, :] = part
+        mh, ml = split(part)
+        high, low = split(decay[...] * cc[i])
+        level[at, :] = (mm(mh, high) + (mm(ml, high) + mm(mh, low))) + share[i]
+    turned = jnp.concatenate([scaled[:, :128].T, scaled[:, 128:].T], axis=0)
+    turned_high[...], turned_low[...] = split(turned)
+
+
+def levels_of(cc, share, coly, rates, matrix):
+    two = lambda shape: pl.BlockSpec(shape, lambda b: (b,) + (0,) * (len(shape) - 1))
+    lanes = pl.BlockSpec((CH, 128), lambda b: (0, b))
+    return pl.pallas_call(
+        levels_kernel,
+        grid=(XB // 2,),
+        in_specs=[two((2, CH, YB)), two((2, LEVELS, YB)), whole((CH, 128)), whole((2, CH)), whole((LEVELS, CH))],
+        out_specs=[two((128, YB)), two((128, CH)), lanes, lanes],
+        out_shape=[
+            jax.ShapeDtypeStruct((XB * LEVELS, YB), f32),
+            jax.ShapeDtypeStruct((XB * LEVELS, CH), f32),
+            jax.ShapeDtypeStruct((CH, XB * LEVELS), bf16),
+            jax.ShapeDtypeStruct((CH, XB * LEVELS), bf16),
         ],
-        out_shape=[
-            jax.ShapeDtypeStruct((XB, CH, YB), f32),
-            jax.ShapeDtypeStruct((XB, LEVELS, YB), f32),
-            jax.ShapeDtypeStruct((XB, LEVELS, CH), bf16),
-            jax.ShapeDtypeStruct((XB, LEVELS, CH), bf16),
-            jax.ShapeDtypeStruct((XB, CH, LEVELS), bf16),
-            jax.ShapeDtypeStruct((XB, CH, LEVELS), bf16),
-        ],
+        scratch_shapes=[pltpu.VMEM((CH, YB), f32)],
         compiler_params=params(57),
-        cost_estimate=pl.CostEstimate(flops=2 * 2 * 4096 * 256 * 256, bytes_accessed=15 << 20, transcendentals=1 << 20),
-        name="local",
-    )(control, control, colx, coly, rates, background, background, weights, matrix, matrix_t, colx)
+        cost_estimate=pl.CostEstimate(flops=2 * 3 * 1024 * 256 * 256, bytes_accessed=8 << 20, transcendentals=1 << 18),
+        name="levels",
+    )(cc, share, coly, rates, matrix)
 
 
 def carry_kernel(reverse, sums, weights, down, requests, out):
@@ -310,61 +337,47 @@
     )(sums, weights, down, requests)
 
 
+def stack_rows(*parts):
+    return jnp.concatenate(parts, axis=0)
+
+
+def stack_lanes(*parts):
+    return jnp.concatenate(parts, axis=1)
+
+
 def observe_kernel(
-    cc_hbm, share_hbm, mh_hbm, ml_hbm, th, tl, entered, coly, level_weights,
-    running_hbm, msg, lh, ll, forced, cc, share, mh, ml, running_out, sems, out_sems,
+    level, scaled, turned_high, turned_low, entered, coly, rates, level_weights,
+    forced_out, msg, left, both, spread, marks,
 ):
-    def arrivals(x):
-        return [
-            pltpu.make_async_copy(source.at[x], target.at[x], sems.at[x, i])
-            for i, (source, target) in enumerate(
-                ((cc_hbm, cc), (share_hbm, share), (mh_hbm, mh), (ml_hbm, ml))
-            )
-        ]
-
+    decay_y = grow(coly[...], CH, -1.0)
+    pick = lambda row: entered[pl.ds(row, PEERS, stride=ROWS), :]
+    high, low = split(stack_rows(stack_lanes(pick(0), pick(1)), stack_lanes(pick(2), pick(3))))
+    sums = upper()
+    eh, el = split(decay_y * (mm(high, sums) + mm(low, sums)))
+    dh, dl = split(decay_y)
+    requests = pick(4).T
     for x in range(XB):
-        for copy in arrivals(x):
-            copy.start()
-
-    decay_y = grow(coly[...], CH, -1.0)
-    entering = jnp.concatenate(
-        [
-            jnp.concatenate(
-                [entered[pl.ds(2 * c + h, PEERS, stride=ROWS), :] for h in range(2)], axis=1
-            )
-            for c in range(2)
-        ],
-        axis=0,
-    )
-    tail = entered[pl.ds(4, PEERS, stride=ROWS), :]
-    high, low = split(entering)
-    sums = upper()
-    entering = mm(high, sums) + mm(low, sums)
-
-    for x in range(XB):
-        for copy in arrivals(x):
-            copy.wait()
-        col = jnp.concatenate([tail[:, x : x + 1], tail[:, 16 + x : 17 + x]], axis=0)
-        smooth = decay_y * ((cc[x] + entering) + col)
-        high, low = split(smooth)
-        level = (mm(mh[x], high) + (mm(ml[x], high) + mm(mh[x], low))) + share[x]
         at = slice(x * LEVELS, (x + 1) * LEVELS)
-        lh[at, :], ll[at, :] = split(level)
-
-    requests = tail.T
+        part = scaled[at, :]
+        high, low = split(part)
+        left[at, 0:256], left[at, 256:512], left[at, 512:768] = high, low, high
+        col = stack_lanes(requests[x : x + 1, :], requests[16 + x : 17 + x, :])
+        high, low = split(part * col)
+        left[at, 768:1024], left[at, 1024:1280], left[at, 1280:1536] = high, low, high
+    total = level[...] + mm(left[...], stack_rows(eh, eh, el, dh, dh, dl))
+    both[:, 0:256], both[:, 256:512] = split(total)
+
     weights = level_weights[...]
     departures = []
     for r in range(0, CAP, 2):
         first, second = REQ + 3 * r, REQ + 3 * r + 3
-        row = lambda i: jnp.concatenate(
-            [requests[first + i : first + i + 1, :], requests[second + i : second + i + 1, :]], axis=1
-        )
+        row = lambda i: stack_lanes(requests[first + i : first + i + 1, :], requests[second + i : second + i + 1, :])
         where = row(0).astype(jnp.int32) - 1
         valid = where >= 0
         at_x, at_y = where // YB, where % YB
         at_x = jnp.where(valid, at_x, -1)
         chosen = jnp.where(iota((YB, 256), 0) == at_y, 1.0, 0.0).astype(bf16)
-        picked = mm(lh[...], chosen) + mm(ll[...], chosen)
+        picked = mm(both[...], stack_rows(chosen, chosen))
         levels = jnp.zeros((LEVELS, 256), f32)
         for x in range(XB):
             levels = jnp.where(at_x == x, picked[x * LEVELS : (x + 1) * LEVELS, :], levels)
@@ -375,89 +388,115 @@
         adjoint = scale * (weights * sigmoid(levels))
         high = adjoint.astype(bf16).astype(f32)
         low = adjoint - high
-        spread_high = jnp.concatenate([jnp.where(at_x == x, high, 0.0).astype(bf16) for x in range(XB)], axis=0)
-        spread_low = jnp.concatenate([jnp.where(at_x == x, low, 0.0).astype(bf16) for x in range(XB)], axis=0)
-        part = mm_nt(spread_high, chosen) + mm_nt(spread_low, chosen)
-        if r == 0:
-            forced[...] = part
-        else:
-            forced[...] = forced[...] + part
+        lanes = 256 * r
+        for x in range(XB):
+            at = slice(x * LEVELS, (x + 1) * LEVELS)
+            spread[at, lanes : lanes + 256] = jnp.where(at_x == x, high, 0.0).astype(bf16)
+            spread[at, lanes + 256 : lanes + 512] = jnp.where(at_x == x, low, 0.0).astype(bf16)
+        marks[:, lanes : lanes + 256] = chosen
+        marks[:, lanes + 256 : lanes + 512] = chosen
         departures += [miss[:, :128], miss[:, 128:]]
-
-    def leaving(x):
-        return pltpu.make_async_copy(running_out.at[x], running_hbm.at[x], out_sems.at[x])
-
-    running = jnp.zeros((CH, YB), f32)
-    lanes = iota((PEERS, 128), 1)
-    message = pltpu.roll(
-        jnp.concatenate(departures + [jnp.zeros((120, 128), f32)], axis=0).T, REQ, 1
-    )
-    for x in range(XB - 1, -1, -1):
-        high, low = split(forced[x * LEVELS : (x + 1) * LEVELS, :])
-        back = mm(th[x], high) + (mm(tl[x], high) + mm(th[x], low))
-        running = running + back * decay_y
-        running_out[x] = running
-        leaving(x).start()
-        total = jnp.sum(running, axis=1, keepdims=True)
-        message = jnp.where(lanes == x, total[:128], message)
-        message = jnp.where(lanes == 16 + x, total[128:], message)
+    forced = mm_nt(spread[...], marks[...])
+    forced_out[...] = forced
+
+    gh, gl = split(forced)
+    th, tl = turned_high[...], turned_low[...]
+    along_x = mm(stack_lanes(th, tl, th), stack_rows(gh, gh, gl)) * decay_y
     for c in range(2):
         for h in range(2):
-            msg[pl.ds(2 * c + h, PEERS, stride=ROWS), :] = running[128 * c : 128 * c + 128, 128 * h : 128 * h + 128]
-    msg[pl.ds(4, PEERS, stride=ROWS), :] = message
-    for x in range(XB):
-        leaving(x).wait()
-
-
-def observations(cc, share, mh, ml, th, tl, entered, coly, level_weights):
+            msg[pl.ds(2 * c + h, PEERS, stride=ROWS), :] = along_x[128 * c : 128 * c + 128, 128 * h : 128 * h + 128]
+    down = jnp.exp(rates[1:2, :] * (iota((YB, CH), 0).astype(f32) * (-1.0 / 4096.0)))
+    dh, dl = split(down)
+    weighed = mm(stack_lanes(gh, gl, gh), stack_rows(dh, dh, dl))
+    running = jnp.zeros((1, CH), f32)
+    rows = [None] * XB
+    for x in range(XB - 1, -1, -1):
+        at = slice(x * LEVELS, (x + 1) * LEVELS)
+        running = running + jnp.sum(weighed[at, :] * scaled[at, :], axis=0, keepdims=True)
+        rows[x] = running
+    turned = [row[:, :128] for row in rows] + [row[:, 128:] for row in rows] + departures
+    turned.append(jnp.zeros((128 - len(turned), 128), f32))
+    msg[pl.ds(4, PEERS, stride=ROWS), :] = stack_rows(*turned).T
+
+
+def observations(level, scaled, turned_high, turned_low, entered, coly, rates, level_weights):
     return pl.pallas_call(
         observe_kernel,
-        in_specs=[ANY] * 4 + [VMEM] * 5,
-        out_specs=[ANY, VMEM],
+        in_specs=[VMEM] * 8,
+        out_specs=[VMEM, VMEM],
         out_shape=[
-            jax.ShapeDtypeStruct((XB, CH, YB), f32),
+            jax.ShapeDtypeStruct((XB * LEVELS, YB), f32),
             jax.ShapeDtypeStruct((PEERS * ROWS, 128), f32),
         ],
         scratch_shapes=[
-            pltpu.VMEM((XB * LEVELS, YB), bf16),
-            pltpu.VMEM((XB * LEVELS, YB), bf16),
-            pltpu.VMEM((XB * LEVELS, YB), f32),
-            pltpu.VMEM((XB, CH, YB), f32),
-            pltpu.VMEM((XB, LEVELS, YB), f32),
-            pltpu.VMEM((XB, LEVELS, CH), bf16),
-            pltpu.VMEM((XB, LEVELS, CH), bf16),
-            pltpu.VMEM((XB, CH, YB), f32),
-            pltpu.SemaphoreType.DMA((XB, 4)),
-            pltpu.SemaphoreType.DMA((XB,)),
+            pltpu.VMEM((XB * LEVELS, 6 * 256), bf16),
+            pltpu.VMEM((XB * LEVELS, 2 * YB), bf16),
+            pltpu.VMEM((XB * LEVELS, 2 * PEERS * CAP), bf16),
+            pltpu.VMEM((YB, 2 * PEERS * CAP), bf16),
         ],
+        compiler_params=params(40),
+        name="observations",
+    )(level, scaled, turned_high, turned_low, entered, coly, rates, level_weights)
+
+
+def planes_back_kernel(forced, turned_high, turned_low, colx, coly, out, running, decay, scale, shrink):
+    b = pl.program_id(0)
+
+    @pl.when(b == 0)
+    def _():
+        running[...] = jnp.zeros((CH, YB), f32)
+        decay[...] = grow(coly[...], CH, -1.0)
+        scale[...] = grow(coly[...], CH) * wide(jnp.exp(colx[...] * float(XB - 1)))
+        shrink[...] = wide(jnp.exp(-colx[...]))
+
+    sums = lower()
+    gh, gl = split(forced[...])
+    none = jnp.zeros((LEVELS, YB), bf16)
+    for i in (1, 0):
+        half = slice(i * LEVELS, (i + 1) * LEVELS)
+        fill = lambda part: stack_rows(none, part[half]) if i else stack_rows(part[half], none)
+        high, low = fill(gh), fill(gl)
+        back = mm(turned_high[...], high) + (mm(turned_low[...], high) + mm(turned_high[...], low))
+        total = running[...] + back * decay[...]
+        running[...] = total
+        high, low = split(total)
+        out[i] = scale[...] * (mm(high, sums) + mm(low, sums))
+        scale[...] = scale[...] * shrink[...]
+
+
+def planes_back(forced, turned_high, turned_low, colx, coly):
+    last = XB // 2 - 1
+    lanes = pl.BlockSpec((CH, 128), lambda b: (0, last - b))
+    field = pltpu.VMEM((CH, YB), f32)
+    return pl.pallas_call(
+        planes_back_kernel,
+        grid=(XB // 2,),
+        in_specs=[pl.BlockSpec((128, YB), lambda b: (last - b, 0)), lanes, lanes, whole((CH, 128)), whole((CH, 128))],
+        out_specs=pl.BlockSpec((2, CH, YB), lambda b: (last - b, 0, 0)),
+        out_shape=jax.ShapeDtypeStruct((XB, CH, YB), f32),
+        scratch_shapes=[field, field, field, field],
         compiler_params=params(57),
-        name="observations",
-    )(cc, share, mh, ml, th, tl, entered, coly, level_weights)
-
-
-def local_back_kernel(control_a, control_b, running, colx, coly, out):
-    high, low = split(running[...].reshape(XB * BLOCK, YB))
-    sums = lower()
-    summed = mm(high, sums) + mm(low, sums)
-    factor = wide(jnp.exp(colx[...]))
-    scale = grow(coly[...], BLOCK)
+        cost_estimate=pl.CostEstimate(flops=2 * 4 * 4096 * 256 * 256, bytes_accessed=8 << 20, transcendentals=1 << 16),
+        name="planes_back",
+    )(forced, turned_high, turned_low, colx, coly)
+
+
+def join_kernel(control_a, control_b, planes, out):
     for x in range(XB):
-        plane = take_plane((control_a, control_b), x, BLOCK)
-        out[x] = plane + scale * summed[x * BLOCK : (x + 1) * BLOCK, :]
-        scale = scale * factor
-
-
-def local_back(control, running, colx, coly):
-    return pl.pallas_call(
-        local_back_kernel,
+        out[x] = planes[x] + take_plane((control_a, control_b), x, BLOCK)
+
+
+def join(control, planes):
+    return pl.pallas_call(
+        join_kernel,
         grid=(CH // BLOCK,),
-        in_specs=CONTROL + [PLANES, STEPS, STEPS],
+        in_specs=CONTROL + [PLANES],
         out_specs=PLANES,
         out_shape=jax.ShapeDtypeStruct((XB, CH, YB), f32),
         compiler_params=params(57),
-        cost_estimate=pl.CostEstimate(flops=2 * 2 * 4096 * 256 * 256, bytes_accessed=12 << 20, transcendentals=1 << 20),
-        name="local_back",
-    )(control, control, running, colx, coly)
+        cost_estimate=pl.CostEstimate(flops=1 << 20, bytes_accessed=12 << 20, transcendentals=0),
+        name="join",
+    )(control, control, planes)
 
 
 def final_kernel(partial, entered, colx, coly, out, whole_a, whole_b, sems):
@@ -570,17 +609,19 @@
     gain = jnp.sqrt(-jnp.expm1(-2.0 * step_x)) * jnp.sqrt(-jnp.expm1(-2.0 * step_y))
     mixed = flash_weights[:, :, None] * vert_factor * gain[:, None, :]
     matrix = mixed.transpose(1, 0, 2).reshape(LEVELS, CH)
-    matrix_t = mixed.transpose(0, 2, 1).reshape(CH, LEVELS)
-    cc, share, mh, ml, th, tl = local(
-        flat, colx, coly, rates, background.reshape(4, LEVELS * XB, YB), flash_weights.T, matrix, matrix_t
-    )
+    cc = local(flat, colx, coly)
+    asked, cc = lax.optimization_barrier((asked, cc))
     entered = everywhere(carry(asked, ahead, down, requests))
-    running, msg_back = observations(
-        cc, share, mh, ml, th, tl, entered, coly, level_weights.reshape(LEVELS, 1)
+    share = background_share(background.reshape(4, LEVELS * XB, YB), flash_weights.T)
+    level, scaled, turned_high, turned_low = levels_of(cc, share, coly, rates, matrix)
+    forced, msg_back = observations(
+        level, scaled, turned_high, turned_low, entered, coly, rates, level_weights.reshape(LEVELS, 1)
     )
     returned = everywhere(msg_back)
-    partial = local_back(flat, running, colx, coly)
+    planes = planes_back(forced, turned_high, turned_low, colx, coly)
+    returned, planes = lax.optimization_barrier((returned, planes))
     entered_back = everywhere(carry(returned, behind, down))
+    partial = join(flat, planes)
     departure = departures(rank, returned)
     grad = final(partial, entered_back, colx, coly)
     return (grad.reshape(shape), departure.reshape(OBS))

time: 113 us -> 122 us (1.080)
  blocking collectives: 21.2 us -> 0 us
  starting transfers between devices: 20.9 us -> 38.7 us
  Pallas kernels: 54.2 us -> 67.2 us
  waiting for transfers between devices: 9.19 us -> 4.58 us
  local copies, waits for them, and re-layouts: 4.58 us -> 8.05 us
    all_to_all x1 -> x0, blocking collectives: 21.2 us -> none  [everywhere(): lax.all_to_all(shaped, ('gx', 'gy'), split_axis=0, concat_axis=0, tiled=T...]
    all_to_all x3 -> x4, starting transfers between devices: 20.9 us -> 38.7 us  [everywhere(): lax.all_to_all(shaped, ('gx', 'gy'), split_axis=0, concat_axis=0, tiled=T...]
    pallas_call x2 -> x5, Pallas kernels: 23.9 us -> 40.2 us  [the longest x1 10.2 us: planes_back(): pl.pallas_call(planes_back_kernel, grid=(XB // 2,), in_specs=[pl.BlockSpe...]
    unnamed x23 -> x35, local copies, waits for them, and re-layouts: 2.2 us -> 7.02 us
    all_to_all x3 -> x4, waiting for transfers between devices: 9.19 us -> 4.58 us  [everywhere(): lax.all_to_all(shaped, ('gx', 'gy'), split_axis=0, concat_axis=0, tiled=T...]
    pallas_call x1, Pallas kernels: 10.8 us -> 7.56 us  [local(): pl.pallas_call(local_kernel, grid=(CH // BLOCK,), in_specs=CONTROL + [STE...]
  transfers between devices with their start and end apart: 3 -> 4, of which waited for: 2 -> 3; matrix products, arithmetic and copies ran while one was open for 3% -> 2% of each run, Pallas kernels for 20% -> 35%
where the time goes in v2:
time: 122 us; the launch traced here: 120 us
  Pallas kernels  67.2 us (55%)
  starting transfers between devices  38.7 us (32%)
  local copies, waits for them, and re-layouts  8.05 us (7%)
  waiting for transfers between devices  4.58 us (4%)
  between operations  1.47 us (1%)
    all_to_all x4, starting transfers between devices, everywhere(): lax.all_to_all(shaped, ('gx', 'gy'), split_axis=0, concat_axis=0, tiled=T...  38.7 us
    pallas_call x1, Pallas kernels, planes_back(): pl.pallas_call(planes_back_kernel, grid=(XB // 2,), in_specs=[pl.BlockSpe...  10.2 us
    pallas_call x1, Pallas kernels, observations(): pl.pallas_call(observe_kernel, in_specs=[VMEM] * 8, out_specs=[VMEM, VMEM...  8.05 us
    pallas_call x1, Pallas kernels, join(): pl.pallas_call(join_kernel, grid=(CH // BLOCK,), in_specs=CONTROL + [PLAN...  8.03 us
    pallas_call x1, Pallas kernels, final(): pl.pallas_call(final_kernel, grid=(CH // BLOCK,), in_specs=[PLANES, whole...  7.77 us
    pallas_call x1, Pallas kernels, local(): pl.pallas_call(local_kernel, grid=(CH // BLOCK,), in_specs=CONTROL + [STE...  7.56 us
    pallas_call x1, Pallas kernels, levels_of(): pl.pallas_call(levels_kernel, grid=(XB // 2,), in_specs=[two((2, CH, YB))...  7.28 us
    unnamed x35, local copies, waits for them, and re-layouts  7.02 us
  transfers between devices with their start and end apart: 4, of which 3 were waited for; matrix products, arithmetic and copies ran while one was open for 2% of the time, Pallas kernels for 35%

profile of v2, /device:TPU:1, one launch (start us, length us, event | category | flops | bytes accessed | tf_op | source)
XLA Modules:
  0.0 120.2 jit_solution(15148970544560854493)
XLA Ops:
  0.6 6.6 %edges.1 = (f32[640,128]{1,0:T(8,128)}, f32[256,128]{1,0:T(8,128)}, f32[256,128]{1,0:T(8,128)}) custom-call(f32[4096,256]{1,0:T(8,128)} %bitcast.41, f32[4096,256]{1,0:T(8,128)} %bitcast.42, f32[2,4,64]{2,1,0:T(4,128)} %rates.1), custom_call_target="tpu_custom_call" | custom-call | tf_op jit(solution)/shard_map/edges/pallas_call | solution.py:129
  7.2 11.5 %all-to-all-start = ((f32[640,1,128]{2,1,0:T(1,128)}), f32[640,1,128]{2,1,0:T(1,128)S(1)}, u32[]{:S(2)}, u32[]{:S(2)}) async-start(f32[640,1,128]{2,1,0:T(1,128)} %bitcast.51), calls=%async_computation | async-start | bytes 655360 | tf_op jit(solution)/shard_map/all_to_all | solution.py:579
  19.5 7.6 %local.1.cc = f32[16,256,256]{2,1,0:T(8,128)} custom-call(f32[4096,256]{1,0:T(8,128)} %bitcast.43, f32[4096,256]{1,0:T(8,128)} %bitcast.44, f32[256,128]{1,0:T(8,128)} %get-tuple-element.21.colx, f32[256,128]{1,0:T(8,128)} %get-tuple-element.22.coly), custom_call_target="tpu_custom_call" | custom-call | flops 1073741824 | bytes 8388608 | tf_op jit(solution)/shard_map/local/pallas_call | solution.py:221
  27.2 1.9 %prepare.1 = (f32[128,128]{1,0:T(8,128)S(1)}, f32[128,512]{1,0:T(8,128)S(1)}, f32[128,512]{1,0:T(8,128)S(1)}, f32[128,512]{1,0:T(8,128)S(1)}, f32[8,128]{1,0:T(8,128)S(1)}) custom-call(s32[3]{0:T(128)S(1)} %pad_add_fusion.place, s32[1]{0:T(128)S(6)} %copy.23.count, f32[2,256]{1,0:T(2,128)S(1)} %reshape.93.rates, s32[1,512]{1,0:T(1,128)S(1)} %bitcast.37, ...), custom_call_target="tpu_custom_call" | custom-call | flops 1073741824 | bytes 1048576 | tf_op jit(solution)/shard_map/prepare/pallas_call | solution.py:187
  29.1 1.0 all-to-all-done
  30.1 1.2 carry.1
  31.2 8.8 %all-to-all-start.1 = ((f32[640,1,128]{2,1,0:T(1,128)}), f32[640,1,128]{2,1,0:T(1,128)S(1)}, u32[]{:S(2)}, u32[]{:S(2)}) async-start(f32[640,1,128]{2,1,0:T(1,128)} %bitcast.16), calls=%async_computation.1 | async-start | bytes 655360 | tf_op jit(solution)/shard_map/all_to_all | solution.py:579
  41.8 6.6 %share.1 = f32[16,64,256]{2,1,0:T(8,128)} custom-call(f32[4,1024,256]{2,1,0:T(8,128)} %bitcast.47, f32[4,1024,256]{2,1,0:T(8,128)} %bitcast.48, f32[64,4]{1,0:T(8,128)} %bitcast.52), custom_call_target="tpu_custom_call" | custom-call | flops 2097152 | bytes 5242880 | tf_op jit(solution)/shard_map/share/pallas_call | solution.py:242
  48.5 7.3 %levels.1 = (f32[1024,256]{1,0:T(8,128)}, f32[1024,256]{1,0:T(8,128)}, bf16[256,1024]{1,0:T(8,128)(2,1)}, bf16[256,1024]{1,0:T(8,128)(2,1)}) custom-call(f32[16,256,256]{2,1,0:T(8,128)} %local.1.cc, f32[16,64,256]{2,1,0:T(8,128)} %share.1, f32[256,128]{1,0:T(8,128)} %get-tuple-element.22.coly, f32[2,256]{1,0:T(2,128)} %copy-done.5, f32[64,256]{1,0:T(8,128)} %reshape.94.matrix), custom_call_target="tpu_custom_call" | custom-call | flops 402653184 | bytes 8388608 | tf_op jit(solution)/shard_map/levels/pallas_call | solution.py:280
  55.8 1.2 %copy-done.1 = f32[1024,256]{1,0:T(8,128)S(1)} copy-done((f32[1024,256]{1,0:T(8,128)S(1)}, f32[1024,256]{1,0:T(8,128)}, u32[]{:S(2)}) %copy-start.1) | copy-done | bytes 1048600
  57.0 1.2 %copy-done.2 = f32[1024,256]{1,0:T(8,128)S(1)} copy-done((f32[1024,256]{1,0:T(8,128)S(1)}, f32[1024,256]{1,0:T(8,128)}, u32[]{:S(2)}) %copy-start.2) | copy-done | bytes 1048600
  58.2 1.0 copy-done.3
  59.3 1.0 copy-done.4
  60.3 8.1 %observations.1 = (f32[1024,256]{1,0:T(8,128)S(1)}, f32[640,128]{1,0:T(8,128)}) custom-call(f32[1024,256]{1,0:T(8,128)S(1)} %copy-done.1, f32[1024,256]{1,0:T(8,128)S(1)} %copy-done.2, bf16[256,1024]{1,0:T(8,128)(2,1)S(1)} %copy-done.3, bf16[256,1024]{1,0:T(8,128)(2,1)S(1)} %copy-done.4, f32[640,128]{1,0:T(8,128)S(1)} %bitcast.35, f32[256,128]{1,0:T(8,128)S(1)} %copy-done, ...), custom_call_target="tpu_custom_call" | custom-call | tf_op jit(solution)/shard_map/observations/pallas_call | solution.py:423
  68.4 1.0 copy-done.7
  69.4 9.8 %all-to-all-start.2 = ((f32[640,1,128]{2,1,0:T(1,128)}), f32[640,1,128]{2,1,0:T(1,128)S(1)}, u32[]{:S(2)}, u32[]{:S(2)}) async-start(f32[640,1,128]{2,1,0:T(1,128)} %bitcast.20), calls=%async_computation.2 | async-start | bytes 655360 | tf_op jit(solution)/shard_map/all_to_all | solution.py:579
  79.1 10.2 %planes_back.1.planes = f32[16,256,256]{2,1,0:T(8,128)} custom-call(f32[1024,256]{1,0:T(8,128)} %copy-done.7, bf16[256,1024]{1,0:T(8,128)(2,1)} %get-tuple-element.26.turned_high, bf16[256,1024]{1,0:T(8,128)(2,1)} %get-tuple-element.27.turned_low, f32[256,128]{1,0:T(8,128)} %get-tuple-element.21.colx, f32[256,128]{1,0:T(8,128)} %get-tuple-element.22.coly), custom_call_target="tpu_custom_call" | custom-call | flops 2147483648 | bytes 8388608 | tf_op jit(solution)/shard_map/planes_back/pallas_call | solution.py:471
  89.3 1.1 all-to-all-done.2
  90.5 1.2 carry_back.1
  91.7 8.6 %all-to-all-start.3 = ((f32[640,1,128]{2,1,0:T(1,128)}), f32[640,1,128]{2,1,0:T(1,128)S(1)}, u32[]{:S(2)}, u32[]{:S(2)}) async-start(f32[640,1,128]{2,1,0:T(1,128)} %bitcast.23), calls=%async_computation.3 | async-start | bytes 655360 | tf_op jit(solution)/shard_map/all_to_all | solution.py:579
  100.3 8.0 %join.1.partial = f32[16,256,256]{2,1,0:T(8,128)} custom-call(f32[4096,256]{1,0:T(8,128)} %bitcast.45, f32[4096,256]{1,0:T(8,128)} %bitcast.46, f32[16,256,256]{2,1,0:T(8,128)} %planes_back.1.planes), custom_call_target="tpu_custom_call" | custom-call | flops 1048576 | bytes 12582912 | tf_op jit(solution)/shard_map/join/pallas_call | solution.py:490
  108.3 0.9 departures.1
  109.2 2.4 %all-to-all-done.3 = f32[640,1,128]{2,1,0:T(1,128)S(1)} async-done(((f32[640,1,128]{2,1,0:T(1,128)}), f32[640,1,128]{2,1,0:T(1,128)S(1)}, u32[]{:S(2)}, u32[]{:S(2)}) %all-to-all-start.3) | async-done | bytes 327712 | tf_op jit(solution)/shard_map/all_to_all | solution.py:579
  112.4 7.8 %final.1 = f32[4096,256]{1,0:T(8,128)} custom-call(f32[16,256,256]{2,1,0:T(8,128)} %join.1.partial, f32[640,128]{1,0:T(8,128)} %bitcast.50, f32[256,128]{1,0:T(8,128)} %get-tuple-element.21.colx, f32[256,128]{1,0:T(8,128)} %get-tuple-element.22.coly), custom_call_target="tpu_custom_call" | custom-call | tf_op jit(solution)/shard_map/final/pallas_call | solution.py:540
  (38 shorter events, 2.7 us)
Async XLA Ops:
  0.6 18.1 %copy-start.14 = (f32[2,4,64]{2,1,0:T(4,128)S(1)}, f32[2,4,64]{2,1,0:T(4,128)}, u32[]{:S(2)}) copy-start(f32[2,4,64]{2,1,0:T(4,128)} %rates.1) | copy-start | bytes 6148
  7.2 22.9 %all-to-all-start = ((f32[640,1,128]{2,1,0:T(1,128)}), f32[640,1,128]{2,1,0:T(1,128)S(1)}, u32[]{:S(2)}, u32[]{:S(2)}) async-start(f32[640,1,128]{2,1,0:T(1,128)} %bitcast.51), calls=%async_computation | async-start | bytes 655360 | tf_op jit(solution)/shard_map/all_to_all | solution.py:579
  18.8 8.4 %copy-start.5 = (f32[2,256]{1,0:T(2,128)}, f32[2,256]{1,0:T(2,128)S(1)}, u32[]{:S(2)}) copy-start(f32[2,256]{1,0:T(2,128)S(1)} %reshape.93.rates) | copy-start | bytes 6148
  19.4 7.7 %copy-start.8 = (s32[512,1]{0,1:T(1,128)S(1)}, s32[512,1]{0,1:T(1,128)}, u32[]{:S(2)}) copy-start(s32[512,1]{0,1:T(1,128)} %param.17) | copy-start | bytes 6148
  19.5 7.7 %copy-start.9 = (s32[512]{0:T(512)S(1)}, s32[512]{0:T(512)}, u32[]{:S(2)}) copy-start(s32[512]{0:T(512)} %param.18) | copy-start | bytes 6148
  19.5 7.7 %copy-start.10 = (f32[512]{0:T(512)S(1)}, f32[512]{0:T(512)}, u32[]{:S(2)}) copy-start(f32[512]{0:T(512)} %param.20) | copy-start | bytes 6148
  19.5 7.7 %copy-start.11 = (f32[512]{0:T(512)S(1)}, f32[512]{0:T(512)}, u32[]{:S(2)}) copy-start(f32[512]{0:T(512)} %param.21) | copy-start | bytes 6148
  27.1 13.0 %copy-start.15 = (f32[4,64]{1,0:T(4,128)S(1)}, f32[4,64]{1,0:T(4,128)}, u32[]{:S(2)}) copy-start(f32[4,64]{1,0:T(4,128)} %param.15) | copy-start | bytes 3076
  27.1 13.7 %copy-start.13 = (f32[4,64,64]{2,1,0:T(8,128)S(1)}, f32[4,64,64]{2,1,0:T(8,128)}, u32[]{:S(2)}) copy-start(f32[4,64,64]{2,1,0:T(8,128)} %param.13) | copy-start | bytes 196612
  27.1 14.7 %copy-start.16 = (f32[64]{0:T(128)S(1)}, f32[64]{0:T(128)}, u32[]{:S(2)}) copy-start(f32[64]{0:T(128)} %param.16) | copy-start | bytes 772
  31.2 24.5 %all-to-all-start.1 = ((f32[640,1,128]{2,1,0:T(1,128)}), f32[640,1,128]{2,1,0:T(1,128)S(1)}, u32[]{:S(2)}, u32[]{:S(2)}) async-start(f32[640,1,128]{2,1,0:T(1,128)} %bitcast.16), calls=%async_computation.1 | async-start | bytes 655360 | tf_op jit(solution)/shard_map/all_to_all | solution.py:579
  48.5 7.3 %copy-start = (f32[256,128]{1,0:T(8,128)S(1)}, f32[256,128]{1,0:T(8,128)}, u32[]{:S(2)}) copy-start(f32[256,128]{1,0:T(8,128)} %get-tuple-element.22.coly) | copy-start | bytes 393220
  48.5 7.3 %copy-start.6 = (f32[2,256]{1,0:T(2,128)S(1)}, f32[2,256]{1,0:T(2,128)}, u32[]{:S(2)}) copy-start(f32[2,256]{1,0:T(2,128)} %copy-done.5) | copy-start | bytes 6148
  55.8 1.2 %copy-start.1 = (f32[1024,256]{1,0:T(8,128)S(1)}, f32[1024,256]{1,0:T(8,128)}, u32[]{:S(2)}) copy-start(f32[1024,256]{1,0:T(8,128)} %get-tuple-element.24.level) | copy-start | bytes 3145732
  57.0 1.2 %copy-start.2 = (f32[1024,256]{1,0:T(8,128)S(1)}, f32[1024,256]{1,0:T(8,128)}, u32[]{:S(2)}) copy-start(f32[1024,256]{1,0:T(8,128)} %get-tuple-element.25.scaled) | copy-start | bytes 3145732
  58.2 1.0 copy-start.3
  59.3 1.0 copy-start.4
  68.4 1.0 copy-start.7
  69.4 21.1 %all-to-all-start.2 = ((f32[640,1,128]{2,1,0:T(1,128)}), f32[640,1,128]{2,1,0:T(1,128)S(1)}, u32[]{:S(2)}, u32[]{:S(2)}) async-start(f32[640,1,128]{2,1,0:T(1,128)} %bitcast.20), calls=%async_computation.2 | async-start | bytes 655360 | tf_op jit(solution)/shard_map/all_to_all | solution.py:579
  91.7 20.0 %all-to-all-start.3 = ((f32[640,1,128]{2,1,0:T(1,128)}), f32[640,1,128]{2,1,0:T(1,128)S(1)}, u32[]{:S(2)}, u32[]{:S(2)}) async-start(f32[640,1,128]{2,1,0:T(1,128)} %bitcast.23), calls=%async_computation.3 | async-start | bytes 655360 | tf_op jit(solution)/shard_map/all_to_all | solution.py:579
  111.7 0.7 copy-start.12

commit v3 on v2

--- a/solution.py
+++ b/solution.py
@@ -92,7 +92,7 @@
     return jnp.exp(wide(step_y) * (iota((rows, YB), 1).astype(f32) * sign))
 
 
-def edges_kernel(control_a, control_b, rates, msg, colx, coly, line, tail):
+def edges_kernel(control_a, control_b, rates, msg, colx, coly, planes, line, tail):
     b = pl.program_id(0)
 
     @pl.when(b == 0)
@@ -111,7 +111,9 @@
     place = iota((BLOCK, 128), 1) - 16 * (b // 4)
     sums = jnp.zeros((BLOCK, 128), f32)
     for x in range(XB):
-        running = running + take_plane((control_a, control_b), x, BLOCK) * scale
+        plane = take_plane((control_a, control_b), x, BLOCK)
+        planes[x] = plane
+        running = running + plane * scale
         scale = scale * factor
         sums = jnp.where(place == x, jnp.sum(running, axis=1, keepdims=True), sums)
     start = (b % 4) * (BLOCK * ROWS) + 2 * (b // 4)
@@ -130,11 +132,12 @@
         edges_kernel,
         grid=(CH // BLOCK,),
         in_specs=CONTROL + [whole((2, 4, LEVELS))],
-        out_specs=[whole((PEERS * ROWS, 128)), whole((CH, 128)), whole((CH, 128))],
+        out_specs=[whole((PEERS * ROWS, 128)), whole((CH, 128)), whole((CH, 128)), PLANES],
         out_shape=[
             jax.ShapeDtypeStruct((PEERS * ROWS, 128), f32),
             jax.ShapeDtypeStruct((CH, 128), f32),
             jax.ShapeDtypeStruct((CH, 128), f32),
+            jax.ShapeDtypeStruct((XB, CH, YB), f32),
         ],
         scratch_shapes=[pltpu.VMEM((8, 128), f32), pltpu.VMEM((PEERS, 128), f32)],
         compiler_params=params(57),
@@ -201,14 +204,14 @@
     )(place, count, rates, owner, cell, flash, sigma)
 
 
-def local_kernel(control_a, control_b, colx, coly, cc):
+def local_kernel(planes, colx, coly, cc):
     factor = wide(jnp.exp(colx[...]))
     scale = grow(coly[...], BLOCK)
     running = jnp.zeros((BLOCK, YB), f32)
     sums = upper()
     highs, lows = [], []
     for x in range(XB):
-        running = running + take_plane((control_a, control_b), x, BLOCK) * scale
+        running = running + planes[x] * scale
         scale = scale * factor
         high, low = split(running)
         highs.append(high)
@@ -217,25 +220,27 @@
     cc[...] = summed.reshape(XB, BLOCK, YB)
 
 
-def local(control, colx, coly):
+def local(planes, colx, coly):
     return pl.pallas_call(
         local_kernel,
         grid=(CH // BLOCK,),
-        in_specs=CONTROL + [STEPS, STEPS],
+        in_specs=[PLANES, STEPS, STEPS],
         out_specs=PLANES,
         out_shape=jax.ShapeDtypeStruct((XB, CH, YB), f32),
         compiler_params=params(57),
         cost_estimate=pl.CostEstimate(flops=2 * 2 * 4096 * 256 * 256, bytes_accessed=8 << 20, transcendentals=1 << 16),
         name="local",
-    )(control, control, colx, coly)
-
-
-def share_kernel(background_a, background_b, weights, share):
+    )(planes, colx, coly)
+
+
+def share_kernel(background, weights, share, half_a, half_b):
+    total = background[0] * weights[:, 0:1]
+    for v in range(1, 4):
+        total = total + background[v] * weights[:, v : v + 1]
+    half_a[...] = total[:, :128]
+    half_b[...] = total[:, 128:]
     for x in range(XB):
-        part = jnp.zeros((8, YB), f32)
-        for v in range(4):
-            part = part + take_plane((background_a, background_b), x, 8, v) * weights[:, v : v + 1]
-        share[x] = part
+        share[x] = take_plane((half_a, half_b), x, 8)
 
 
 def background_share(background, weights):
@@ -243,16 +248,16 @@
         share_kernel,
         grid=(8,),
         in_specs=[
-            pl.BlockSpec((4, 128, 128), lambda b: (0, b, 0)),
-            pl.BlockSpec((4, 128, 128), lambda b: (0, b, 1)),
-            pl.BlockSpec((8, 4), lambda b: (b, 0)),
+            pl.BlockSpec((4, 128, YB), lambda b: (0, b, 0)),
+            pl.BlockSpec((128, 4), lambda b: (b, 0)),
         ],
         out_specs=pl.BlockSpec((XB, 8, YB), lambda b: (0, b, 0)),
         out_shape=jax.ShapeDtypeStruct((XB, LEVELS, YB), f32),
+        scratch_shapes=[pltpu.VMEM((128, 128), f32), pltpu.VMEM((128, 128), f32)],
         compiler_params=params(57),
         cost_estimate=pl.CostEstimate(flops=1 << 21, bytes_accessed=5 << 20, transcendentals=0),
         name="share",
-    )(background, background, weights)
+    )(background, weights)
 
 
 def levels_kernel(cc, share, coly, rates, matrix, level, scaled, turned_high, turned_low, decay):
@@ -269,7 +274,8 @@
         scaled[at, :] = part
         mh, ml = split(part)
         high, low = split(decay[...] * cc[i])
-        level[at, :] = (mm(mh, high) + (mm(ml, high) + mm(mh, low))) + share[i]
+        pair = mm(jnp.concatenate([mh, ml], axis=0), high)
+        level[at, :] = (pair[:LEVELS] + (pair[LEVELS:] + mm(mh, low))) + share[i]
     turned = jnp.concatenate([scaled[:, :128].T, scaled[:, 128:].T], axis=0)
     turned_high[...], turned_low[...] = split(turned)
 
@@ -434,69 +440,70 @@
             pltpu.VMEM((XB * LEVELS, 2 * PEERS * CAP), bf16),
             pltpu.VMEM((YB, 2 * PEERS * CAP), bf16),
         ],
-        compiler_params=params(40),
+        compiler_params=params(57),
         name="observations",
     )(level, scaled, turned_high, turned_low, entered, coly, rates, level_weights)
 
 
-def planes_back_kernel(forced, turned_high, turned_low, colx, coly, out, running, decay, scale, shrink):
+def planes_back_kernel(forced, turned_high, turned_low, coly, out, running, decay):
     b = pl.program_id(0)
 
     @pl.when(b == 0)
     def _():
         running[...] = jnp.zeros((CH, YB), f32)
         decay[...] = grow(coly[...], CH, -1.0)
-        scale[...] = grow(coly[...], CH) * wide(jnp.exp(colx[...] * float(XB - 1)))
-        shrink[...] = wide(jnp.exp(-colx[...]))
-
-    sums = lower()
+
     gh, gl = split(forced[...])
+    th, tl = turned_high[...], turned_low[...]
     none = jnp.zeros((LEVELS, YB), bf16)
     for i in (1, 0):
         half = slice(i * LEVELS, (i + 1) * LEVELS)
         fill = lambda part: stack_rows(none, part[half]) if i else stack_rows(part[half], none)
         high, low = fill(gh), fill(gl)
-        back = mm(turned_high[...], high) + (mm(turned_low[...], high) + mm(turned_high[...], low))
-        total = running[...] + back * decay[...]
-        running[...] = total
-        high, low = split(total)
-        out[i] = scale[...] * (mm(high, sums) + mm(low, sums))
-        scale[...] = scale[...] * shrink[...]
-
-
-def planes_back(forced, turned_high, turned_low, colx, coly):
+        back = mm(stack_lanes(th, tl), stack_rows(high, high)) + mm(th, low)
+        running[...] = running[...] + back * decay[...]
+        out[i] = running[...]
+
+
+def planes_back(forced, turned_high, turned_low, coly):
     last = XB // 2 - 1
     lanes = pl.BlockSpec((CH, 128), lambda b: (0, last - b))
     field = pltpu.VMEM((CH, YB), f32)
     return pl.pallas_call(
         planes_back_kernel,
         grid=(XB // 2,),
-        in_specs=[pl.BlockSpec((128, YB), lambda b: (last - b, 0)), lanes, lanes, whole((CH, 128)), whole((CH, 128))],
+        in_specs=[pl.BlockSpec((128, YB), lambda b: (last - b, 0)), lanes, lanes, whole((CH, 128))],
         out_specs=pl.BlockSpec((2, CH, YB), lambda b: (last - b, 0, 0)),
         out_shape=jax.ShapeDtypeStruct((XB, CH, YB), f32),
-        scratch_shapes=[field, field, field, field],
+        scratch_shapes=[field, field],
         compiler_params=params(57),
         cost_estimate=pl.CostEstimate(flops=2 * 4 * 4096 * 256 * 256, bytes_accessed=8 << 20, transcendentals=1 << 16),
         name="planes_back",
-    )(forced, turned_high, turned_low, colx, coly)
-
-
-def join_kernel(control_a, control_b, planes, out):
+    )(forced, turned_high, turned_low, coly)
+
+
+def join_kernel(control, running, colx, coly, out):
+    high, low = split(running[...].reshape(XB * BLOCK, YB))
+    sums = lower()
+    summed = mm(high, sums) + mm(low, sums)
+    factor = wide(jnp.exp(colx[...]))
+    scale = grow(coly[...], BLOCK)
     for x in range(XB):
-        out[x] = planes[x] + take_plane((control_a, control_b), x, BLOCK)
-
-
-def join(control, planes):
+        out[x] = control[x] + scale * summed[x * BLOCK : (x + 1) * BLOCK, :]
+        scale = scale * factor
+
+
+def join(control, running, colx, coly):
     return pl.pallas_call(
         join_kernel,
         grid=(CH // BLOCK,),
-        in_specs=CONTROL + [PLANES],
+        in_specs=[PLANES, PLANES, STEPS, STEPS],
         out_specs=PLANES,
         out_shape=jax.ShapeDtypeStruct((XB, CH, YB), f32),
         compiler_params=params(57),
-        cost_estimate=pl.CostEstimate(flops=1 << 20, bytes_accessed=12 << 20, transcendentals=0),
+        cost_estimate=pl.CostEstimate(flops=2 * 2 * 4096 * 256 * 256, bytes_accessed=12 << 20, transcendentals=0),
         name="join",
-    )(control, control, planes)
+    )(control, running, colx, coly)
 
 
 def final_kernel(partial, entered, colx, coly, out, whole_a, whole_b, sems):
@@ -595,7 +602,7 @@
 ):
     shape = control.shape
     flat = control.reshape(CH * XB, YB)
-    msg, colx, coly = edges(flat, length_rates)
+    msg, colx, coly, control_planes = edges(flat, length_rates)
     asked = everywhere(msg)
 
     gx, gy = lax.axis_index("gx"), lax.axis_index("gy")
@@ -609,19 +616,19 @@
     gain = jnp.sqrt(-jnp.expm1(-2.0 * step_x)) * jnp.sqrt(-jnp.expm1(-2.0 * step_y))
     mixed = flash_weights[:, :, None] * vert_factor * gain[:, None, :]
     matrix = mixed.transpose(1, 0, 2).reshape(LEVELS, CH)
-    cc = local(flat, colx, coly)
+    cc = local(control_planes, colx, coly)
     asked, cc = lax.optimization_barrier((asked, cc))
     entered = everywhere(carry(asked, ahead, down, requests))
-    share = background_share(background.reshape(4, LEVELS * XB, YB), flash_weights.T)
+    share = background_share(background.reshape(4, LEVELS * XB, YB), jnp.repeat(flash_weights.T, XB, axis=0))
     level, scaled, turned_high, turned_low = levels_of(cc, share, coly, rates, matrix)
     forced, msg_back = observations(
         level, scaled, turned_high, turned_low, entered, coly, rates, level_weights.reshape(LEVELS, 1)
     )
     returned = everywhere(msg_back)
-    planes = planes_back(forced, turned_high, turned_low, colx, coly)
+    planes = planes_back(forced, turned_high, turned_low, coly)
     returned, planes = lax.optimization_barrier((returned, planes))
     entered_back = everywhere(carry(returned, behind, down))
-    partial = join(flat, planes)
+    partial = join(control_planes, planes, colx, coly)
     departure = departures(rank, returned)
     grad = final(partial, entered_back, colx, coly)
     return (grad.reshape(shape), departure.reshape(OBS))

time: 122 us -> 118 us (0.967)
  local copies, waits for them, and re-layouts: 8.05 us -> 4.07 us
  starting transfers between devices: 38.7 us -> 35.8 us
  waiting for transfers between devices: 4.58 us -> 7 us
    unnamed x35 -> x22, local copies, waits for them, and re-layouts: 7.02 us -> 1.48 us
    pallas_call x1, Pallas kernels: 10.2 us -> 7.2 us  [planes_back(): pl.pallas_call(planes_back_kernel, grid=(XB // 2,), in_specs=[pl.BlockSpe...]
    all_to_all x4, starting transfers between devices: 38.7 us -> 35.8 us  [everywhere(): lax.all_to_all(shaped, ('gx', 'gy'), split_axis=0, concat_axis=0, tiled=T...]
    all_to_all x4, waiting for transfers between devices: 4.58 us -> 7 us  [everywhere(): lax.all_to_all(shaped, ('gx', 'gy'), split_axis=0, concat_axis=0, tiled=T...]
    pallas_call x1, Pallas kernels: 8.05 us -> 10 us  [observations(): pl.pallas_call(observe_kernel, in_specs=[VMEM] * 8, out_specs=[VMEM, VMEM...]
    pallas_call x1, Pallas kernels: 6.55 us -> 7.79 us  [edges(): pl.pallas_call(edges_kernel, grid=(CH // BLOCK,), in_specs=CONTROL + [who...]
  transfers between devices with their start and end apart: 4 -> 4, of which waited for: 3 -> 3; matrix products, arithmetic and copies ran while one was open for 2% -> 2% of each run, Pallas kernels for 35% -> 34%
where the time goes in v3:
time: 118 us; the launch traced here: 116 us
  Pallas kernels  67.7 us (57%)
  starting transfers between devices  35.8 us (30%)
  waiting for transfers between devices  7 us (6%)
  local copies, waits for them, and re-layouts  4.07 us (3%)
  between operations  1.45 us (1%)
    all_to_all x4, starting transfers between devices, everywhere(): lax.all_to_all(shaped, ('gx', 'gy'), split_axis=0, concat_axis=0, tiled=T...  35.8 us
    pallas_call x1, Pallas kernels, observations(): pl.pallas_call(observe_kernel, in_specs=[VMEM] * 8, out_specs=[VMEM, VMEM...  10 us
    pallas_call x1, Pallas kernels, join(): pl.pallas_call(join_kernel, grid=(CH // BLOCK,), in_specs=[PLANES, PLANES...  8.51 us
    pallas_call x1, Pallas kernels, edges(): pl.pallas_call(edges_kernel, grid=(CH // BLOCK,), in_specs=CONTROL + [who...  7.79 us
    pallas_call x1, Pallas kernels, final(): pl.pallas_call(final_kernel, grid=(CH // BLOCK,), in_specs=[PLANES, whole...  7.77 us
    pallas_call x1, Pallas kernels, local(): pl.pallas_call(local_kernel, grid=(CH // BLOCK,), in_specs=[PLANES, STEPS...  7.67 us
    pallas_call x1, Pallas kernels, planes_back(): pl.pallas_call(planes_back_kernel, grid=(XB // 2,), in_specs=[pl.BlockSpe...  7.2 us
    pallas_call x1, Pallas kernels, levels_of(): pl.pallas_call(levels_kernel, grid=(XB // 2,), in_specs=[two((2, CH, YB))...  7.11 us
  transfers between devices with their start and end apart: 4, of which 3 were waited for; matrix products, arithmetic and copies ran while one was open for 2% of the time, Pallas kernels for 34%

profile of v3, /device:TPU:1, one launch (start us, length us, event | category | flops | bytes accessed | tf_op | source)
XLA Modules:
  0.0 116.1 jit_solution(14594510864214779592)
XLA Ops:
  0.6 7.8 %edges.1 = (f32[640,128]{1,0:T(8,128)}, f32[256,128]{1,0:T(8,128)}, f32[256,128]{1,0:T(8,128)}, f32[16,256,256]{2,1,0:T(8,128)}) custom-call(f32[4096,256]{1,0:T(8,128)} %bitcast.41, f32[4096,256]{1,0:T(8,128)} %bitcast.42, f32[2,4,64]{2,1,0:T(4,128)} %rates.1), custom_call_target="tpu_custom_call" | custom-call | tf_op jit(solution)/shard_map/edges/pallas_call | solution.py:131
  8.4 11.5 %all-to-all-start = ((f32[640,1,128]{2,1,0:T(1,128)}), f32[640,1,128]{2,1,0:T(1,128)S(1)}, u32[]{:S(2)}, u32[]{:S(2)}) async-start(f32[640,1,128]{2,1,0:T(1,128)} %bitcast.48), calls=%async_computation | async-start | bytes 655360 | tf_op jit(solution)/shard_map/all_to_all | solution.py:586
  20.7 7.7 %local.1.cc = f32[16,256,256]{2,1,0:T(8,128)} custom-call(f32[16,256,256]{2,1,0:T(8,128)} %get-tuple-element.21.planes.control, f32[256,128]{1,0:T(8,128)} %get-tuple-element.23.colx, f32[256,128]{1,0:T(8,128)} %get-tuple-element.24.coly), custom_call_target="tpu_custom_call" | custom-call | flops 1073741824 | bytes 8388608 | tf_op jit(solution)/shard_map/local/pallas_call | solution.py:224
  28.5 1.9 %prepare.1 = (f32[128,128]{1,0:T(8,128)S(1)}, f32[128,512]{1,0:T(8,128)S(1)}, f32[128,512]{1,0:T(8,128)S(1)}, f32[128,512]{1,0:T(8,128)S(1)}, f32[8,128]{1,0:T(8,128)S(1)}) custom-call(s32[3]{0:T(128)S(1)} %pad_add_fusion.place, s32[1]{0:T(128)S(6)} %copy.23.count, f32[2,256]{1,0:T(2,128)S(1)} %reshape.97.rates, s32[1,512]{1,0:T(1,128)S(1)} %bitcast.37, ...), custom_call_target="tpu_custom_call" | custom-call | flops 1073741824 | bytes 1048576 | tf_op jit(solution)/shard_map/prepare/pallas_call | solution.py:190
  30.4 0.9 all-to-all-done
  31.3 1.2 %carry.1 = f32[640,128]{1,0:T(8,128)} custom-call(f32[640,128]{1,0:T(8,128)S(1)} %bitcast.36, f32[128,512]{1,0:T(8,128)S(1)} %get-tuple-element.31.weights, f32[8,128]{1,0:T(8,128)S(1)} %get-tuple-element.32.down.refs_2_, f32[128,128]{1,0:T(8,128)S(1)} %get-tuple-element.33.requests), custom_call_target="tpu_custom_call" | custom-call | tf_op jit(solution)/shard_map/carry/pallas_call | solution.py:340
  32.5 8.9 %all-to-all-start.1 = ((f32[640,1,128]{2,1,0:T(1,128)}), f32[640,1,128]{2,1,0:T(1,128)S(1)}, u32[]{:S(2)}, u32[]{:S(2)}) async-start(f32[640,1,128]{2,1,0:T(1,128)} %bitcast.17), calls=%async_computation.1 | async-start | bytes 655360 | tf_op jit(solution)/shard_map/all_to_all | solution.py:586
  41.7 0.8 reshape.98.matrix
  42.5 0.7 copy.20.level_weights
  43.2 0.8 broadcast_in_dim.2
  44.0 6.4 %share.1 = f32[16,64,256]{2,1,0:T(8,128)} custom-call(f32[4,1024,256]{2,1,0:T(8,128)} %bitcast.43, f32[1024,4]{1,0:T(8,128)} %bitcast.45), custom_call_target="tpu_custom_call" | custom-call | flops 2097152 | bytes 5242880 | tf_op jit(solution)/shard_map/share/pallas_call | solution.py:247
  50.5 7.1 %levels.1 = (f32[1024,256]{1,0:T(8,128)}, f32[1024,256]{1,0:T(8,128)}, bf16[256,1024]{1,0:T(8,128)(2,1)}, bf16[256,1024]{1,0:T(8,128)(2,1)}) custom-call(f32[16,256,256]{2,1,0:T(8,128)} %local.1.cc, f32[16,64,256]{2,1,0:T(8,128)} %share.1, f32[256,128]{1,0:T(8,128)} %get-tuple-element.24.coly, f32[2,256]{1,0:T(2,128)} %copy-done, f32[64,256]{1,0:T(8,128)} %reshape.98.matrix), custom_call_target="tpu_custom_call" | custom-call | flops 402653184 | bytes 8388608 | tf_op jit(solution)/shard_map/levels/pallas_call | solution.py:286
  57.6 0.7 copy-done.6
  58.3 10.0 %observations.1 = (f32[1024,256]{1,0:T(8,128)}, f32[640,128]{1,0:T(8,128)}) custom-call(f32[1024,256]{1,0:T(8,128)} %get-tuple-element.26.level, f32[1024,256]{1,0:T(8,128)} %get-tuple-element.27.scaled, bf16[256,1024]{1,0:T(8,128)(2,1)} %get-tuple-element.28.turned_high, bf16[256,1024]{1,0:T(8,128)(2,1)} %get-tuple-element.29.turned_low, ...), custom_call_target="tpu_custom_call" | custom-call | tf_op jit(solution)/shard_map/observations/pallas_call | solution.py:429
  68.4 9.8 %all-to-all-start.2 = ((f32[640,1,128]{2,1,0:T(1,128)}), f32[640,1,128]{2,1,0:T(1,128)S(1)}, u32[]{:S(2)}, u32[]{:S(2)}) async-start(f32[640,1,128]{2,1,0:T(1,128)} %bitcast.49), calls=%async_computation.2 | async-start | bytes 655360 | tf_op jit(solution)/shard_map/all_to_all | solution.py:586
  78.1 7.2 %planes_back.1.running = f32[16,256,256]{2,1,0:T(8,128)} custom-call(f32[1024,256]{1,0:T(8,128)} %get-tuple-element.35.forced, bf16[256,1024]{1,0:T(8,128)(2,1)} %get-tuple-element.28.turned_high, bf16[256,1024]{1,0:T(8,128)(2,1)} %get-tuple-element.29.turned_low, f32[256,128]{1,0:T(8,128)} %get-tuple-element.24.coly), custom_call_target="tpu_custom_call" | custom-call | flops 2147483648 | bytes 8388608 | tf_op jit(solution)/shard_map/planes_back/pallas_call | solution.py:472
  85.3 4.2 %all-to-all-done.2 = f32[640,1,128]{2,1,0:T(1,128)S(1)} async-done(((f32[640,1,128]{2,1,0:T(1,128)}), f32[640,1,128]{2,1,0:T(1,128)S(1)}, u32[]{:S(2)}, u32[]{:S(2)}) %all-to-all-start.2) | async-done | bytes 327712 | tf_op jit(solution)/shard_map/all_to_all | solution.py:586
  89.5 1.2 %carry_back.1 = f32[640,128]{1,0:T(8,128)} custom-call(f32[640,128]{1,0:T(8,128)S(1)} %bitcast.34, f32[128,512]{1,0:T(8,128)S(1)} %get-tuple-element.38.refs_1_, f32[8,128]{1,0:T(8,128)S(1)} %get-tuple-element.32.down.refs_2_), custom_call_target="tpu_custom_call" | custom-call | tf_op jit(solution)/shard_map/carry_back/pallas_call | solution.py:336
  90.7 5.6 %all-to-all-start.3 = ((f32[640,1,128]{2,1,0:T(1,128)}), f32[640,1,128]{2,1,0:T(1,128)S(1)}, u32[]{:S(2)}, u32[]{:S(2)}) async-start(f32[640,1,128]{2,1,0:T(1,128)} %bitcast.24), calls=%async_computation.3 | async-start | bytes 655360 | tf_op jit(solution)/shard_map/all_to_all | solution.py:586
  96.3 0.9 departures.1
  97.2 8.5 %join.1.partial = f32[16,256,256]{2,1,0:T(8,128)} custom-call(f32[16,256,256]{2,1,0:T(8,128)} %get-tuple-element.21.planes.control, f32[16,256,256]{2,1,0:T(8,128)} %planes_back.1.running, f32[256,128]{1,0:T(8,128)} %get-tuple-element.23.colx, f32[256,128]{1,0:T(8,128)} %get-tuple-element.24.coly), custom_call_target="tpu_custom_call" | custom-call | flops 1073741824 | bytes 12582912 | tf_op jit(solution)/shard_map/join/pallas_call | solution.py:497
  105.7 2.0 %all-to-all-done.3 = f32[640,1,128]{2,1,0:T(1,128)S(1)} async-done(((f32[640,1,128]{2,1,0:T(1,128)}), f32[640,1,128]{2,1,0:T(1,128)S(1)}, u32[]{:S(2)}, u32[]{:S(2)}) %all-to-all-start.3) | async-done | bytes 327712 | tf_op jit(solution)/shard_map/all_to_all | solution.py:586
  107.6 0.7 copy-done.5
  108.4 7.8 %final.1 = f32[4096,256]{1,0:T(8,128)} custom-call(f32[16,256,256]{2,1,0:T(8,128)} %join.1.partial, f32[640,128]{1,0:T(8,128)} %bitcast.46, f32[256,128]{1,0:T(8,128)} %get-tuple-element.23.colx, f32[256,128]{1,0:T(8,128)} %get-tuple-element.24.coly), custom_call_target="tpu_custom_call" | custom-call | tf_op jit(solution)/shard_map/final/pallas_call | solution.py:547
  (27 shorter events, 0.5 us)
Async XLA Ops:
  0.6 19.3 %copy-start.8 = (f32[2,4,64]{2,1,0:T(4,128)S(1)}, f32[2,4,64]{2,1,0:T(4,128)}, u32[]{:S(2)}) copy-start(f32[2,4,64]{2,1,0:T(4,128)} %rates.1) | copy-start | bytes 6148
  8.4 22.9 %all-to-all-start = ((f32[640,1,128]{2,1,0:T(1,128)}), f32[640,1,128]{2,1,0:T(1,128)S(1)}, u32[]{:S(2)}, u32[]{:S(2)}) async-start(f32[640,1,128]{2,1,0:T(1,128)} %bitcast.48), calls=%async_computation | async-start | bytes 655360 | tf_op jit(solution)/shard_map/all_to_all | solution.py:586
  20.0 8.5 %copy-start = (f32[2,256]{1,0:T(2,128)}, f32[2,256]{1,0:T(2,128)S(1)}, u32[]{:S(2)}) copy-start(f32[2,256]{1,0:T(2,128)S(1)} %reshape.97.rates) | copy-start | bytes 6148
  20.7 7.8 %copy-start.1 = (s32[512,1]{0,1:T(1,128)S(1)}, s32[512,1]{0,1:T(1,128)}, u32[]{:S(2)}) copy-start(s32[512,1]{0,1:T(1,128)} %param.17) | copy-start | bytes 6148
  20.7 7.8 %copy-start.2 = (s32[512]{0:T(512)S(1)}, s32[512]{0:T(512)}, u32[]{:S(2)}) copy-start(s32[512]{0:T(512)} %param.18) | copy-start | bytes 6148
  20.7 7.8 %copy-start.3 = (f32[512]{0:T(512)S(1)}, f32[512]{0:T(512)}, u32[]{:S(2)}) copy-start(f32[512]{0:T(512)} %param.20) | copy-start | bytes 6148
  20.7 7.8 %copy-start.4 = (f32[512]{0:T(512)S(1)}, f32[512]{0:T(512)}, u32[]{:S(2)}) copy-start(f32[512]{0:T(512)} %param.21) | copy-start | bytes 6148
  28.4 13.0 %copy-start.9 = (f32[4,64]{1,0:T(4,128)S(1)}, f32[4,64]{1,0:T(4,128)}, u32[]{:S(2)}) copy-start(f32[4,64]{1,0:T(4,128)} %param.15) | copy-start | bytes 3076
  28.4 13.1 %copy-start.7 = (f32[4,64,64]{2,1,0:T(8,128)S(1)}, f32[4,64,64]{2,1,0:T(8,128)}, u32[]{:S(2)}) copy-start(f32[4,64,64]{2,1,0:T(8,128)} %param.13) | copy-start | bytes 196612
  28.4 14.1 %copy-start.10 = (f32[64]{0:T(128)S(1)}, f32[64]{0:T(128)}, u32[]{:S(2)}) copy-start(f32[64]{0:T(128)} %param.16) | copy-start | bytes 772
  32.5 25.1 %all-to-all-start.1 = ((f32[640,1,128]{2,1,0:T(1,128)}), f32[640,1,128]{2,1,0:T(1,128)S(1)}, u32[]{:S(2)}, u32[]{:S(2)}) async-start(f32[640,1,128]{2,1,0:T(1,128)} %bitcast.17), calls=%async_computation.1 | async-start | bytes 655360 | tf_op jit(solution)/shard_map/all_to_all | solution.py:586
  57.6 0.7 copy-start.6
  68.4 21.1 %all-to-all-start.2 = ((f32[640,1,128]{2,1,0:T(1,128)}), f32[640,1,128]{2,1,0:T(1,128)S(1)}, u32[]{:S(2)}, u32[]{:S(2)}) async-start(f32[640,1,128]{2,1,0:T(1,128)} %bitcast.49), calls=%async_computation.2 | async-start | bytes 655360 | tf_op jit(solution)/shard_map/all_to_all | solution.py:586
  90.7 17.0 %all-to-all-start.3 = ((f32[640,1,128]{2,1,0:T(1,128)}), f32[640,1,128]{2,1,0:T(1,128)S(1)}, u32[]{:S(2)}, u32[]{:S(2)}) async-start(f32[640,1,128]{2,1,0:T(1,128)} %bitcast.24), calls=%async_computation.3 | async-start | bytes 655360 | tf_op jit(solution)/shard_map/all_to_all | solution.py:586
  107.6 0.7 copy-start.5

commit v4 on v3

--- a/solution.py
+++ b/solution.py
@@ -14,7 +14,9 @@
 CH, LEVELS, XB, YB = 256, 64, 16, 256
 OBS, PEERS, CAP = 512, 128, 8
 N_X, N_Y = 8, 16
-BLOCK = 32
+BLOCK = 64
+HALF = 128 // BLOCK
+DEEP = 4
 REQ = 32
 ROWS = 5
 MIB = 1024 * 1024
@@ -108,7 +110,7 @@
     factor = wide(jnp.exp(colx[rows, :]))
     scale = grow(coly[rows, :], BLOCK)
     running = jnp.zeros((BLOCK, YB), f32)
-    place = iota((BLOCK, 128), 1) - 16 * (b // 4)
+    place = iota((BLOCK, 128), 1) - 16 * (b // HALF)
     sums = jnp.zeros((BLOCK, 128), f32)
     for x in range(XB):
         plane = take_plane((control_a, control_b), x, BLOCK)
@@ -116,10 +118,10 @@
         running = running + plane * scale
         scale = scale * factor
         sums = jnp.where(place == x, jnp.sum(running, axis=1, keepdims=True), sums)
-    start = (b % 4) * (BLOCK * ROWS) + 2 * (b // 4)
+    start = (b % HALF) * (BLOCK * ROWS) + 2 * (b // HALF)
     msg[pl.ds(start, BLOCK, stride=ROWS), :] = running[:, :128]
     msg[pl.ds(start + 1, BLOCK, stride=ROWS), :] = running[:, 128:]
-    back = pl.ds(pl.multiple_of((b % 4) * BLOCK, BLOCK), BLOCK)
+    back = pl.ds(pl.multiple_of((b % HALF) * BLOCK, BLOCK), BLOCK)
     tail[back, :] = tail[back, :] + sums
 
     @pl.when(b == CH // BLOCK - 1)
@@ -240,20 +242,20 @@
     half_a[...] = total[:, :128]
     half_b[...] = total[:, 128:]
     for x in range(XB):
-        share[x] = take_plane((half_a, half_b), x, 8)
+        share[x] = take_plane((half_a, half_b), x, 32)
 
 
 def background_share(background, weights):
     return pl.pallas_call(
         share_kernel,
-        grid=(8,),
+        grid=(2,),
         in_specs=[
-            pl.BlockSpec((4, 128, YB), lambda b: (0, b, 0)),
-            pl.BlockSpec((128, 4), lambda b: (b, 0)),
+            pl.BlockSpec((4, 512, YB), lambda b: (0, b, 0)),
+            pl.BlockSpec((512, 4), lambda b: (b, 0)),
         ],
-        out_specs=pl.BlockSpec((XB, 8, YB), lambda b: (0, b, 0)),
+        out_specs=pl.BlockSpec((XB, 32, YB), lambda b: (0, b, 0)),
         out_shape=jax.ShapeDtypeStruct((XB, LEVELS, YB), f32),
-        scratch_shapes=[pltpu.VMEM((128, 128), f32), pltpu.VMEM((128, 128), f32)],
+        scratch_shapes=[pltpu.VMEM((512, 128), f32), pltpu.VMEM((512, 128), f32)],
         compiler_params=params(57),
         cost_estimate=pl.CostEstimate(flops=1 << 21, bytes_accessed=5 << 20, transcendentals=0),
         name="share",
@@ -267,8 +269,8 @@
     def _():
         decay[...] = grow(coly[...], CH, -1.0)
 
-    for i in range(2):
-        x = (2 * b + i).astype(f32)
+    for i in range(DEEP):
+        x = (DEEP * b + i).astype(f32)
         at = slice(i * LEVELS, (i + 1) * LEVELS)
         part = matrix[...] * jnp.exp(rates[0:1, :] * (x * (-1.0 / 128.0)))
         scaled[at, :] = part
@@ -276,18 +278,20 @@
         high, low = split(decay[...] * cc[i])
         pair = mm(jnp.concatenate([mh, ml], axis=0), high)
         level[at, :] = (pair[:LEVELS] + (pair[LEVELS:] + mm(mh, low))) + share[i]
-    turned = jnp.concatenate([scaled[:, :128].T, scaled[:, 128:].T], axis=0)
-    turned_high[...], turned_low[...] = split(turned)
+    for i in range(0, DEEP * LEVELS, 128):
+        part = scaled[i : i + 128, :]
+        turned = jnp.concatenate([part[:, :128].T, part[:, 128:].T], axis=0)
+        turned_high[:, i : i + 128], turned_low[:, i : i + 128] = split(turned)
 
 
 def levels_of(cc, share, coly, rates, matrix):
     two = lambda shape: pl.BlockSpec(shape, lambda b: (b,) + (0,) * (len(shape) - 1))
-    lanes = pl.BlockSpec((CH, 128), lambda b: (0, b))
+    lanes = pl.BlockSpec((CH, DEEP * LEVELS), lambda b: (0, b))
     return pl.pallas_call(
         levels_kernel,
-        grid=(XB // 2,),
-        in_specs=[two((2, CH, YB)), two((2, LEVELS, YB)), whole((CH, 128)), whole((2, CH)), whole((LEVELS, CH))],
-        out_specs=[two((128, YB)), two((128, CH)), lanes, lanes],
+        grid=(XB // DEEP,),
+        in_specs=[two((DEEP, CH, YB)), two((DEEP, LEVELS, YB)), whole((CH, 128)), whole((2, CH)), whole((LEVELS, CH))],
+        out_specs=[two((DEEP * LEVELS, YB)), two((DEEP * LEVELS, CH)), lanes, lanes],
         out_shape=[
             jax.ShapeDtypeStruct((XB * LEVELS, YB), f32),
             jax.ShapeDtypeStruct((XB * LEVELS, CH), f32),
@@ -456,24 +460,25 @@
     gh, gl = split(forced[...])
     th, tl = turned_high[...], turned_low[...]
     none = jnp.zeros((LEVELS, YB), bf16)
-    for i in (1, 0):
+    for i in range(DEEP - 1, -1, -1):
         half = slice(i * LEVELS, (i + 1) * LEVELS)
-        fill = lambda part: stack_rows(none, part[half]) if i else stack_rows(part[half], none)
+        at = slice(i // 2 * 128, i // 2 * 128 + 128)
+        fill = lambda part: stack_rows(none, part[half]) if i % 2 else stack_rows(part[half], none)
         high, low = fill(gh), fill(gl)
-        back = mm(stack_lanes(th, tl), stack_rows(high, high)) + mm(th, low)
+        back = mm(stack_lanes(th[:, at], tl[:, at]), stack_rows(high, high)) + mm(th[:, at], low)
         running[...] = running[...] + back * decay[...]
         out[i] = running[...]
 
 
 def planes_back(forced, turned_high, turned_low, coly):
-    last = XB // 2 - 1
-    lanes = pl.BlockSpec((CH, 128), lambda b: (0, last - b))
+    last = XB // DEEP - 1
+    lanes = pl.BlockSpec((CH, DEEP * LEVELS), lambda b: (0, last - b))
     field = pltpu.VMEM((CH, YB), f32)
     return pl.pallas_call(
         planes_back_kernel,
-        grid=(XB // 2,),
-        in_specs=[pl.BlockSpec((128, YB), lambda b: (last - b, 0)), lanes, lanes, whole((CH, 128))],
-        out_specs=pl.BlockSpec((2, CH, YB), lambda b: (last - b, 0, 0)),
+        grid=(XB // DEEP,),
+        in_specs=[pl.BlockSpec((DEEP * LEVELS, YB), lambda b: (last - b, 0)), lanes, lanes, whole((CH, 128))],
+        out_specs=pl.BlockSpec((DEEP, CH, YB), lambda b: (last - b, 0, 0)),
         out_shape=jax.ShapeDtypeStruct((XB, CH, YB), f32),
         scratch_shapes=[field, field],
         compiler_params=params(57),
@@ -508,15 +513,15 @@
 
 def final_kernel(partial, entered, colx, coly, out, whole_a, whole_b, sems):
     b = pl.program_id(0)
-    start = (b % 4) * (BLOCK * ROWS)
+    start = (b % HALF) * (BLOCK * ROWS)
     entering = jnp.concatenate(
-        [entered[pl.ds(start + 2 * (b // 4) + h, BLOCK, stride=ROWS), :] for h in range(2)], axis=1
+        [entered[pl.ds(start + 2 * (b // HALF) + h, BLOCK, stride=ROWS), :] for h in range(2)], axis=1
     )
     high, low = split(entering)
     sums = lower()
     entering = mm(high, sums) + mm(low, sums)
     tail = entered[pl.ds(start + 4, BLOCK, stride=ROWS), :]
-    mine = jnp.where(b < 4, tail, pltpu.roll(tail, 112, 1))
+    mine = jnp.where(b < HALF, tail, pltpu.roll(tail, 112, 1))
     factor = wide(jnp.exp(colx[...]))
     scale = grow(coly[...], BLOCK)
     for x in range(XB):

time: 118 us -> 106 us (0.90)
  Pallas kernels: 67.7 us -> 53.6 us
  waiting for transfers between devices: 7 us -> 13.1 us
  starting transfers between devices: 35.8 us -> 32.8 us
    pallas_call x3, Pallas kernels: 20.8 us -> 14 us  [the longest x1 5.21 us: planes_back(): pl.pallas_call(planes_back_kernel, grid=(XB // DEEP,), in_specs=[pl.Block...]
    all_to_all x4, waiting for transfers between devices: 7 us -> 13.1 us  [everywhere(): lax.all_to_all(shaped, ('gx', 'gy'), split_axis=0, concat_axis=0, tiled=T...]
    all_to_all x4, starting transfers between devices: 35.8 us -> 32.8 us  [everywhere(): lax.all_to_all(shaped, ('gx', 'gy'), split_axis=0, concat_axis=0, tiled=T...]
    pallas_call x1, Pallas kernels: 7.67 us -> 5.67 us  [local(): pl.pallas_call(local_kernel, grid=(CH // BLOCK,), in_specs=[PLANES, STEPS...]
    pallas_call x1, Pallas kernels: 8.51 us -> 6.57 us  [join(): pl.pallas_call(join_kernel, grid=(CH // BLOCK,), in_specs=[PLANES, PLANES...]
    pallas_call x1, Pallas kernels: 7.77 us -> 5.95 us  [final(): pl.pallas_call(final_kernel, grid=(CH // BLOCK,), in_specs=[PLANES, whole...]
    pallas_call x1, Pallas kernels: 7.79 us -> 6.24 us  [edges(): pl.pallas_call(edges_kernel, grid=(CH // BLOCK,), in_specs=CONTROL + [who...]
  transfers between devices with their start and end apart: 4 -> 4, of which waited for: 3 -> 3; matrix products, arithmetic and copies ran while one was open for 2% -> 3% of each run, Pallas kernels for 34% -> 28%
where the time goes in v4:
time: 106 us; the launch traced here: 105 us
  Pallas kernels  53.6 us (51%)
  starting transfers between devices  32.8 us (31%)
  waiting for transfers between devices  13.1 us (12%)
  local copies, waits for them, and re-layouts  4.07 us (4%)
  between operations  1.45 us (1%)
    all_to_all x4, starting transfers between devices, everywhere(): lax.all_to_all(shaped, ('gx', 'gy'), split_axis=0, concat_axis=0, tiled=T...  32.8 us
    all_to_all x4, waiting for transfers between devices, everywhere(): lax.all_to_all(shaped, ('gx', 'gy'), split_axis=0, concat_axis=0, tiled=T...  13.1 us
    pallas_call x1, Pallas kernels, observations(): pl.pallas_call(observe_kernel, in_specs=[VMEM] * 8, out_specs=[VMEM, VMEM...  10 us
    pallas_call x1, Pallas kernels, join(): pl.pallas_call(join_kernel, grid=(CH // BLOCK,), in_specs=[PLANES, PLANES...  6.57 us
    pallas_call x1, Pallas kernels, edges(): pl.pallas_call(edges_kernel, grid=(CH // BLOCK,), in_specs=CONTROL + [who...  6.24 us
    pallas_call x1, Pallas kernels, final(): pl.pallas_call(final_kernel, grid=(CH // BLOCK,), in_specs=[PLANES, whole...  5.95 us
    pallas_call x1, Pallas kernels, local(): pl.pallas_call(local_kernel, grid=(CH // BLOCK,), in_specs=[PLANES, STEPS...  5.67 us
    pallas_call x1, Pallas kernels, planes_back(): pl.pallas_call(planes_back_kernel, grid=(XB // DEEP,), in_specs=[pl.Block...  5.21 us
  transfers between devices with their start and end apart: 4, of which 3 were waited for; matrix products, arithmetic and copies ran while one was open for 3% of the time, Pallas kernels for 28%

profile of v4, /device:TPU:1, one launch (start us, length us, event | category | flops | bytes accessed | tf_op | source)
XLA Modules:
  0.0 105.2 jit_solution(11560014224348305646)
XLA Ops:
  0.6 6.2 %edges.1 = (f32[640,128]{1,0:T(8,128)}, f32[256,128]{1,0:T(8,128)}, f32[256,128]{1,0:T(8,128)}, f32[16,256,256]{2,1,0:T(8,128)}) custom-call(f32[4096,256]{1,0:T(8,128)} %bitcast.41, f32[4096,256]{1,0:T(8,128)} %bitcast.42, f32[2,4,64]{2,1,0:T(4,128)} %rates.1), custom_call_target="tpu_custom_call" | custom-call | tf_op jit(solution)/shard_map/edges/pallas_call | solution.py:133
  6.9 11.5 %all-to-all-start = ((f32[640,1,128]{2,1,0:T(1,128)}), f32[640,1,128]{2,1,0:T(1,128)S(1)}, u32[]{:S(2)}, u32[]{:S(2)}) async-start(f32[640,1,128]{2,1,0:T(1,128)} %bitcast.48), calls=%async_computation | async-start | bytes 655360 | tf_op jit(solution)/shard_map/all_to_all | solution.py:591
  19.2 5.7 %local.1.cc = f32[16,256,256]{2,1,0:T(8,128)} custom-call(f32[16,256,256]{2,1,0:T(8,128)} %get-tuple-element.21.planes.control, f32[256,128]{1,0:T(8,128)} %get-tuple-element.23.colx, f32[256,128]{1,0:T(8,128)} %get-tuple-element.24.coly), custom_call_target="tpu_custom_call" | custom-call | flops 1073741824 | bytes 8388608 | tf_op jit(solution)/shard_map/local/pallas_call | solution.py:226
  25.0 1.9 %prepare.1 = (f32[128,128]{1,0:T(8,128)S(1)}, f32[128,512]{1,0:T(8,128)S(1)}, f32[128,512]{1,0:T(8,128)S(1)}, f32[128,512]{1,0:T(8,128)S(1)}, f32[8,128]{1,0:T(8,128)S(1)}) custom-call(s32[3]{0:T(128)S(1)} %pad_add_fusion.place, s32[1]{0:T(128)S(6)} %copy.23.count, f32[2,256]{1,0:T(2,128)S(1)} %reshape.97.rates, s32[1,512]{1,0:T(1,128)S(1)} %bitcast.37, ...), custom_call_target="tpu_custom_call" | custom-call | flops 1073741824 | bytes 1048576 | tf_op jit(solution)/shard_map/prepare/pallas_call | solution.py:192
  26.9 2.9 %all-to-all-done = f32[640,1,128]{2,1,0:T(1,128)S(1)} async-done(((f32[640,1,128]{2,1,0:T(1,128)}), f32[640,1,128]{2,1,0:T(1,128)S(1)}, u32[]{:S(2)}, u32[]{:S(2)}) %all-to-all-start) | async-done | bytes 327712 | tf_op jit(solution)/shard_map/all_to_all | solution.py:591
  29.7 1.2 %carry.1 = f32[640,128]{1,0:T(8,128)} custom-call(f32[640,128]{1,0:T(8,128)S(1)} %bitcast.36, f32[128,512]{1,0:T(8,128)S(1)} %get-tuple-element.31.weights, f32[8,128]{1,0:T(8,128)S(1)} %get-tuple-element.32.down.refs_2_, f32[128,128]{1,0:T(8,128)S(1)} %get-tuple-element.33.requests), custom_call_target="tpu_custom_call" | custom-call | tf_op jit(solution)/shard_map/carry/pallas_call | solution.py:344
  30.9 6.9 %all-to-all-start.1 = ((f32[640,1,128]{2,1,0:T(1,128)}), f32[640,1,128]{2,1,0:T(1,128)S(1)}, u32[]{:S(2)}, u32[]{:S(2)}) async-start(f32[640,1,128]{2,1,0:T(1,128)} %bitcast.17), calls=%async_computation.1 | async-start | bytes 655360 | tf_op jit(solution)/shard_map/all_to_all | solution.py:591
  38.2 0.8 reshape.98.matrix
  38.9 0.7 copy.20.level_weights
  39.7 0.8 broadcast_in_dim.2
  40.5 3.7 %share.1 = f32[16,64,256]{2,1,0:T(8,128)} custom-call(f32[4,1024,256]{2,1,0:T(8,128)} %bitcast.43, f32[1024,4]{1,0:T(8,128)} %bitcast.45), custom_call_target="tpu_custom_call" | custom-call | flops 2097152 | bytes 5242880 | tf_op jit(solution)/shard_map/share/pallas_call | solution.py:249
  44.2 5.1 %levels.1 = (f32[1024,256]{1,0:T(8,128)}, f32[1024,256]{1,0:T(8,128)}, bf16[256,1024]{1,0:T(8,128)(2,1)}, bf16[256,1024]{1,0:T(8,128)(2,1)}) custom-call(f32[16,256,256]{2,1,0:T(8,128)} %local.1.cc, f32[16,64,256]{2,1,0:T(8,128)} %share.1, f32[256,128]{1,0:T(8,128)} %get-tuple-element.24.coly, f32[2,256]{1,0:T(2,128)} %copy-done, f32[64,256]{1,0:T(8,128)} %reshape.98.matrix), custom_call_target="tpu_custom_call" | custom-call | flops 402653184 | bytes 8388608 | tf_op jit(solution)/shard_map/levels/pallas_call | solution.py:290
  49.3 0.7 copy-done.6
  50.0 10.0 %observations.1 = (f32[1024,256]{1,0:T(8,128)}, f32[640,128]{1,0:T(8,128)}) custom-call(f32[1024,256]{1,0:T(8,128)} %get-tuple-element.26.level, f32[1024,256]{1,0:T(8,128)} %get-tuple-element.27.scaled, bf16[256,1024]{1,0:T(8,128)(2,1)} %get-tuple-element.28.turned_high, bf16[256,1024]{1,0:T(8,128)(2,1)} %get-tuple-element.29.turned_low, ...), custom_call_target="tpu_custom_call" | custom-call | tf_op jit(solution)/shard_map/observations/pallas_call | solution.py:433
  60.1 9.8 %all-to-all-start.2 = ((f32[640,1,128]{2,1,0:T(1,128)}), f32[640,1,128]{2,1,0:T(1,128)S(1)}, u32[]{:S(2)}, u32[]{:S(2)}) async-start(f32[640,1,128]{2,1,0:T(1,128)} %bitcast.49), calls=%async_computation.2 | async-start | bytes 655360 | tf_op jit(solution)/shard_map/all_to_all | solution.py:591
  69.8 5.2 %planes_back.1.running = f32[16,256,256]{2,1,0:T(8,128)} custom-call(f32[1024,256]{1,0:T(8,128)} %get-tuple-element.35.forced, bf16[256,1024]{1,0:T(8,128)(2,1)} %get-tuple-element.28.turned_high, bf16[256,1024]{1,0:T(8,128)(2,1)} %get-tuple-element.29.turned_low, f32[256,128]{1,0:T(8,128)} %get-tuple-element.24.coly), custom_call_target="tpu_custom_call" | custom-call | flops 2147483648 | bytes 8388608 | tf_op jit(solution)/shard_map/planes_back/pallas_call | solution.py:477
  75.0 6.1 %all-to-all-done.2 = f32[640,1,128]{2,1,0:T(1,128)S(1)} async-done(((f32[640,1,128]{2,1,0:T(1,128)}), f32[640,1,128]{2,1,0:T(1,128)S(1)}, u32[]{:S(2)}, u32[]{:S(2)}) %all-to-all-start.2) | async-done | bytes 327712 | tf_op jit(solution)/shard_map/all_to_all | solution.py:591
  81.2 1.2 %carry_back.1 = f32[640,128]{1,0:T(8,128)} custom-call(f32[640,128]{1,0:T(8,128)S(1)} %bitcast.34, f32[128,512]{1,0:T(8,128)S(1)} %get-tuple-element.38.refs_1_, f32[8,128]{1,0:T(8,128)S(1)} %get-tuple-element.32.down.refs_2_), custom_call_target="tpu_custom_call" | custom-call | tf_op jit(solution)/shard_map/carry_back/pallas_call | solution.py:340
  82.4 4.7 %all-to-all-start.3 = ((f32[640,1,128]{2,1,0:T(1,128)}), f32[640,1,128]{2,1,0:T(1,128)S(1)}, u32[]{:S(2)}, u32[]{:S(2)}) async-start(f32[640,1,128]{2,1,0:T(1,128)} %bitcast.24), calls=%async_computation.3 | async-start | bytes 655360 | tf_op jit(solution)/shard_map/all_to_all | solution.py:591
  87.1 0.9 departures.1
  87.9 6.6 %join.1.partial = f32[16,256,256]{2,1,0:T(8,128)} custom-call(f32[16,256,256]{2,1,0:T(8,128)} %get-tuple-element.21.planes.control, f32[16,256,256]{2,1,0:T(8,128)} %planes_back.1.running, f32[256,128]{1,0:T(8,128)} %get-tuple-element.23.colx, f32[256,128]{1,0:T(8,128)} %get-tuple-element.24.coly), custom_call_target="tpu_custom_call" | custom-call | flops 1073741824 | bytes 12582912 | tf_op jit(solution)/shard_map/join/pallas_call | solution.py:502
  94.5 4.0 %all-to-all-done.3 = f32[640,1,128]{2,1,0:T(1,128)S(1)} async-done(((f32[640,1,128]{2,1,0:T(1,128)}), f32[640,1,128]{2,1,0:T(1,128)S(1)}, u32[]{:S(2)}, u32[]{:S(2)}) %all-to-all-start.3) | async-done | bytes 327712 | tf_op jit(solution)/shard_map/all_to_all | solution.py:591
  98.6 0.7 copy-done.5
  99.3 6.0 %final.1 = f32[4096,256]{1,0:T(8,128)} custom-call(f32[16,256,256]{2,1,0:T(8,128)} %join.1.partial, f32[640,128]{1,0:T(8,128)} %bitcast.46, f32[256,128]{1,0:T(8,128)} %get-tuple-element.23.colx, f32[256,128]{1,0:T(8,128)} %get-tuple-element.24.coly), custom_call_target="tpu_custom_call" | custom-call | tf_op jit(solution)/shard_map/final/pallas_call | solution.py:552
  (27 shorter events, 0.5 us)
Async XLA Ops:
  0.6 17.8 %copy-start.8 = (f32[2,4,64]{2,1,0:T(4,128)S(1)}, f32[2,4,64]{2,1,0:T(4,128)}, u32[]{:S(2)}) copy-start(f32[2,4,64]{2,1,0:T(4,128)} %rates.1) | copy-start | bytes 6148
  6.9 22.9 %all-to-all-start = ((f32[640,1,128]{2,1,0:T(1,128)}), f32[640,1,128]{2,1,0:T(1,128)S(1)}, u32[]{:S(2)}, u32[]{:S(2)}) async-start(f32[640,1,128]{2,1,0:T(1,128)} %bitcast.48), calls=%async_computation | async-start | bytes 655360 | tf_op jit(solution)/shard_map/all_to_all | solution.py:591
  18.5 6.5 %copy-start = (f32[2,256]{1,0:T(2,128)}, f32[2,256]{1,0:T(2,128)S(1)}, u32[]{:S(2)}) copy-start(f32[2,256]{1,0:T(2,128)S(1)} %reshape.97.rates) | copy-start | bytes 6148
  19.1 5.8 %copy-start.1 = (s32[512,1]{0,1:T(1,128)S(1)}, s32[512,1]{0,1:T(1,128)}, u32[]{:S(2)}) copy-start(s32[512,1]{0,1:T(1,128)} %param.17) | copy-start | bytes 6148
  19.1 5.8 %copy-start.2 = (s32[512]{0:T(512)S(1)}, s32[512]{0:T(512)}, u32[]{:S(2)}) copy-start(s32[512]{0:T(512)} %param.18) | copy-start | bytes 6148
  19.2 5.8 %copy-start.3 = (f32[512]{0:T(512)S(1)}, f32[512]{0:T(512)}, u32[]{:S(2)}) copy-start(f32[512]{0:T(512)} %param.20) | copy-start | bytes 6148
  19.2 5.8 %copy-start.4 = (f32[512]{0:T(512)S(1)}, f32[512]{0:T(512)}, u32[]{:S(2)}) copy-start(f32[512]{0:T(512)} %param.21) | copy-start | bytes 6148
  24.9 13.0 %copy-start.9 = (f32[4,64]{1,0:T(4,128)S(1)}, f32[4,64]{1,0:T(4,128)}, u32[]{:S(2)}) copy-start(f32[4,64]{1,0:T(4,128)} %param.15) | copy-start | bytes 3076
  24.9 13.1 %copy-start.7 = (f32[4,64,64]{2,1,0:T(8,128)S(1)}, f32[4,64,64]{2,1,0:T(8,128)}, u32[]{:S(2)}) copy-start(f32[4,64,64]{2,1,0:T(8,128)} %param.13) | copy-start | bytes 196612
  24.9 14.1 %copy-start.10 = (f32[64]{0:T(128)S(1)}, f32[64]{0:T(128)}, u32[]{:S(2)}) copy-start(f32[64]{0:T(128)} %param.16) | copy-start | bytes 772
  30.9 18.4 %all-to-all-start.1 = ((f32[640,1,128]{2,1,0:T(1,128)}), f32[640,1,128]{2,1,0:T(1,128)S(1)}, u32[]{:S(2)}, u32[]{:S(2)}) async-start(f32[640,1,128]{2,1,0:T(1,128)} %bitcast.17), calls=%async_computation.1 | async-start | bytes 655360 | tf_op jit(solution)/shard_map/all_to_all | solution.py:591
  49.3 0.7 copy-start.6
  60.1 21.1 %all-to-all-start.2 = ((f32[640,1,128]{2,1,0:T(1,128)}), f32[640,1,128]{2,1,0:T(1,128)S(1)}, u32[]{:S(2)}, u32[]{:S(2)}) async-start(f32[640,1,128]{2,1,0:T(1,128)} %bitcast.49), calls=%async_computation.2 | async-start | bytes 655360 | tf_op jit(solution)/shard_map/all_to_all | solution.py:591
  82.4 16.2 %all-to-all-start.3 = ((f32[640,1,128]{2,1,0:T(1,128)}), f32[640,1,128]{2,1,0:T(1,128)S(1)}, u32[]{:S(2)}, u32[]{:S(2)}) async-start(f32[640,1,128]{2,1,0:T(1,128)} %bitcast.24), calls=%async_computation.3 | async-start | bytes 655360 | tf_op jit(solution)/shard_map/all_to_all | solution.py:591
  98.6 0.7 copy-start.5

commit v5 on v4

--- a/solution.py
+++ b/solution.py
@@ -14,9 +14,10 @@
 CH, LEVELS, XB, YB = 256, 64, 16, 256
 OBS, PEERS, CAP = 512, 128, 8
 N_X, N_Y = 8, 16
-BLOCK = 64
+BLOCK = 128
+SUB = 32
 HALF = 128 // BLOCK
-DEEP = 4
+DEEP = 8
 REQ = 32
 ROWS = 5
 MIB = 1024 * 1024
@@ -106,23 +107,24 @@
                 out[v * LEVELS : (v + 1) * LEVELS, :] = turned[0:LEVELS, :] * (1.0 / count)
         tail[...] = jnp.zeros((PEERS, 128), f32)
 
-    rows = pl.ds(pl.multiple_of(b * BLOCK, BLOCK), BLOCK)
-    factor = wide(jnp.exp(colx[rows, :]))
-    scale = grow(coly[rows, :], BLOCK)
-    running = jnp.zeros((BLOCK, YB), f32)
-    place = iota((BLOCK, 128), 1) - 16 * (b // HALF)
-    sums = jnp.zeros((BLOCK, 128), f32)
-    for x in range(XB):
-        plane = take_plane((control_a, control_b), x, BLOCK)
-        planes[x] = plane
-        running = running + plane * scale
-        scale = scale * factor
-        sums = jnp.where(place == x, jnp.sum(running, axis=1, keepdims=True), sums)
-    start = (b % HALF) * (BLOCK * ROWS) + 2 * (b // HALF)
-    msg[pl.ds(start, BLOCK, stride=ROWS), :] = running[:, :128]
-    msg[pl.ds(start + 1, BLOCK, stride=ROWS), :] = running[:, 128:]
-    back = pl.ds(pl.multiple_of((b % HALF) * BLOCK, BLOCK), BLOCK)
-    tail[back, :] = tail[back, :] + sums
+    place = iota((SUB, 128), 1) - 16 * (b // HALF)
+    for s in range(0, BLOCK, SUB):
+        rows = pl.ds(pl.multiple_of(b * BLOCK + s, SUB), SUB)
+        factor = wide(jnp.exp(colx[rows, :]))
+        scale = grow(coly[rows, :], SUB)
+        running = jnp.zeros((SUB, YB), f32)
+        sums = jnp.zeros((SUB, 128), f32)
+        for x in range(XB):
+            plane = take_plane((control_a, control_b), s * XB + x, SUB)
+            planes[x, s : s + SUB, :] = plane
+            running = running + plane * scale
+            scale = scale * factor
+            sums = jnp.where(place == x, jnp.sum(running, axis=1, keepdims=True), sums)
+        start = ((b % HALF) * BLOCK + s) * ROWS + 2 * (b // HALF)
+        msg[pl.ds(start, SUB, stride=ROWS), :] = running[:, :128]
+        msg[pl.ds(start + 1, SUB, stride=ROWS), :] = running[:, 128:]
+        back = pl.ds(pl.multiple_of((b % HALF) * BLOCK + s, SUB), SUB)
+        tail[back, :] = tail[back, :] + sums
 
     @pl.when(b == CH // BLOCK - 1)
     def _():
@@ -207,19 +209,21 @@
 
 
 def local_kernel(planes, colx, coly, cc):
-    factor = wide(jnp.exp(colx[...]))
-    scale = grow(coly[...], BLOCK)
-    running = jnp.zeros((BLOCK, YB), f32)
     sums = upper()
-    highs, lows = [], []
-    for x in range(XB):
-        running = running + planes[x] * scale
-        scale = scale * factor
-        high, low = split(running)
-        highs.append(high)
-        lows.append(low)
-    summed = mm(jnp.concatenate(highs, axis=0), sums) + mm(jnp.concatenate(lows, axis=0), sums)
-    cc[...] = summed.reshape(XB, BLOCK, YB)
+    for s in range(0, BLOCK, SUB):
+        at = slice(s, s + SUB)
+        factor = wide(jnp.exp(colx[at, :]))
+        scale = grow(coly[at, :], SUB)
+        running = jnp.zeros((SUB, YB), f32)
+        highs, lows = [], []
+        for x in range(XB):
+            running = running + planes[x, at, :] * scale
+            scale = scale * factor
+            high, low = split(running)
+            highs.append(high)
+            lows.append(low)
+        summed = mm(jnp.concatenate(highs, axis=0), sums) + mm(jnp.concatenate(lows, axis=0), sums)
+        cc[:, at, :] = summed.reshape(XB, SUB, YB)
 
 
 def local(planes, colx, coly):
@@ -357,7 +361,7 @@
 
 def observe_kernel(
     level, scaled, turned_high, turned_low, entered, coly, rates, level_weights,
-    forced_out, msg, left, both, spread, marks,
+    forced_out, msg, left, both, spread, marks, line,
 ):
     decay_y = grow(coly[...], CH, -1.0)
     pick = lambda row: entered[pl.ds(row, PEERS, stride=ROWS), :]
@@ -377,7 +381,8 @@
     total = level[...] + mm(left[...], stack_rows(eh, eh, el, dh, dh, dl))
     both[:, 0:256], both[:, 256:512] = split(total)
 
-    weights = level_weights[...]
+    line[0:1, 0:LEVELS] = level_weights[...]
+    weights = wide(jnp.broadcast_to(line[0:1, :], (128, 128)).T[:LEVELS, :])
     departures = []
     for r in range(0, CAP, 2):
         first, second = REQ + 3 * r, REQ + 3 * r + 3
@@ -443,6 +448,7 @@
             pltpu.VMEM((XB * LEVELS, 2 * YB), bf16),
             pltpu.VMEM((XB * LEVELS, 2 * PEERS * CAP), bf16),
             pltpu.VMEM((YB, 2 * PEERS * CAP), bf16),
+            pltpu.VMEM((8, 128), f32),
         ],
         compiler_params=params(57),
         name="observations",
@@ -488,14 +494,16 @@
 
 
 def join_kernel(control, running, colx, coly, out):
-    high, low = split(running[...].reshape(XB * BLOCK, YB))
     sums = lower()
-    summed = mm(high, sums) + mm(low, sums)
-    factor = wide(jnp.exp(colx[...]))
-    scale = grow(coly[...], BLOCK)
-    for x in range(XB):
-        out[x] = control[x] + scale * summed[x * BLOCK : (x + 1) * BLOCK, :]
-        scale = scale * factor
+    for s in range(0, BLOCK, SUB):
+        at = slice(s, s + SUB)
+        high, low = split(running[:, at, :].reshape(XB * SUB, YB))
+        summed = mm(high, sums) + mm(low, sums)
+        factor = wide(jnp.exp(colx[at, :]))
+        scale = grow(coly[at, :], SUB)
+        for x in range(XB):
+            out[x, at, :] = control[x, at, :] + scale * summed[x * SUB : (x + 1) * SUB, :]
+            scale = scale * factor
 
 
 def join(control, running, colx, coly):
@@ -522,14 +530,16 @@
     entering = mm(high, sums) + mm(low, sums)
     tail = entered[pl.ds(start + 4, BLOCK, stride=ROWS), :]
     mine = jnp.where(b < HALF, tail, pltpu.roll(tail, 112, 1))
-    factor = wide(jnp.exp(colx[...]))
-    scale = grow(coly[...], BLOCK)
-    for x in range(XB):
-        plane = partial[x] + scale * (entering + mine[:, x : x + 1])
-        scale = scale * factor
-        at = pl.ds(b * (BLOCK * XB) + x, BLOCK, stride=XB)
-        whole_a[at, :] = plane[:, :128]
-        whole_b[at, :] = plane[:, 128:]
+    for s in range(0, BLOCK, SUB):
+        own = slice(s, s + SUB)
+        factor = wide(jnp.exp(colx[own, :]))
+        scale = grow(coly[own, :], SUB)
+        for x in range(XB):
+            plane = partial[x, own, :] + scale * (entering[own, :] + mine[own, x : x + 1])
+            scale = scale * factor
+            at = pl.ds((b * BLOCK + s) * XB + x, SUB, stride=XB)
+            whole_a[at, :] = plane[:, :128]
+            whole_b[at, :] = plane[:, 128:]
 
     def copies(step):
         at = pl.ds(pl.multiple_of(step * (BLOCK * XB), BLOCK * XB), BLOCK * XB)
@@ -627,7 +637,7 @@
     share = background_share(background.reshape(4, LEVELS * XB, YB), jnp.repeat(flash_weights.T, XB, axis=0))
     level, scaled, turned_high, turned_low = levels_of(cc, share, coly, rates, matrix)
     forced, msg_back = observations(
-        level, scaled, turned_high, turned_low, entered, coly, rates, level_weights.reshape(LEVELS, 1)
+        level, scaled, turned_high, turned_low, entered, coly, rates, level_weights.reshape(1, LEVELS)
     )
     returned = everywhere(msg_back)
     planes = planes_back(forced, turned_high, turned_low, coly)

time: 106 us -> 101 us (0.953)
  Pallas kernels: 53.6 us -> 48.2 us
  waiting for transfers between devices: 13.1 us -> 17.6 us
  starting transfers between devices: 32.8 us -> 30.2 us
    all_to_all x4, waiting for transfers between devices: 13.1 us -> 17.6 us  [everywhere(): lax.all_to_all(shaped, ('gx', 'gy'), split_axis=0, concat_axis=0, tiled=T...]
    all_to_all x4, starting transfers between devices: 32.8 us -> 30.2 us  [everywhere(): lax.all_to_all(shaped, ('gx', 'gy'), split_axis=0, concat_axis=0, tiled=T...]
    pallas_call x1, Pallas kernels: 5.67 us -> 4.54 us  [local(): pl.pallas_call(local_kernel, grid=(CH // BLOCK,), in_specs=[PLANES, STEPS...]
  transfers between devices with their start and end apart: 4 -> 4, of which waited for: 3 -> 4; matrix products, arithmetic and copies ran while one was open for 3% -> 2% of each run, Pallas kernels for 28% -> 25%
where the time goes in v5:
time: 101 us
  Pallas kernels  48.2 us (48%)
  starting transfers between devices  30.2 us (30%)
  waiting for transfers between devices  17.6 us (17%)
  local copies, waits for them, and re-layouts  3.36 us (3%)
  between operations  1.59 us (2%)
    all_to_all x4, starting transfers between devices, everywhere(): lax.all_to_all(shaped, ('gx', 'gy'), split_axis=0, concat_axis=0, tiled=T...  30.2 us
    all_to_all x4, waiting for transfers between devices, everywhere(): lax.all_to_all(shaped, ('gx', 'gy'), split_axis=0, concat_axis=0, tiled=T...  17.6 us
    pallas_call x1, Pallas kernels, observations(): pl.pallas_call(observe_kernel, in_specs=[VMEM] * 8, out_specs=[VMEM, VMEM...  10 us
    pallas_call x1, Pallas kernels, join(): pl.pallas_call(join_kernel, grid=(CH // BLOCK,), in_specs=[PLANES, PLANES...  5.6 us
    pallas_call x1, Pallas kernels, edges(): pl.pallas_call(edges_kernel, grid=(CH // BLOCK,), in_specs=CONTROL + [who...  5.49 us
    pallas_call x1, Pallas kernels, final(): pl.pallas_call(final_kernel, grid=(CH // BLOCK,), in_specs=[PLANES, whole...  5.18 us
    pallas_call x1, Pallas kernels, local(): pl.pallas_call(local_kernel, grid=(CH // BLOCK,), in_specs=[PLANES, STEPS...  4.54 us
    pallas_call x1, Pallas kernels, planes_back(): pl.pallas_call(planes_back_kernel, grid=(XB // DEEP,), in_specs=[pl.Block...  4.31 us
  transfers between devices with their start and end apart: 4, of which 4 were waited for; matrix products, arithmetic and copies ran while one was open for 2% of the time, Pallas kernels for 25%

profile of v5, /device:TPU:1, one launch (start us, length us, event | category | flops | bytes accessed | tf_op | source)
XLA Modules:
  0.0 101.1 jit_solution(5221132135995269096)
XLA Ops:
  0.6 5.5 %edges.1 = (f32[640,128]{1,0:T(8,128)}, f32[256,128]{1,0:T(8,128)}, f32[256,128]{1,0:T(8,128)}, f32[16,256,256]{2,1,0:T(8,128)}) custom-call(f32[4096,256]{1,0:T(8,128)} %bitcast.41, f32[4096,256]{1,0:T(8,128)} %bitcast.42, f32[2,4,64]{2,1,0:T(4,128)} %rates.1), custom_call_target="tpu_custom_call" | custom-call | tf_op jit(solution)/shard_map/edges/pallas_call | solution.py:135
  6.1 11.5 %all-to-all-start = ((f32[640,1,128]{2,1,0:T(1,128)}), f32[640,1,128]{2,1,0:T(1,128)S(1)}, u32[]{:S(2)}, u32[]{:S(2)}) async-start(f32[640,1,128]{2,1,0:T(1,128)} %bitcast.48), calls=%async_computation | async-start | bytes 655360 | tf_op jit(solution)/shard_map/all_to_all | solution.py:601
  18.4 4.5 %local.1.cc = f32[16,256,256]{2,1,0:T(8,128)} custom-call(f32[16,256,256]{2,1,0:T(8,128)} %get-tuple-element.21.planes.control, f32[256,128]{1,0:T(8,128)} %get-tuple-element.23.colx, f32[256,128]{1,0:T(8,128)} %get-tuple-element.24.coly), custom_call_target="tpu_custom_call" | custom-call | flops 1073741824 | bytes 8388608 | tf_op jit(solution)/shard_map/local/pallas_call | solution.py:230
  23.1 1.9 %prepare.1 = (f32[128,128]{1,0:T(8,128)S(1)}, f32[128,512]{1,0:T(8,128)S(1)}, f32[128,512]{1,0:T(8,128)S(1)}, f32[128,512]{1,0:T(8,128)S(1)}, f32[8,128]{1,0:T(8,128)S(1)}) custom-call(s32[3]{0:T(128)S(1)} %pad_add_fusion.place, s32[1]{0:T(128)S(6)} %copy.21.count, f32[2,256]{1,0:T(2,128)S(1)} %reshape.97.rates, s32[1,512]{1,0:T(1,128)S(1)} %bitcast.37, ...), custom_call_target="tpu_custom_call" | custom-call | flops 1073741824 | bytes 1048576 | tf_op jit(solution)/shard_map/prepare/pallas_call | solution.py:194
  25.0 4.0 %all-to-all-done = f32[640,1,128]{2,1,0:T(1,128)S(1)} async-done(((f32[640,1,128]{2,1,0:T(1,128)}), f32[640,1,128]{2,1,0:T(1,128)S(1)}, u32[]{:S(2)}, u32[]{:S(2)}) %all-to-all-start) | async-done | bytes 327712 | tf_op jit(solution)/shard_map/all_to_all | solution.py:601
  29.0 1.2 %carry.1 = f32[640,128]{1,0:T(8,128)} custom-call(f32[640,128]{1,0:T(8,128)S(1)} %bitcast.36, f32[128,512]{1,0:T(8,128)S(1)} %get-tuple-element.31.weights, f32[8,128]{1,0:T(8,128)S(1)} %get-tuple-element.32.down.refs_2_, f32[128,128]{1,0:T(8,128)S(1)} %get-tuple-element.33.requests), custom_call_target="tpu_custom_call" | custom-call | tf_op jit(solution)/shard_map/carry/pallas_call | solution.py:348
  30.2 5.7 %all-to-all-start.1 = ((f32[640,1,128]{2,1,0:T(1,128)}), f32[640,1,128]{2,1,0:T(1,128)S(1)}, u32[]{:S(2)}, u32[]{:S(2)}) async-start(f32[640,1,128]{2,1,0:T(1,128)} %bitcast.17), calls=%async_computation.1 | async-start | bytes 655360 | tf_op jit(solution)/shard_map/all_to_all | solution.py:601
  36.3 0.8 reshape.98.matrix
  37.0 0.8 broadcast_in_dim.2
  37.9 3.7 %share.1 = f32[16,64,256]{2,1,0:T(8,128)} custom-call(f32[4,1024,256]{2,1,0:T(8,128)} %bitcast.43, f32[1024,4]{1,0:T(8,128)} %bitcast.45), custom_call_target="tpu_custom_call" | custom-call | flops 2097152 | bytes 5242880 | tf_op jit(solution)/shard_map/share/pallas_call | solution.py:253
  41.5 4.2 %levels.1 = (f32[1024,256]{1,0:T(8,128)}, f32[1024,256]{1,0:T(8,128)}, bf16[256,1024]{1,0:T(8,128)(2,1)}, bf16[256,1024]{1,0:T(8,128)(2,1)}) custom-call(f32[16,256,256]{2,1,0:T(8,128)} %local.1.cc, f32[16,64,256]{2,1,0:T(8,128)} %share.1, f32[256,128]{1,0:T(8,128)} %get-tuple-element.24.coly, f32[2,256]{1,0:T(2,128)} %copy-done, f32[64,256]{1,0:T(8,128)} %reshape.98.matrix), custom_call_target="tpu_custom_call" | custom-call | flops 402653184 | bytes 8388608 | tf_op jit(solution)/shard_map/levels/pallas_call | solution.py:294
  45.8 1.5 %all-to-all-done.1 = f32[640,1,128]{2,1,0:T(1,128)S(1)} async-done(((f32[640,1,128]{2,1,0:T(1,128)}), f32[640,1,128]{2,1,0:T(1,128)S(1)}, u32[]{:S(2)}, u32[]{:S(2)}) %all-to-all-start.1) | async-done | bytes 327712 | tf_op jit(solution)/shard_map/all_to_all | solution.py:601
  47.3 0.7 copy-done.6
  48.0 10.0 %observations.1 = (f32[1024,256]{1,0:T(8,128)}, f32[640,128]{1,0:T(8,128)}) custom-call(f32[1024,256]{1,0:T(8,128)} %get-tuple-element.26.level, f32[1024,256]{1,0:T(8,128)} %get-tuple-element.27.scaled, bf16[256,1024]{1,0:T(8,128)(2,1)} %get-tuple-element.28.turned_high, bf16[256,1024]{1,0:T(8,128)(2,1)} %get-tuple-element.29.turned_low, ...), custom_call_target="tpu_custom_call" | custom-call | tf_op jit(solution)/shard_map/observations/pallas_call | solution.py:438
  58.1 8.2 %all-to-all-start.2 = ((f32[640,1,128]{2,1,0:T(1,128)}), f32[640,1,128]{2,1,0:T(1,128)S(1)}, u32[]{:S(2)}, u32[]{:S(2)}) async-start(f32[640,1,128]{2,1,0:T(1,128)} %bitcast.49), calls=%async_computation.2 | async-start | bytes 655360 | tf_op jit(solution)/shard_map/all_to_all | solution.py:601
  66.3 4.3 %planes_back.1.running = f32[16,256,256]{2,1,0:T(8,128)} custom-call(f32[1024,256]{1,0:T(8,128)} %get-tuple-element.35.forced, bf16[256,1024]{1,0:T(8,128)(2,1)} %get-tuple-element.28.turned_high, bf16[256,1024]{1,0:T(8,128)(2,1)} %get-tuple-element.29.turned_low, f32[256,128]{1,0:T(8,128)} %get-tuple-element.24.coly), custom_call_target="tpu_custom_call" | custom-call | flops 2147483648 | bytes 8388608 | tf_op jit(solution)/shard_map/planes_back/pallas_call | solution.py:483
  70.6 7.0 %all-to-all-done.2 = f32[640,1,128]{2,1,0:T(1,128)S(1)} async-done(((f32[640,1,128]{2,1,0:T(1,128)}), f32[640,1,128]{2,1,0:T(1,128)S(1)}, u32[]{:S(2)}, u32[]{:S(2)}) %all-to-all-start.2) | async-done | bytes 327712 | tf_op jit(solution)/shard_map/all_to_all | solution.py:601
  77.7 1.2 %carry_back.1 = f32[640,128]{1,0:T(8,128)} custom-call(f32[640,128]{1,0:T(8,128)S(1)} %bitcast.34, f32[128,512]{1,0:T(8,128)S(1)} %get-tuple-element.38.refs_1_, f32[8,128]{1,0:T(8,128)S(1)} %get-tuple-element.32.down.refs_2_), custom_call_target="tpu_custom_call" | custom-call | tf_op jit(solution)/shard_map/carry_back/pallas_call | solution.py:344
  78.8 4.7 %all-to-all-start.3 = ((f32[640,1,128]{2,1,0:T(1,128)}), f32[640,1,128]{2,1,0:T(1,128)S(1)}, u32[]{:S(2)}, u32[]{:S(2)}) async-start(f32[640,1,128]{2,1,0:T(1,128)} %bitcast.24), calls=%async_computation.3 | async-start | bytes 655360 | tf_op jit(solution)/shard_map/all_to_all | solution.py:601
  83.6 0.9 departures.1
  84.4 5.6 %join.1.partial = f32[16,256,256]{2,1,0:T(8,128)} custom-call(f32[16,256,256]{2,1,0:T(8,128)} %get-tuple-element.21.planes.control, f32[16,256,256]{2,1,0:T(8,128)} %planes_back.1.running, f32[256,128]{1,0:T(8,128)} %get-tuple-element.23.colx, f32[256,128]{1,0:T(8,128)} %get-tuple-element.24.coly), custom_call_target="tpu_custom_call" | custom-call | flops 1073741824 | bytes 12582912 | tf_op jit(solution)/shard_map/join/pallas_call | solution.py:510
  90.0 5.0 %all-to-all-done.3 = f32[640,1,128]{2,1,0:T(1,128)S(1)} async-done(((f32[640,1,128]{2,1,0:T(1,128)}), f32[640,1,128]{2,1,0:T(1,128)S(1)}, u32[]{:S(2)}, u32[]{:S(2)}) %all-to-all-start.3) | async-done | bytes 327712 | tf_op jit(solution)/shard_map/all_to_all | solution.py:601
  95.0 0.7 copy-done.5
  95.8 5.2 %final.1 = f32[4096,256]{1,0:T(8,128)} custom-call(f32[16,256,256]{2,1,0:T(8,128)} %join.1.partial, f32[640,128]{1,0:T(8,128)} %bitcast.46, f32[256,128]{1,0:T(8,128)} %get-tuple-element.23.colx, f32[256,128]{1,0:T(8,128)} %get-tuple-element.24.coly), custom_call_target="tpu_custom_call" | custom-call | tf_op jit(solution)/shard_map/final/pallas_call | solution.py:562
  (24 shorter events, 0.5 us)
Async XLA Ops:
  0.6 17.0 %copy-start.8 = (f32[2,4,64]{2,1,0:T(4,128)S(1)}, f32[2,4,64]{2,1,0:T(4,128)}, u32[]{:S(2)}) copy-start(f32[2,4,64]{2,1,0:T(4,128)} %rates.1) | copy-start | bytes 6148
  6.1 22.9 %all-to-all-start = ((f32[640,1,128]{2,1,0:T(1,128)}), f32[640,1,128]{2,1,0:T(1,128)S(1)}, u32[]{:S(2)}, u32[]{:S(2)}) async-start(f32[640,1,128]{2,1,0:T(1,128)} %bitcast.48), calls=%async_computation | async-start | bytes 655360 | tf_op jit(solution)/shard_map/all_to_all | solution.py:601
  17.7 5.3 %copy-start = (f32[2,256]{1,0:T(2,128)}, f32[2,256]{1,0:T(2,128)S(1)}, u32[]{:S(2)}) copy-start(f32[2,256]{1,0:T(2,128)S(1)} %reshape.97.rates) | copy-start | bytes 6148
  18.4 4.7 %copy-start.1 = (s32[512,1]{0,1:T(1,128)S(1)}, s32[512,1]{0,1:T(1,128)}, u32[]{:S(2)}) copy-start(s32[512,1]{0,1:T(1,128)} %param.17) | copy-start | bytes 6148
  18.4 4.7 %copy-start.2 = (s32[512]{0:T(512)S(1)}, s32[512]{0:T(512)}, u32[]{:S(2)}) copy-start(s32[512]{0:T(512)} %param.18) | copy-start | bytes 6148
  18.4 4.7 %copy-start.3 = (f32[512]{0:T(512)S(1)}, f32[512]{0:T(512)}, u32[]{:S(2)}) copy-start(f32[512]{0:T(512)} %param.20) | copy-start | bytes 6148
  18.4 4.7 %copy-start.4 = (f32[512]{0:T(512)S(1)}, f32[512]{0:T(512)}, u32[]{:S(2)}) copy-start(f32[512]{0:T(512)} %param.21) | copy-start | bytes 6148
  23.0 13.0 %copy-start.9 = (f32[4,64]{1,0:T(4,128)S(1)}, f32[4,64]{1,0:T(4,128)}, u32[]{:S(2)}) copy-start(f32[4,64]{1,0:T(4,128)} %param.15) | copy-start | bytes 3076
  23.0 13.1 %copy-start.7 = (f32[4,64,64]{2,1,0:T(8,128)S(1)}, f32[4,64,64]{2,1,0:T(8,128)}, u32[]{:S(2)}) copy-start(f32[4,64,64]{2,1,0:T(8,128)} %param.13) | copy-start | bytes 196612
  30.2 17.1 %all-to-all-start.1 = ((f32[640,1,128]{2,1,0:T(1,128)}), f32[640,1,128]{2,1,0:T(1,128)S(1)}, u32[]{:S(2)}, u32[]{:S(2)}) async-start(f32[640,1,128]{2,1,0:T(1,128)} %bitcast.17), calls=%async_computation.1 | async-start | bytes 655360 | tf_op jit(solution)/shard_map/all_to_all | solution.py:601
  47.3 0.7 copy-start.6
  58.1 19.6 %all-to-all-start.2 = ((f32[640,1,128]{2,1,0:T(1,128)}), f32[640,1,128]{2,1,0:T(1,128)S(1)}, u32[]{:S(2)}, u32[]{:S(2)}) async-start(f32[640,1,128]{2,1,0:T(1,128)} %bitcast.49), calls=%async_computation.2 | async-start | bytes 655360 | tf_op jit(solution)/shard_map/all_to_all | solution.py:601
  78.8 16.2 %all-to-all-start.3 = ((f32[640,1,128]{2,1,0:T(1,128)}), f32[640,1,128]{2,1,0:T(1,128)S(1)}, u32[]{:S(2)}, u32[]{:S(2)}) async-start(f32[640,1,128]{2,1,0:T(1,128)} %bitcast.24), calls=%async_computation.3 | async-start | bytes 655360 | tf_op jit(solution)/shard_map/all_to_all | solution.py:601
  95.0 0.7 copy-start.5

commit v6 on v5

--- a/solution.py
+++ b/solution.py
@@ -360,9 +360,16 @@
 
 
 def observe_kernel(
-    level, scaled, turned_high, turned_low, entered, coly, rates, level_weights,
-    forced_out, msg, left, both, spread, marks, line,
+    level_hbm, scaled, high_hbm, low_hbm, entered, coly, rates, level_weights,
+    forced_hbm, msg, left, both, spread, marks, line, level, turned_high, turned_low, forced_out, sems,
 ):
+    arrivals = [
+        pltpu.make_async_copy(level_hbm, level, sems.at[0]),
+        pltpu.make_async_copy(high_hbm, turned_high, sems.at[1]),
+        pltpu.make_async_copy(low_hbm, turned_low, sems.at[2]),
+    ]
+    for copy in arrivals:
+        copy.start()
     decay_y = grow(coly[...], CH, -1.0)
     pick = lambda row: entered[pl.ds(row, PEERS, stride=ROWS), :]
     high, low = split(stack_rows(stack_lanes(pick(0), pick(1)), stack_lanes(pick(2), pick(3))))
@@ -378,6 +385,7 @@
         col = stack_lanes(requests[x : x + 1, :], requests[16 + x : 17 + x, :])
         high, low = split(part * col)
         left[at, 768:1024], left[at, 1024:1280], left[at, 1280:1536] = high, low, high
+    arrivals[0].wait()
     total = level[...] + mm(left[...], stack_rows(eh, eh, el, dh, dh, dl))
     both[:, 0:256], both[:, 256:512] = split(total)
 
@@ -413,6 +421,10 @@
         departures += [miss[:, :128], miss[:, 128:]]
     forced = mm_nt(spread[...], marks[...])
     forced_out[...] = forced
+    leaving = pltpu.make_async_copy(forced_out, forced_hbm, sems.at[3])
+    leaving.start()
+    arrivals[1].wait()
+    arrivals[2].wait()
 
     gh, gl = split(forced)
     th, tl = turned_high[...], turned_low[...]
@@ -432,13 +444,14 @@
     turned = [row[:, :128] for row in rows] + [row[:, 128:] for row in rows] + departures
     turned.append(jnp.zeros((128 - len(turned), 128), f32))
     msg[pl.ds(4, PEERS, stride=ROWS), :] = stack_rows(*turned).T
+    leaving.wait()
 
 
 def observations(level, scaled, turned_high, turned_low, entered, coly, rates, level_weights):
     return pl.pallas_call(
         observe_kernel,
-        in_specs=[VMEM] * 8,
-        out_specs=[VMEM, VMEM],
+        in_specs=[ANY, VMEM, ANY, ANY] + [VMEM] * 4,
+        out_specs=[ANY, VMEM],
         out_shape=[
             jax.ShapeDtypeStruct((XB * LEVELS, YB), f32),
             jax.ShapeDtypeStruct((PEERS * ROWS, 128), f32),
@@ -449,6 +462,11 @@
             pltpu.VMEM((XB * LEVELS, 2 * PEERS * CAP), bf16),
             pltpu.VMEM((YB, 2 * PEERS * CAP), bf16),
             pltpu.VMEM((8, 128), f32),
+            pltpu.VMEM((XB * LEVELS, YB), f32),
+            pltpu.VMEM((CH, XB * LEVELS), bf16),
+            pltpu.VMEM((CH, XB * LEVELS), bf16),
+            pltpu.VMEM((XB * LEVELS, YB), f32),
+            pltpu.SemaphoreType.DMA((4,)),
         ],
         compiler_params=params(57),
         name="observations",

time: 101 us -> 102 us (level)
  no operation moved by 1% of the time
where the time goes in v6:
time: 102 us
  Pallas kernels  48.9 us (48%)
  starting transfers between devices  30.2 us (30%)
  waiting for transfers between devices  17.6 us (17%)
  local copies, waits for them, and re-layouts  3.36 us (3%)
  between operations  1.6 us (2%)
    all_to_all x4, starting transfers between devices, everywhere(): lax.all_to_all(shaped, ('gx', 'gy'), split_axis=0, concat_axis=0, tiled=T...  30.2 us
    all_to_all x4, waiting for transfers between devices, everywhere(): lax.all_to_all(shaped, ('gx', 'gy'), split_axis=0, concat_axis=0, tiled=T...  17.6 us
    pallas_call x1, Pallas kernels, observations(): pl.pallas_call(observe_kernel, in_specs=[ANY, VMEM, ANY, ANY] + [VMEM] *...  10.7 us
    pallas_call x1, Pallas kernels, join(): pl.pallas_call(join_kernel, grid=(CH // BLOCK,), in_specs=[PLANES, PLANES...  5.6 us
    pallas_call x1, Pallas kernels, edges(): pl.pallas_call(edges_kernel, grid=(CH // BLOCK,), in_specs=CONTROL + [who...  5.49 us
    pallas_call x1, Pallas kernels, final(): pl.pallas_call(final_kernel, grid=(CH // BLOCK,), in_specs=[PLANES, whole...  5.18 us
    pallas_call x1, Pallas kernels, local(): pl.pallas_call(local_kernel, grid=(CH // BLOCK,), in_specs=[PLANES, STEPS...  4.54 us
    pallas_call x1, Pallas kernels, planes_back(): pl.pallas_call(planes_back_kernel, grid=(XB // DEEP,), in_specs=[pl.Block...  4.31 us
  transfers between devices with their start and end apart: 4, of which 4 were waited for; matrix products, arithmetic and copies ran while one was open for 2% of the time, Pallas kernels for 25%

profile of v6, /device:TPU:1, one launch (start us, length us, event | category | flops | bytes accessed | tf_op | source)
XLA Modules:
  0.0 101.8 jit_solution(2774225265214822703)
XLA Ops:
  0.6 5.5 %edges.1 = (f32[640,128]{1,0:T(8,128)}, f32[256,128]{1,0:T(8,128)}, f32[256,128]{1,0:T(8,128)}, f32[16,256,256]{2,1,0:T(8,128)}) custom-call(f32[4096,256]{1,0:T(8,128)} %bitcast.41, f32[4096,256]{1,0:T(8,128)} %bitcast.42, f32[2,4,64]{2,1,0:T(4,128)} %rates.1), custom_call_target="tpu_custom_call" | custom-call | tf_op jit(solution)/shard_map/edges/pallas_call | solution.py:135
  6.1 11.5 %all-to-all-start = ((f32[640,1,128]{2,1,0:T(1,128)}), f32[640,1,128]{2,1,0:T(1,128)S(1)}, u32[]{:S(2)}, u32[]{:S(2)}) async-start(f32[640,1,128]{2,1,0:T(1,128)} %bitcast.48), calls=%async_computation | async-start | bytes 655360 | tf_op jit(solution)/shard_map/all_to_all | solution.py:619
  18.4 4.5 %local.1.cc = f32[16,256,256]{2,1,0:T(8,128)} custom-call(f32[16,256,256]{2,1,0:T(8,128)} %get-tuple-element.21.planes.control, f32[256,128]{1,0:T(8,128)} %get-tuple-element.23.colx, f32[256,128]{1,0:T(8,128)} %get-tuple-element.24.coly), custom_call_target="tpu_custom_call" | custom-call | flops 1073741824 | bytes 8388608 | tf_op jit(solution)/shard_map/local/pallas_call | solution.py:230
  23.1 1.9 %prepare.1 = (f32[128,128]{1,0:T(8,128)S(1)}, f32[128,512]{1,0:T(8,128)S(1)}, f32[128,512]{1,0:T(8,128)S(1)}, f32[128,512]{1,0:T(8,128)S(1)}, f32[8,128]{1,0:T(8,128)S(1)}) custom-call(s32[3]{0:T(128)S(1)} %pad_add_fusion.place, s32[1]{0:T(128)S(6)} %copy.21.count, f32[2,256]{1,0:T(2,128)S(1)} %reshape.97.rates, s32[1,512]{1,0:T(1,128)S(1)} %bitcast.37, ...), custom_call_target="tpu_custom_call" | custom-call | flops 1073741824 | bytes 1048576 | tf_op jit(solution)/shard_map/prepare/pallas_call | solution.py:194
  25.0 4.0 %all-to-all-done = f32[640,1,128]{2,1,0:T(1,128)S(1)} async-done(((f32[640,1,128]{2,1,0:T(1,128)}), f32[640,1,128]{2,1,0:T(1,128)S(1)}, u32[]{:S(2)}, u32[]{:S(2)}) %all-to-all-start) | async-done | bytes 327712 | tf_op jit(solution)/shard_map/all_to_all | solution.py:619
  29.0 1.2 %carry.1 = f32[640,128]{1,0:T(8,128)} custom-call(f32[640,128]{1,0:T(8,128)S(1)} %bitcast.36, f32[128,512]{1,0:T(8,128)S(1)} %get-tuple-element.31.weights, f32[8,128]{1,0:T(8,128)S(1)} %get-tuple-element.32.down.refs_2_, f32[128,128]{1,0:T(8,128)S(1)} %get-tuple-element.33.requests), custom_call_target="tpu_custom_call" | custom-call | tf_op jit(solution)/shard_map/carry/pallas_call | solution.py:348
  30.2 5.7 %all-to-all-start.1 = ((f32[640,1,128]{2,1,0:T(1,128)}), f32[640,1,128]{2,1,0:T(1,128)S(1)}, u32[]{:S(2)}, u32[]{:S(2)}) async-start(f32[640,1,128]{2,1,0:T(1,128)} %bitcast.17), calls=%async_computation.1 | async-start | bytes 655360 | tf_op jit(solution)/shard_map/all_to_all | solution.py:619
  36.3 0.8 reshape.98.matrix
  37.0 0.8 broadcast_in_dim.2
  37.9 3.7 %share.1 = f32[16,64,256]{2,1,0:T(8,128)} custom-call(f32[4,1024,256]{2,1,0:T(8,128)} %bitcast.43, f32[1024,4]{1,0:T(8,128)} %bitcast.45), custom_call_target="tpu_custom_call" | custom-call | flops 2097152 | bytes 5242880 | tf_op jit(solution)/shard_map/share/pallas_call | solution.py:253
  41.5 4.2 %levels.1 = (f32[1024,256]{1,0:T(8,128)}, f32[1024,256]{1,0:T(8,128)}, bf16[256,1024]{1,0:T(8,128)(2,1)}, bf16[256,1024]{1,0:T(8,128)(2,1)}) custom-call(f32[16,256,256]{2,1,0:T(8,128)} %local.1.cc, f32[16,64,256]{2,1,0:T(8,128)} %share.1, f32[256,128]{1,0:T(8,128)} %get-tuple-element.24.coly, f32[2,256]{1,0:T(2,128)} %copy-done, f32[64,256]{1,0:T(8,128)} %reshape.98.matrix), custom_call_target="tpu_custom_call" | custom-call | flops 402653184 | bytes 8388608 | tf_op jit(solution)/shard_map/levels/pallas_call | solution.py:294
  45.8 1.5 %all-to-all-done.1 = f32[640,1,128]{2,1,0:T(1,128)S(1)} async-done(((f32[640,1,128]{2,1,0:T(1,128)}), f32[640,1,128]{2,1,0:T(1,128)S(1)}, u32[]{:S(2)}, u32[]{:S(2)}) %all-to-all-start.1) | async-done | bytes 327712 | tf_op jit(solution)/shard_map/all_to_all | solution.py:619
  47.3 0.7 copy-done.6
  48.0 10.7 %observations.1 = (f32[1024,256]{1,0:T(8,128)}, f32[640,128]{1,0:T(8,128)}) custom-call(f32[1024,256]{1,0:T(8,128)} %get-tuple-element.26.level_hbm, f32[1024,256]{1,0:T(8,128)} %get-tuple-element.27.scaled, bf16[256,1024]{1,0:T(8,128)(2,1)} %get-tuple-element.28.high_hbm.turned_high, bf16[256,1024]{1,0:T(8,128)(2,1)} %get-tuple-element.29.low_hbm.turned_low, ...), custom_call_target="tpu_custom_call" | custom-call | tf_op jit(solution)/shard_map/observations/pallas_call | solution.py:451
  58.7 8.2 %all-to-all-start.2 = ((f32[640,1,128]{2,1,0:T(1,128)}), f32[640,1,128]{2,1,0:T(1,128)S(1)}, u32[]{:S(2)}, u32[]{:S(2)}) async-start(f32[640,1,128]{2,1,0:T(1,128)} %bitcast.49), calls=%async_computation.2 | async-start | bytes 655360 | tf_op jit(solution)/shard_map/all_to_all | solution.py:619
  67.0 4.3 %planes_back.1.running = f32[16,256,256]{2,1,0:T(8,128)} custom-call(f32[1024,256]{1,0:T(8,128)} %get-tuple-element.35.forced, bf16[256,1024]{1,0:T(8,128)(2,1)} %get-tuple-element.28.high_hbm.turned_high, bf16[256,1024]{1,0:T(8,128)(2,1)} %get-tuple-element.29.low_hbm.turned_low, f32[256,128]{1,0:T(8,128)} %get-tuple-element.24.coly), custom_call_target="tpu_custom_call" | custom-call | flops 2147483648 | bytes 8388608 | tf_op jit(solution)/shard_map/planes_back/pallas_call | solution.py:501
  71.3 7.0 %all-to-all-done.2 = f32[640,1,128]{2,1,0:T(1,128)S(1)} async-done(((f32[640,1,128]{2,1,0:T(1,128)}), f32[640,1,128]{2,1,0:T(1,128)S(1)}, u32[]{:S(2)}, u32[]{:S(2)}) %all-to-all-start.2) | async-done | bytes 327712 | tf_op jit(solution)/shard_map/all_to_all | solution.py:619
  78.3 1.2 %carry_back.1 = f32[640,128]{1,0:T(8,128)} custom-call(f32[640,128]{1,0:T(8,128)S(1)} %bitcast.34, f32[128,512]{1,0:T(8,128)S(1)} %get-tuple-element.38.refs_1_, f32[8,128]{1,0:T(8,128)S(1)} %get-tuple-element.32.down.refs_2_), custom_call_target="tpu_custom_call" | custom-call | tf_op jit(solution)/shard_map/carry_back/pallas_call | solution.py:344
  79.5 4.7 %all-to-all-start.3 = ((f32[640,1,128]{2,1,0:T(1,128)}), f32[640,1,128]{2,1,0:T(1,128)S(1)}, u32[]{:S(2)}, u32[]{:S(2)}) async-start(f32[640,1,128]{2,1,0:T(1,128)} %bitcast.24), calls=%async_computation.3 | async-start | bytes 655360 | tf_op jit(solution)/shard_map/all_to_all | solution.py:619
  84.2 0.9 departures.1
  85.1 5.6 %join.1.partial = f32[16,256,256]{2,1,0:T(8,128)} custom-call(f32[16,256,256]{2,1,0:T(8,128)} %get-tuple-element.21.planes.control, f32[16,256,256]{2,1,0:T(8,128)} %planes_back.1.running, f32[256,128]{1,0:T(8,128)} %get-tuple-element.23.colx, f32[256,128]{1,0:T(8,128)} %get-tuple-element.24.coly), custom_call_target="tpu_custom_call" | custom-call | flops 1073741824 | bytes 12582912 | tf_op jit(solution)/shard_map/join/pallas_call | solution.py:528
  90.7 5.0 %all-to-all-done.3 = f32[640,1,128]{2,1,0:T(1,128)S(1)} async-done(((f32[640,1,128]{2,1,0:T(1,128)}), f32[640,1,128]{2,1,0:T(1,128)S(1)}, u32[]{:S(2)}, u32[]{:S(2)}) %all-to-all-start.3) | async-done | bytes 327712 | tf_op jit(solution)/shard_map/all_to_all | solution.py:619
  95.7 0.7 copy-done.5
  96.4 5.2 %final.1 = f32[4096,256]{1,0:T(8,128)} custom-call(f32[16,256,256]{2,1,0:T(8,128)} %join.1.partial, f32[640,128]{1,0:T(8,128)} %bitcast.46, f32[256,128]{1,0:T(8,128)} %get-tuple-element.23.colx, f32[256,128]{1,0:T(8,128)} %get-tuple-element.24.coly), custom_call_target="tpu_custom_call" | custom-call | tf_op jit(solution)/shard_map/final/pallas_call | solution.py:580
  (24 shorter events, 0.5 us)
Async XLA Ops:
  0.6 17.0 %copy-start.8 = (f32[2,4,64]{2,1,0:T(4,128)S(1)}, f32[2,4,64]{2,1,0:T(4,128)}, u32[]{:S(2)}) copy-start(f32[2,4,64]{2,1,0:T(4,128)} %rates.1) | copy-start | bytes 6148
  6.1 22.9 %all-to-all-start = ((f32[640,1,128]{2,1,0:T(1,128)}), f32[640,1,128]{2,1,0:T(1,128)S(1)}, u32[]{:S(2)}, u32[]{:S(2)}) async-start(f32[640,1,128]{2,1,0:T(1,128)} %bitcast.48), calls=%async_computation | async-start | bytes 655360 | tf_op jit(solution)/shard_map/all_to_all | solution.py:619
  17.7 5.3 %copy-start = (f32[2,256]{1,0:T(2,128)}, f32[2,256]{1,0:T(2,128)S(1)}, u32[]{:S(2)}) copy-start(f32[2,256]{1,0:T(2,128)S(1)} %reshape.97.rates) | copy-start | bytes 6148
  18.4 4.7 %copy-start.1 = (s32[512,1]{0,1:T(1,128)S(1)}, s32[512,1]{0,1:T(1,128)}, u32[]{:S(2)}) copy-start(s32[512,1]{0,1:T(1,128)} %param.17) | copy-start | bytes 6148
  18.4 4.7 %copy-start.2 = (s32[512]{0:T(512)S(1)}, s32[512]{0:T(512)}, u32[]{:S(2)}) copy-start(s32[512]{0:T(512)} %param.18) | copy-start | bytes 6148
  18.4 4.7 %copy-start.3 = (f32[512]{0:T(512)S(1)}, f32[512]{0:T(512)}, u32[]{:S(2)}) copy-start(f32[512]{0:T(512)} %param.20) | copy-start | bytes 6148
  18.4 4.7 %copy-start.4 = (f32[512]{0:T(512)S(1)}, f32[512]{0:T(512)}, u32[]{:S(2)}) copy-start(f32[512]{0:T(512)} %param.21) | copy-start | bytes 6148
  23.0 13.0 %copy-start.9 = (f32[4,64]{1,0:T(4,128)S(1)}, f32[4,64]{1,0:T(4,128)}, u32[]{:S(2)}) copy-start(f32[4,64]{1,0:T(4,128)} %param.15) | copy-start | bytes 3076
  23.0 13.1 %copy-start.7 = (f32[4,64,64]{2,1,0:T(8,128)S(1)}, f32[4,64,64]{2,1,0:T(8,128)}, u32[]{:S(2)}) copy-start(f32[4,64,64]{2,1,0:T(8,128)} %param.13) | copy-start | bytes 196612
  30.2 17.1 %all-to-all-start.1 = ((f32[640,1,128]{2,1,0:T(1,128)}), f32[640,1,128]{2,1,0:T(1,128)S(1)}, u32[]{:S(2)}, u32[]{:S(2)}) async-start(f32[640,1,128]{2,1,0:T(1,128)} %bitcast.17), calls=%async_computation.1 | async-start | bytes 655360 | tf_op jit(solution)/shard_map/all_to_all | solution.py:619
  47.3 0.7 copy-start.6
  58.7 19.6 %all-to-all-start.2 = ((f32[640,1,128]{2,1,0:T(1,128)}), f32[640,1,128]{2,1,0:T(1,128)S(1)}, u32[]{:S(2)}, u32[]{:S(2)}) async-start(f32[640,1,128]{2,1,0:T(1,128)} %bitcast.49), calls=%async_computation.2 | async-start | bytes 655360 | tf_op jit(solution)/shard_map/all_to_all | solution.py:619
  79.5 16.2 %all-to-all-start.3 = ((f32[640,1,128]{2,1,0:T(1,128)}), f32[640,1,128]{2,1,0:T(1,128)S(1)}, u32[]{:S(2)}, u32[]{:S(2)}) async-start(f32[640,1,128]{2,1,0:T(1,128)} %bitcast.24), calls=%async_computation.3 | async-start | bytes 655360 | tf_op jit(solution)/shard_map/all_to_all | solution.py:619
  95.7 0.7 copy-start.5
